TPU v7x, 32 devices: a whole 2x2x4 slice. The times are simulated.
32 devices in a mesh: dp: 8 (over z, core), tensor: 4 (over y, x).
Axes of the slice: x: 2, y: 2, z: 4, core: 2. Of those that a mesh axis runs over, the one named last changes fastest.
Arguments:
- tokens: bfloat16 [8192, 2048], P(('dp', 'tensor')), may hold values from -6 to 6
- lengths: int32 [8, 3], P('dp'), may hold values from 1 to 512, 768 in all within a row
- query_weight: bfloat16 [2048, 2048], P('dp', 'tensor'), may hold values from -0.125 to 0.125
- key_weight: bfloat16 [2048, 2048], P('dp', 'tensor'), may hold values from -0.125 to 0.125
- value_weight: bfloat16 [2048, 2048], P('dp', 'tensor'), may hold values from -0.125 to 0.125
- output_weight: bfloat16 [2048, 2048], P('tensor', 'dp'), may hold values from -1.5 to 1.5
- gate_weight: bfloat16 [2048, 8192], P('dp', 'tensor'), may hold values from -0.125 to 0.125
- up_weight: bfloat16 [2048, 8192], P('dp', 'tensor'), may hold values from -0.125 to 0.125
- down_weight: bfloat16 [8192, 2048], P('tensor', 'dp'), may hold values from -0.0625 to 0.0625
- cotangent: bfloat16 [8192, 2048], P(('dp', 'tensor')), may hold values from -6 to 6
Outputs:
- output: bfloat16 [8192, 2048], P(('dp', 'tensor'))
- input_grad: bfloat16 [8192, 2048], P(('dp', 'tensor'))
- query_grad: float32 [2048, 2048], P('dp', 'tensor')
- key_grad: float32 [2048, 2048], P('dp', 'tensor')
- value_grad: float32 [2048, 2048], P('dp', 'tensor')
- output_grad: float32 [2048, 2048], P('tensor', 'dp')
- gate_grad: float32 [2048, 8192], P('dp', 'tensor')
- up_grad: float32 [2048, 8192], P('dp', 'tensor')
- down_grad: float32 [8192, 2048], P('tensor', 'dp')
Inputs may be any that keep to these rules, and one draw needn't show every extreme that they name: Each row holds the lengths of the 3 documents packed from the start of a slot of 1024 positions; the rest of the slot is padding. Every row's largest length is 512 and its lengths add to 768.
All inputs are finite; a program needn't handle non-finite values.
Results may differ from a plain program's by a relative error of at most 0.023.
Values may be sent and summed in bfloat16 or wider, within the bound.
No kernel may reach another device: no remote copies, remote signals or barrier semaphores. Data moves between devices by JAX's collectives and lax.ppermute only.
A program may use at most 256 MiB of HBM per device.

v0:
```python
import math

import jax
import jax.numpy as jnp
from jax import lax
from jax.sharding import PartitionSpec as P

HD = 128
QBLOCK = 512


EPSILON = 1e-05
ROPE_BASE = 10000.0
MASKED = -1e30


def layer_norm(rows):
    centre = jnp.mean(rows, axis=-1, keepdims=True)
    centered = rows - centre
    spread = jnp.mean(centered * centered, axis=-1, keepdims=True)
    return centered * lax.rsqrt(spread + EPSILON)


def slot_layout(lengths_row, row_total):
    ends = jnp.cumsum(lengths_row)
    places = jnp.arange(row_total, dtype=jnp.int32)
    segment = jnp.sum((places[:, None] >= ends[None, :]).astype(jnp.int32), axis=1)
    starts = jnp.concatenate([jnp.zeros((1,), jnp.int32), ends])
    picks = jnp.arange(starts.shape[0], dtype=jnp.int32)
    begins = jnp.sum(jnp.where(segment[:, None] == picks[None, :], starts[None, :], 0), axis=1)
    position = places - begins
    valid = (places < ends[-1]).astype(jnp.int32)
    return (segment, position, places, valid)


def rope_tables(position, head_size):
    half_size = head_size // 2
    steps_float = jnp.arange(half_size, dtype=jnp.float32)
    freqs = jnp.exp(steps_float * (-2.0 * math.log(ROPE_BASE) / head_size))
    angles = position.astype(jnp.float32)[:, None] * freqs[None, :]
    return (jnp.cos(angles), jnp.sin(angles))


def rotate(values, cosine_table, sine_table):
    half_size = values.shape[-1] // 2
    first_half = values[..., :half_size]
    second_half = values[..., half_size:]
    cosine_wide = cosine_table[:, None, :]
    sine_wide = sine_table[:, None, :]
    return jnp.concatenate(
        [
            first_half * cosine_wide - second_half * sine_wide,
            second_half * cosine_wide + first_half * sine_wide,
        ],
        axis=-1,
    )


def swish_product(gate_pre, up_pre):
    return jax.nn.silu(gate_pre) * up_pre


def dot_first(left, right):
    return lax.dot_general(
        left, right, (((0,), (0,)), ((), ())), preferred_element_type=jnp.float32
    )


def dot_last(left, right):
    return lax.dot_general(
        left, right, (((1,), (1,)), ((), ())), preferred_element_type=jnp.float32
    )


def block_scores(queries, keys_turned, segment_rows, segment_cols, place_rows, place_cols, scale):
    raw_scores = (
        jnp.einsum("qhd,khd->hqk", queries, keys_turned, preferred_element_type=jnp.float32) * scale
    )
    allowed = (segment_rows[:, None] == segment_cols[None, :]) & (
        place_rows[:, None] >= place_cols[None, :]
    )
    return jnp.where(allowed[None], raw_scores, MASKED)


def attend_forward(queries, keys_turned, values, segment, places, block_rows):
    slot_rows = queries.shape[0]
    scale = queries.shape[2] ** (-0.5)
    context_blocks = []
    log_totals = []
    for block_index in range(slot_rows // block_rows):
        lower_row = block_index * block_rows
        reach_row = lower_row + block_rows
        scores = block_scores(
            queries[lower_row:reach_row],
            keys_turned[:reach_row],
            segment[lower_row:reach_row],
            segment[:reach_row],
            places[lower_row:reach_row],
            places[:reach_row],
            scale,
        )
        row_peak = jnp.max(scores, axis=-1, keepdims=True)
        weights = jnp.exp(scores - row_peak)
        row_total = jnp.sum(weights, axis=-1, keepdims=True)
        probs = (weights / row_total).astype(jnp.bfloat16)
        context_blocks.append(
            jnp.einsum(
                "hqk,khd->qhd", probs, values[:reach_row], preferred_element_type=jnp.float32
            ).astype(jnp.bfloat16)
        )
        log_totals.append(row_peak + jnp.log(row_total))
    return (jnp.concatenate(context_blocks, axis=0), log_totals)


def attend_backward(
    queries, keys_turned, values, segment, places, log_totals, d_context, block_rows
):
    slot_rows, heads_here, head_size = queries.shape
    scale = head_size ** (-0.5)
    d_keys = jnp.zeros((slot_rows, heads_here, head_size), jnp.float32)
    d_values = jnp.zeros((slot_rows, heads_here, head_size), jnp.float32)
    d_query_blocks = []
    for block_index in range(slot_rows // block_rows):
        lower_row = block_index * block_rows
        reach_row = lower_row + block_rows
        query_block = queries[lower_row:reach_row]
        scores = block_scores(
            query_block,
            keys_turned[:reach_row],
            segment[lower_row:reach_row],
            segment[:reach_row],
            places[lower_row:reach_row],
            places[:reach_row],
            scale,
        )
        probs = jnp.exp(scores - log_totals[block_index])
        grads_block = d_context[lower_row:reach_row]
        d_probs = jnp.einsum(
            "qhd,khd->hqk", grads_block, values[:reach_row], preferred_element_type=jnp.float32
        )
        inner = jnp.sum(probs * d_probs, axis=-1, keepdims=True)
        d_scores = (probs * (d_probs - inner) * scale).astype(jnp.bfloat16)
        d_query_blocks.append(
            jnp.einsum(
                "hqk,khd->qhd",
                d_scores,
                keys_turned[:reach_row],
                preferred_element_type=jnp.float32,
            )
        )
        d_keys = d_keys.at[:reach_row].add(
            jnp.einsum("hqk,qhd->khd", d_scores, query_block, preferred_element_type=jnp.float32)
        )
        d_values = d_values.at[:reach_row].add(
            jnp.einsum(
                "hqk,qhd->khd",
                probs.astype(jnp.bfloat16),
                grads_block,
                preferred_element_type=jnp.float32,
            )
        )
    return (jnp.concatenate(d_query_blocks, axis=0), d_keys, d_values)


def per_device(
    tokens,
    lengths,
    query_weight,
    key_weight,
    value_weight,
    output_weight,
    gate_weight,
    up_weight,
    down_weight,
    cotangent,
):
    row_count = tokens.shape[0]
    slot_rows = row_count * lax.axis_size("tensor")
    first_row = lax.axis_index("tensor") * row_count
    segment, position, places, valid_all = slot_layout(lengths[0], slot_rows)
    valid_rows = lax.dynamic_slice_in_dim(valid_all, first_row, row_count, 0).astype(jnp.float32)[
        :, None
    ]
    cosine_table, sine_table = rope_tables(position, HD)
    heads_here = query_weight.shape[1] // HD
    weights = (
        lax.all_gather(query_weight, "dp", axis=0, tiled=True),
        lax.all_gather(key_weight, "dp", axis=0, tiled=True),
        lax.all_gather(value_weight, "dp", axis=0, tiled=True),
        lax.all_gather(output_weight, "dp", axis=1, tiled=True),
        lax.all_gather(gate_weight, "dp", axis=0, tiled=True),
        lax.all_gather(up_weight, "dp", axis=0, tiled=True),
        lax.all_gather(down_weight, "dp", axis=1, tiled=True),
    )
    residual_in = tokens.astype(jnp.float32)
    normed_one = layer_norm(residual_in).astype(jnp.bfloat16)
    gathered_one = lax.all_gather(normed_one, "tensor", axis=0, tiled=True)
    query_pre = jnp.dot(gathered_one, weights[0], preferred_element_type=jnp.float32).reshape(
        slot_rows, heads_here, HD
    )
    key_pre = jnp.dot(gathered_one, weights[1], preferred_element_type=jnp.float32).reshape(
        slot_rows, heads_here, HD
    )
    values = (
        jnp.dot(gathered_one, weights[2], preferred_element_type=jnp.float32)
        .astype(jnp.bfloat16)
        .reshape(slot_rows, heads_here, HD)
    )
    queries = rotate(query_pre, cosine_table, sine_table).astype(jnp.bfloat16)
    keys_turned = rotate(key_pre, cosine_table, sine_table).astype(jnp.bfloat16)
    context, log_totals = attend_forward(queries, keys_turned, values, segment, places, QBLOCK)
    context_flat = context.reshape(slot_rows, heads_here * HD)
    picked = context_flat
    attention_out = lax.psum_scatter(
        jnp.dot(picked, weights[3], preferred_element_type=jnp.float32).astype(jnp.bfloat16),
        "tensor",
        scatter_dimension=0,
        tiled=True,
    ).astype(jnp.float32)
    middle = residual_in + attention_out
    normed_two = layer_norm(middle).astype(jnp.bfloat16)
    gathered_two = lax.all_gather(normed_two, "tensor", axis=0, tiled=True)
    gate_pre = jnp.dot(gathered_two, weights[4], preferred_element_type=jnp.float32)
    up_pre = jnp.dot(gathered_two, weights[5], preferred_element_type=jnp.float32)
    hidden = swish_product(gate_pre, up_pre).astype(jnp.bfloat16)
    picked = hidden
    feed_out = lax.psum_scatter(
        jnp.dot(picked, weights[6], preferred_element_type=jnp.float32).astype(jnp.bfloat16),
        "tensor",
        scatter_dimension=0,
        tiled=True,
    ).astype(jnp.float32)
    output = (valid_rows * (middle + feed_out)).astype(jnp.bfloat16)
    weights = (
        lax.all_gather(query_weight, "dp", axis=0, tiled=True),
        lax.all_gather(key_weight, "dp", axis=0, tiled=True),
        lax.all_gather(value_weight, "dp", axis=0, tiled=True),
        lax.all_gather(output_weight, "dp", axis=1, tiled=True),
        lax.all_gather(gate_weight, "dp", axis=0, tiled=True),
        lax.all_gather(up_weight, "dp", axis=0, tiled=True),
        lax.all_gather(down_weight, "dp", axis=1, tiled=True),
    )
    masked_grad = valid_rows * cotangent.astype(jnp.float32)
    feed_grad = masked_grad.astype(jnp.bfloat16)
    rows_piece = lax.all_gather(feed_grad, "tensor", axis=0, tiled=True)
    picked = hidden
    down_part = dot_first(picked, rows_piece)
    hidden_part = dot_last(rows_piece, weights[6])
    _, swish_pull = jax.vjp(swish_product, gate_pre, up_pre)
    d_gate, d_up = swish_pull(hidden_part)
    d_gate = d_gate.astype(jnp.bfloat16)
    d_up = d_up.astype(jnp.bfloat16)
    gate_local = dot_first(gathered_two, d_gate)
    up_local = dot_first(gathered_two, d_up)
    d_normed_two = lax.psum_scatter(
        (dot_last(d_gate, weights[4]) + dot_last(d_up, weights[5])).astype(jnp.bfloat16),
        "tensor",
        scatter_dimension=0,
        tiled=True,
    ).astype(jnp.float32)
    _, second_pull = jax.vjp(layer_norm, middle)
    d_middle = masked_grad + second_pull(d_normed_two)[0]
    attention_grad = d_middle.astype(jnp.bfloat16)
    rows_piece = lax.all_gather(attention_grad, "tensor", axis=0, tiled=True)
    picked = context_flat
    weight_part = dot_first(picked, rows_piece)
    context_part = dot_last(rows_piece, weights[3])
    d_context = context_part
    d_context = d_context.astype(jnp.bfloat16).reshape(slot_rows, heads_here, HD)
    d_queries, d_keys, d_values = attend_backward(
        queries, keys_turned, values, segment, places, log_totals, d_context, QBLOCK
    )
    _, turn_pull = jax.vjp(lambda moved: rotate(moved, cosine_table, sine_table), query_pre)
    d_query_pre = turn_pull(d_queries)[0].astype(jnp.bfloat16).reshape(slot_rows, heads_here * HD)
    d_key_pre = turn_pull(d_keys)[0].astype(jnp.bfloat16).reshape(slot_rows, heads_here * HD)
    d_value_pre = d_values.astype(jnp.bfloat16).reshape(slot_rows, heads_here * HD)
    query_local = dot_first(gathered_one, d_query_pre)
    key_local = dot_first(gathered_one, d_key_pre)
    value_local = dot_first(gathered_one, d_value_pre)
    d_normed_one = lax.psum_scatter(
        (
            dot_last(d_query_pre, weights[0])
            + dot_last(d_key_pre, weights[1])
            + dot_last(d_value_pre, weights[2])
        ).astype(jnp.bfloat16),
        "tensor",
        scatter_dimension=0,
        tiled=True,
    ).astype(jnp.float32)
    _, first_pull = jax.vjp(layer_norm, residual_in)
    input_grad = (d_middle + first_pull(d_normed_one)[0]).astype(jnp.bfloat16)
    query_sum, key_sum, value_sum, output_sum, gate_sum, up_sum, down_sum = (
        lax.psum_scatter(
            query_local.astype(jnp.bfloat16), "dp", scatter_dimension=0, tiled=True
        ).astype(jnp.float32),
        lax.psum_scatter(
            key_local.astype(jnp.bfloat16), "dp", scatter_dimension=0, tiled=True
        ).astype(jnp.float32),
        lax.psum_scatter(
            value_local.astype(jnp.bfloat16), "dp", scatter_dimension=0, tiled=True
        ).astype(jnp.float32),
        lax.psum_scatter(
            weight_part.astype(jnp.bfloat16), "dp", scatter_dimension=1, tiled=True
        ).astype(jnp.float32),
        lax.psum_scatter(
            gate_local.astype(jnp.bfloat16), "dp", scatter_dimension=0, tiled=True
        ).astype(jnp.float32),
        lax.psum_scatter(
            up_local.astype(jnp.bfloat16), "dp", scatter_dimension=0, tiled=True
        ).astype(jnp.float32),
        lax.psum_scatter(
            down_part.astype(jnp.bfloat16), "dp", scatter_dimension=1, tiled=True
        ).astype(jnp.float32),
    )
    return (
        output,
        input_grad,
        query_sum,
        key_sum,
        value_sum,
        output_sum,
        gate_sum,
        up_sum,
        down_sum,
    )


def solution(mesh):
    return jax.shard_map(
        per_device,
        mesh=mesh,
        in_specs=(
            P(("dp", "tensor"), None),
            P("dp", None),
            P("dp", "tensor"),
            P("dp", "tensor"),
            P("dp", "tensor"),
            P("tensor", "dp"),
            P("dp", "tensor"),
            P("dp", "tensor"),
            P("tensor", "dp"),
            P(("dp", "tensor"), None),
        ),
        out_specs=(
            P(("dp", "tensor"), None),
            P(("dp", "tensor"), None),
            P("dp", "tensor"),
            P("dp", "tensor"),
            P("dp", "tensor"),
            P("tensor", "dp"),
            P("dp", "tensor"),
            P("dp", "tensor"),
            P("tensor", "dp"),
        ),
        check_vma=False,
    )
```

profile of v0, /device:TPU:0, one launch (start us, length us, event | category | flops | bytes accessed | tf_op | source)
XLA Modules:
  0.0 1302.9 jit_solution(14232833161550070507)
XLA Ops:
  22.0 19.5 %all-gather.18.cloned.1.call-done = bf16[2048,512]{1,0:T(8,128)(2,1)} async-done(((bf16[256,512]{1,0:T(8,128)(2,1)}), bf16[2048,512]{1,0:T(8,128)(2,1)}) %all-gather.18.cloned.1.call-update) | async-done | bytes 2097168 | tf_op jit(solution)/shard_map/all_gather | solution.py:188
  41.5 54.4 %all-gather.12.cloned.1.call-done = bf16[1024,2048]{1,0:T(8,128)(2,1)} async-done(((bf16[256,2048]{1,0:T(8,128)(2,1)}), bf16[1024,2048]{1,0:T(8,128)(2,1)}) %all-gather.12.cloned.1.call-update) | async-done | bytes 4194320 | tf_op jit(solution)/shard_map/all_gather | solution.py:197
  105.2 21.5 %all-gather.16.cloned.1.call-done = bf16[2048,512]{1,0:T(8,128)(2,1)} async-done(((bf16[256,512]{1,0:T(8,128)(2,1)}), bf16[2048,512]{1,0:T(8,128)(2,1)}) %all-gather.16.cloned.1.call-update) | async-done | bytes 2097168 | tf_op jit(solution)/shard_map/all_gather | solution.py:187
  143.5 13.3 %all-gather.14.cloned.1.call-done = bf16[2048,512]{1,0:T(8,128)(2,1)} async-done(((bf16[256,512]{1,0:T(8,128)(2,1)}), bf16[2048,512]{1,0:T(8,128)(2,1)}) %all-gather.14.cloned.1.call-update) | async-done | bytes 2097168 | tf_op jit(solution)/shard_map/all_gather | solution.py:189
  174.7 13.5 %all-gather.20.cloned.1.call-done = bf16[512,2048]{1,0:T(8,128)(2,1)} async-done(((bf16[512,256]{1,0:T(8,128)(2,1)}), bf16[512,2048]{1,0:T(8,128)(2,1)}) %all-gather.20.cloned.1.call-update) | async-done | bytes 2097168 | tf_op jit(solution)/shard_map/all_gather | solution.py:190
  195.0 51.0 %reduce-scatter.12.cloned.1.call-done = bf16[256,2048]{1,0:T(8,128)(2,1)} async-done(((bf16[1024,2048]{1,0:T(8,128)(2,1)}), bf16[256,2048]{1,0:T(8,128)(2,1)}) %reduce-scatter.12.cloned.1.call-update) | async-done | bytes 1048592 | tf_op jit(solution)/shard_map/reduce_scatter | solution.py:214
  255.1 74.6 %all-gather.26.cloned.1.call-done = bf16[2048,2048]{1,0:T(8,128)(2,1)} async-done(((bf16[256,2048]{1,0:T(8,128)(2,1)}), bf16[2048,2048]{1,0:T(8,128)(2,1)}) %all-gather.26.cloned.1.call-update) | async-done | bytes 8388624 | tf_op jit(solution)/shard_map/all_gather | solution.py:192
  329.7 53.5 %all-gather.22.cloned.1.call-done = bf16[1024,2048]{1,0:T(8,128)(2,1)} async-done(((bf16[256,2048]{1,0:T(8,128)(2,1)}), bf16[1024,2048]{1,0:T(8,128)(2,1)}) %all-gather.22.cloned.1.call-update) | async-done | bytes 4194320 | tf_op jit(solution)/shard_map/all_gather | solution.py:222
  383.2 14.8 %fusion.133 = f32[1024,2048]{1,0:T(8,128)} fusion(bf16[1024,2048]{1,0:T(8,128)(2,1)} %all-gather.22.cloned.1.call-done, bf16[2048,2048]{1,0:T(8,128)(2,1)} %all-gather.26.cloned.1.call-done), kind=kOutput, calls=%fused_computation.177 | convolution fusion | flops 8589934592 | bytes 20971520 | tf_op jit(solution)/shard_map/dot_general | solution.py:224
  398.0 68.9 %all-gather.24.cloned.1.call-done = bf16[2048,2048]{1,0:T(8,128)(2,1)} async-done(((bf16[256,2048]{1,0:T(8,128)(2,1)}), bf16[2048,2048]{1,0:T(8,128)(2,1)}) %all-gather.24.cloned.1.call-update) | async-done | bytes 8388624 | tf_op jit(solution)/shard_map/all_gather | solution.py:191
  466.9 14.4 %fusion.132 = f32[1024,2048]{1,0:T(8,128)} fusion(bf16[1024,2048]{1,0:T(8,128)(2,1)} %all-gather.22.cloned.1.call-done, bf16[2048,2048]{1,0:T(8,128)(2,1)} %all-gather.24.cloned.1.call-done), kind=kOutput, calls=%fused_computation.176 | convolution fusion | flops 8589934592 | bytes 20971520 | tf_op jit(solution)/shard_map/dot_general | solution.py:223
  481.3 39.0 %all-gather.30.cloned.1.call-done = bf16[1024,2048]{1,0:T(8,128)(2,1)} async-done(((bf16[256,2048]{1,0:T(8,128)(2,1)}), bf16[1024,2048]{1,0:T(8,128)(2,1)}) %all-gather.30.cloned.1.call-update) | async-done | bytes 4194320 | tf_op jit(solution)/shard_map/all_gather | solution.py:245
  520.3 84.1 %all-gather.28.cloned.1.call-done = bf16[2048,2048]{1,0:T(8,128)(2,1)} async-done(((bf16[2048,256]{1,0:T(8,128)(2,1)}), bf16[2048,2048]{1,0:T(8,128)(2,1)}) %all-gather.28.cloned.1.call-update) | async-done | bytes 8388624 | tf_op jit(solution)/shard_map/all_gather | solution.py:193
  604.4 21.7 %multiply_convert_fusion.1 = (bf16[1024,2048]{1,0:T(8,128)(2,1)}, bf16[1024,2048]{1,0:T(8,128)(2,1)}, bf16[1024,2048]{1,0:T(8,128)(2,1)}) fusion(f32[1024,2048]{1,0:T(8,128)} %fusion.132, f32[1024,2048]{1,0:T(8,128)} %fusion.133, bf16[1024,2048]{1,0:T(8,128)(2,1)} %all-gather.30.cloned.1.call-done, bf16[2048,2048]{1,0:T(8,128)(2,1)} %all-gather.28.cloned.1.call-done), kind=kOutput, calls=%fused_computation.12 | convolution fusion | flops 8623489024 | bytes 41943040 | tf_op jit(solution)/shard_map/dot_general | solution.py:70
  626.1 12.9 fusion.134
  639.0 12.9 add_convert_fusion.1
  652.0 50.9 %reduce-scatter.16.cloned.1.call-done = bf16[256,2048]{1,0:T(8,128)(2,1)} async-done(((bf16[1024,2048]{1,0:T(8,128)(2,1)}), bf16[256,2048]{1,0:T(8,128)(2,1)}) %reduce-scatter.16.cloned.1.call-update) | async-done | bytes 1048592 | tf_op jit(solution)/shard_map/reduce_scatter | solution.py:255
  709.4 14.4 %convolution_convert_fusion.1 = bf16[2048,2048]{1,0:T(8,128)(2,1)} fusion(bf16[1024,2048]{1,0:T(8,128)(2,1)} %all-gather.22.cloned.1.call-done, bf16[1024,2048]{1,0:T(8,128)(2,1)} %get-tuple-element.73), kind=kOutput, calls=%fused_computation.20 | convolution fusion | flops 8594128896 | bytes 16777216 | tf_op jit(solution)/shard_map/dot_general | solution.py:64
  723.8 14.1 %convolution_convert_fusion.2 = bf16[2048,2048]{1,0:T(8,128)(2,1)} fusion(bf16[1024,2048]{1,0:T(8,128)(2,1)} %all-gather.22.cloned.1.call-done, bf16[1024,2048]{1,0:T(8,128)(2,1)} %get-tuple-element.74), kind=kOutput, calls=%fused_computation.21 | convolution fusion | flops 8594128896 | bytes 16777216 | tf_op jit(solution)/shard_map/dot_general | solution.py:64
  738.0 14.3 %convolution_convert_fusion = bf16[2048,2048]{1,0:T(8,128)(2,1)} fusion(bf16[1024,2048]{1,0:T(8,128)(2,1)} %get-tuple-element.75, bf16[1024,2048]{1,0:T(8,128)(2,1)} %all-gather.30.cloned.1.call-done), kind=kOutput, calls=%fused_computation.19 | convolution fusion | flops 8594128896 | bytes 16777216 | tf_op jit(solution)/shard_map/dot_general | solution.py:64
  752.5 9.6 all-gather.32.cloned.1.call-done
  803.5 20.9 %fusion.89 = f32[512,4,128]{2,0,1:T(8,128)} fusion(f32[4,512,1024]{2,1,0:T(8,128)} %fusion.136, f32[4,512,1024]{2,1,0:T(8,128)} %copy-done.6, f32[4,512]{1,0:T(4,128)S(1)} %log_add_fusion, pred[512,1024]{1,0:T(8,128)(4,1)S(1)} %copy-done.20, bf16[1024,4,64]{2,0,1:T(8,128)(2,1)S(1)} %copy-done.13, bf16[1024,4,64]{2,0,1:T(8,128)(2,1)S(1)} %copy-done.11), kind=kOutput, calls=%fused_computation.113 | convolution fusion | flops 562039808 | bytes 19406848 | tf_op jit(solution)/shard_map/hqk,khd->qhd/dot_general | solution.py:144
  833.8 26.0 %bitcast_add_fusion.1 = f32[1024,4,128]{2,0,1:T(8,128)} fusion(f32[512,4,128]{2,0,1:T(8,128)S(1)} %copy-done.63, bf16[512,4,128]{2,0,1:T(8,128)(2,1)S(1)} %copy-done.25, f32[4,512,1024]{2,1,0:T(8,128)} %fusion.136, f32[4,512,1024]{2,1,0:T(8,128)} %copy-done.6, f32[4,512]{1,0:T(4,128)S(1)} %log_add_fusion, pred[512,1024]{1,0:T(8,128)(4,1)S(1)} %copy-done.20), kind=kOutput, calls=%fused_computation.79 | convolution fusion | flops 560466944 | bytes 20979712 | tf_op jit(solution)/shard_map/hqk,qhd->khd/dot_general | solution.py:152
  895.9 13.9 %convolution_convert_fusion.3 = bf16[1024,2048]{1,0:T(8,128)(2,1)} fusion(bf16[1024,2048]{1,0:T(8,128)(2,1)} %get-tuple-element.75, bf16[2048,2048]{1,0:T(8,128)(2,1)} %all-gather.28.cloned.1.call-done), kind=kOutput, calls=%fused_computation.48 | convolution fusion | flops 8592031744 | bytes 16777216 | tf_op jit(solution)/shard_map/dot_general | solution.py:228
  912.7 31.3 %reduce-scatter.28.cloned.1.call-done = bf16[256,2048]{1,0:T(8,128)(2,1)} async-done(((bf16[2048,2048]{1,0:T(8,128)(2,1)}), bf16[256,2048]{1,0:T(8,128)(2,1)}) %reduce-scatter.28.cloned.1.call-update) | async-done | bytes 1048592 | tf_op jit(solution)/shard_map/reduce_scatter | solution.py:305
  946.8 87.4 %reduce-scatter.32.cloned.1.call-done = bf16[2048,256]{1,0:T(8,128)(2,1)} async-done(((bf16[2048,2048]{1,0:T(8,128)(2,1)}), bf16[2048,256]{1,0:T(8,128)(2,1)}) %reduce-scatter.32.cloned.1.call-update) | async-done | bytes 1048592 | tf_op jit(solution)/shard_map/reduce_scatter | solution.py:311
  1036.9 34.0 %reduce-scatter.26.cloned.1.call-done = bf16[512,256]{1,0:T(8,128)(2,1)} async-done(((bf16[512,2048]{1,0:T(8,128)(2,1)}), bf16[512,256]{1,0:T(8,128)(2,1)}) %reduce-scatter.26.cloned.1.call-update) | async-done | bytes 262160 | tf_op jit(solution)/shard_map/reduce_scatter | solution.py:302
  1072.6 35.1 %reduce-scatter.24.cloned.1.call-done = bf16[256,512]{1,0:T(8,128)(2,1)} async-done(((bf16[2048,512]{1,0:T(8,128)(2,1)}), bf16[256,512]{1,0:T(8,128)(2,1)}) %reduce-scatter.24.cloned.1.call-update) | async-done | bytes 262160 | tf_op jit(solution)/shard_map/reduce_scatter | solution.py:299
  1109.5 35.2 %reduce-scatter.20.cloned.1.call-done = bf16[256,512]{1,0:T(8,128)(2,1)} async-done(((bf16[2048,512]{1,0:T(8,128)(2,1)}), bf16[256,512]{1,0:T(8,128)(2,1)}) %reduce-scatter.20.cloned.1.call-update) | async-done | bytes 262160 | tf_op jit(solution)/shard_map/reduce_scatter | solution.py:293
  1146.5 35.0 %reduce-scatter.22.cloned.1.call-done = bf16[256,512]{1,0:T(8,128)(2,1)} async-done(((bf16[2048,512]{1,0:T(8,128)(2,1)}), bf16[256,512]{1,0:T(8,128)(2,1)}) %reduce-scatter.22.cloned.1.call-update) | async-done | bytes 262160 | tf_op jit(solution)/shard_map/reduce_scatter | solution.py:296
  1183.3 52.4 %reduce-scatter.18.cloned.1.call-done = bf16[256,2048]{1,0:T(8,128)(2,1)} async-done(((bf16[1024,2048]{1,0:T(8,128)(2,1)}), bf16[256,2048]{1,0:T(8,128)(2,1)}) %reduce-scatter.18.cloned.1.call-update) | async-done | bytes 1048592 | tf_op jit(solution)/shard_map/reduce_scatter | solution.py:280
  1239.4 51.9 %reduce-scatter.14.cloned.1.call-done = bf16[256,2048]{1,0:T(8,128)(2,1)} async-done(((bf16[1024,2048]{1,0:T(8,128)(2,1)}), bf16[256,2048]{1,0:T(8,128)(2,1)}) %reduce-scatter.14.cloned.1.call-update) | async-done | bytes 1048592 | tf_op jit(solution)/shard_map/reduce_scatter | solution.py:227
  (267 shorter events, 191.0 us)
Async XLA Ops:
  7.2 34.3 %all-gather.18.cloned.1.call-start = ((), (), s32[]{:S(2)}) async-start(), calls=%async_computation.14 | async-start | bytes 2359296 | tf_op jit(solution)/shard_map/all_gather | solution.py:188
  7.9 88.0 %all-gather.12.cloned.1.call-start = ((), (), s32[]{:S(2)}) async-start(), calls=%async_computation.11 | async-start | bytes 5242880 | tf_op jit(solution)/shard_map/all_gather | solution.py:197
  14.7 112.0 %all-gather.16.cloned.1.call-start = ((), (), s32[]{:S(2)}) async-start(), calls=%async_computation.13 | async-start | bytes 2359296 | tf_op jit(solution)/shard_map/all_gather | solution.py:187
  15.5 141.3 %all-gather.14.cloned.1.call-start = ((), (), s32[]{:S(2)}) async-start(), calls=%async_computation.12 | async-start | bytes 2359296 | tf_op jit(solution)/shard_map/all_gather | solution.py:189
  16.1 172.2 %all-gather.20.cloned.1.call-start = ((), (), s32[]{:S(2)}) async-start(), calls=%async_computation.15 | async-start | bytes 2359296 | tf_op jit(solution)/shard_map/all_gather | solution.py:190
  16.6 229.4 %reduce-scatter.12.cloned.1.call-start = ((), (), s32[]{:S(2)}) async-start(), calls=%async_computation.16 | async-start | bytes 5242880 | tf_op jit(solution)/shard_map/reduce_scatter | solution.py:214
  194.2 135.5 %all-gather.26.cloned.1.call-start = ((), (), s32[]{:S(2)}) async-start(), calls=%async_computation.19 | async-start | bytes 9437184 | tf_op jit(solution)/shard_map/all_gather | solution.py:192
  195.0 188.2 %all-gather.22.cloned.1.call-start = ((), (), s32[]{:S(2)}) async-start(), calls=%async_computation.17 | async-start | bytes 5242880 | tf_op jit(solution)/shard_map/all_gather | solution.py:222
  247.7 459.1 %copy-start.39 = (f32[256]{0:T(256)}, f32[256]{0:T(256)S(1)}, u32[]{:S(2)}) copy-start(f32[256]{0:T(256)S(1)} %broadcast_multiply_fusion) | copy-start | bytes 3076
  249.5 457.3 %copy-start.47 = (f32[256]{0:T(256)}, f32[256]{0:T(256)S(1)}, u32[]{:S(2)}) copy-start(f32[256]{0:T(256)S(1)} %fusion.101) | copy-start | bytes 3076
  250.9 215.9 %all-gather.24.cloned.1.call-start = ((), (), s32[]{:S(2)}) async-start(), calls=%async_computation.18 | async-start | bytes 9437184 | tf_op jit(solution)/shard_map/all_gather | solution.py:191
  251.7 268.6 %all-gather.30.cloned.1.call-start = ((), (), s32[]{:S(2)}) async-start(), calls=%async_computation.22 | async-start | bytes 5242880 | tf_op jit(solution)/shard_map/all_gather | solution.py:245
  253.1 453.8 %copy-start.53 = (f32[256]{0:T(256)}, f32[256]{0:T(256)S(1)}, u32[]{:S(2)}) copy-start(f32[256]{0:T(256)S(1)} %dynamic-slice_convert_fusion) | copy-start | bytes 3076
  254.3 350.1 %all-gather.28.cloned.1.call-start = ((), (), s32[]{:S(2)}) async-start(), calls=%async_computation.20 | async-start | bytes 9437184 | tf_op jit(solution)/shard_map/all_gather | solution.py:193
  255.0 447.8 %reduce-scatter.16.cloned.1.call-start = ((), (), s32[]{:S(2)}) async-start(), calls=%async_computation.23 | async-start | bytes 5242880 | tf_op jit(solution)/shard_map/reduce_scatter | solution.py:255
  651.9 110.2 %all-gather.32.cloned.1.call-start = ((), (), s32[]{:S(2)}) async-start(), calls=%async_computation.24 | async-start | bytes 5242880 | tf_op jit(solution)/shard_map/all_gather | solution.py:264
  709.4 200.5 %reduce-scatter.30.cloned.1.call-start = ((), (), s32[]{:S(2)}) async-start(), calls=%async_computation.31 | async-start | bytes 9437184 | tf_op jit(solution)/shard_map/reduce_scatter | solution.py:308
  723.8 220.2 %reduce-scatter.28.cloned.1.call-start = ((), (), s32[]{:S(2)}) async-start(), calls=%async_computation.30 | async-start | bytes 9437184 | tf_op jit(solution)/shard_map/reduce_scatter | solution.py:305
  738.0 296.2 %reduce-scatter.32.cloned.1.call-start = ((), (), s32[]{:S(2)}) async-start(), calls=%async_computation.32 | async-start | bytes 9437184 | tf_op jit(solution)/shard_map/reduce_scatter | solution.py:311
  752.4 318.4 %reduce-scatter.26.cloned.1.call-start = ((), (), s32[]{:S(2)}) async-start(), calls=%async_computation.29 | async-start | bytes 2359296 | tf_op jit(solution)/shard_map/reduce_scatter | solution.py:302
  768.0 339.7 %reduce-scatter.24.cloned.1.call-start = ((), (), s32[]{:S(2)}) async-start(), calls=%async_computation.28 | async-start | bytes 2359296 | tf_op jit(solution)/shard_map/reduce_scatter | solution.py:299
  784.3 360.4 %reduce-scatter.20.cloned.1.call-start = ((), (), s32[]{:S(2)}) async-start(), calls=%async_computation.26 | async-start | bytes 2359296 | tf_op jit(solution)/shard_map/reduce_scatter | solution.py:293
  875.6 305.9 %reduce-scatter.22.cloned.1.call-start = ((), (), s32[]{:S(2)}) async-start(), calls=%async_computation.27 | async-start | bytes 2359296 | tf_op jit(solution)/shard_map/reduce_scatter | solution.py:296
  884.7 351.0 %reduce-scatter.18.cloned.1.call-start = ((), (), s32[]{:S(2)}) async-start(), calls=%async_computation.25 | async-start | bytes 5242880 | tf_op jit(solution)/shard_map/reduce_scatter | solution.py:280
  895.5 395.8 %reduce-scatter.14.cloned.1.call-start = ((), (), s32[]{:S(2)}) async-start(), calls=%async_computation.21 | async-start | bytes 5242880 | tf_op jit(solution)/shard_map/reduce_scatter | solution.py:227
  912.7 323.0 %copy-start.1 = (bf16[256,2048]{1,0:T(8,128)(2,1)S(1)}, bf16[256,2048]{1,0:T(8,128)(2,1)}, u32[]{:S(2)}) copy-start(bf16[256,2048]{1,0:T(8,128)(2,1)} %param.22) | copy-start | bytes 3145732
  912.7 323.0 %copy-start.42 = (f32[256]{0:T(256)S(1)}, f32[256]{0:T(256)}, u32[]{:S(2)}) copy-start(f32[256]{0:T(256)} %copy-done.41) | copy-start | bytes 3076
  946.8 290.7 %copy-start.58 = (f32[256]{0:T(256)S(1)}, f32[256]{0:T(256)}, u32[]{:S(2)}) copy-start(f32[256]{0:T(256)} %copy-done.57) | copy-start | bytes 3076
  946.8 290.7 %copy-start.50 = (f32[256]{0:T(256)S(1)}, f32[256]{0:T(256)}, u32[]{:S(2)}) copy-start(f32[256]{0:T(256)} %copy-done.49) | copy-start | bytes 3076
  1036.9 254.5 %copy-start.52 = (f32[256]{0:T(256)S(1)}, f32[256]{0:T(256)}, u32[]{:S(2)}) copy-start(f32[256]{0:T(256)} %copy-done.51) | copy-start | bytes 3076
  1036.9 254.5 %copy-start.54 = (f32[256]{0:T(256)S(1)}, f32[256]{0:T(256)}, u32[]{:S(2)}) copy-start(f32[256]{0:T(256)} %copy-done.53) | copy-start | bytes 3076
  1036.9 254.5 %copy-start.56 = (f32[256]{0:T(256)S(1)}, f32[256]{0:T(256)}, u32[]{:S(2)}) copy-start(f32[256]{0:T(256)} %copy-done.55) | copy-start | bytes 3076
  (57 other events, 1466.1 us)
Sparse Core Ops, SparseCore 0:
  9.6 31.8 all-gather.17
  43.9 51.9 all-gather.11
  97.5 29.1 all-gather.15
  128.2 28.5 all-gather.13
  158.2 30.0 all-gather.19
  194.4 51.6 reduce-scatter.11
  247.6 82.0 all-gather.25
  332.1 51.0 all-gather.21
  384.8 82.0 all-gather.23
  469.2 51.0 all-gather.29
  521.8 82.4 all-gather.27
  652.0 50.7 reduce-scatter.15
  709.5 52.5 all-gather.31
  764.3 89.5 reduce-scatter.29
  856.0 87.9 reduce-scatter.27
  946.1 87.9 reduce-scatter.31
  1036.3 34.5 reduce-scatter.25
  1073.0 34.6 reduce-scatter.23
  1110.0 34.6 reduce-scatter.19
  1146.8 34.5 reduce-scatter.21
  1184.4 51.2 reduce-scatter.17
  1238.7 52.5 reduce-scatter.13
where the time goes:
time: 1310 us; the launch traced here: 1300 us
  waiting for transfers between devices  921 us (70%)
  matrix products  281 us (21%)
  other arithmetic  67.1 us (5%)
  local copies, waits for them, and re-layouts  16.4 us (1%)
  between operations  15.6 us (1%)
    reduce_scatter x1, waiting for transfers between devices, per_device(): lax.psum_scatter(down_part.astype(jnp.bfloat16), 'dp', scatter_dimension=...  87.4 us
    all_gather x1, waiting for transfers between devices, per_device(): lax.all_gather(down_weight, 'dp', axis=1, tiled=True)  84.1 us
    all_gather x1, waiting for transfers between devices, per_device(): lax.all_gather(up_weight, 'dp', axis=0, tiled=True)  74.6 us
    all_gather x1, waiting for transfers between devices, per_device(): lax.all_gather(gate_weight, 'dp', axis=0, tiled=True)  68.9 us
    dot_general x7, matrix products, dot_first(): lax.dot_general(left, right, (((0,), (0,)), ((), ())), preferred_element_...  65 us
    dot_general x7, matrix products, dot_last(): lax.dot_general(left, right, (((1,), (1,)), ((), ())), preferred_element_...  64.1 us
    all_gather x1, waiting for transfers between devices, per_device(): gathered_one = lax.all_gather(normed_one, 'tensor', axis=0, tiled=True)  54.4 us
    all_gather x1, waiting for transfers between devices, per_device(): gathered_two = lax.all_gather(normed_two, 'tensor', axis=0, tiled=True)  53.5 us
  transfers between devices with their start and end apart: 22, of which 21 were waited for; matrix products, arithmetic and copies ran while one was open for 23% of the time, Pallas kernels for 0%

commit v1 on v0

v1 whole, which is shorter than its diff:
```python
import math

import jax
import jax.numpy as jnp
from jax import lax
from jax.experimental import pallas as pl
from jax.experimental.pallas import tpu as pltpu
from jax.sharding import PartitionSpec as P

HD = 128
EPSILON = 1e-05
ROPE_BASE = 10000.0
MASKED = -1e30
F32 = jnp.float32
BF16 = jnp.bfloat16


def norm_forward(rows):
    centre = jnp.mean(rows, axis=-1, keepdims=True)
    centered = rows - centre
    spread = jnp.mean(centered * centered, axis=-1, keepdims=True)
    inverse = lax.rsqrt(spread + EPSILON)
    return centered * inverse, inverse


def norm_backward(normed, inverse, grad):
    mean_grad = jnp.mean(grad, axis=-1, keepdims=True)
    mean_both = jnp.mean(grad * normed, axis=-1, keepdims=True)
    return (grad - mean_grad - normed * mean_both) * inverse


def slot_layout(lengths_row, row_total):
    ends = jnp.cumsum(lengths_row)
    places = jnp.arange(row_total, dtype=jnp.int32)
    segment = jnp.sum((places[:, None] >= ends[None, :]).astype(jnp.int32), axis=1)
    starts = jnp.concatenate([jnp.zeros((1,), jnp.int32), ends])
    picks = jnp.arange(starts.shape[0], dtype=jnp.int32)
    begins = jnp.sum(jnp.where(segment[:, None] == picks[None, :], starts[None, :], 0), axis=1)
    valid = (places < ends[-1]).astype(jnp.int32)
    return segment, places - begins, valid


def rope_wide(position):
    half = HD // 2
    steps = jnp.arange(half, dtype=F32)
    freqs = jnp.exp(steps * (-2.0 * math.log(ROPE_BASE) / HD))
    angles = position.astype(F32)[:, None] * freqs[None, :]
    cosine, sine = jnp.cos(angles), jnp.sin(angles)
    return (
        jnp.concatenate([cosine, cosine], axis=1),
        jnp.concatenate([-sine, sine], axis=1),
    )


def dot_plain(left, right):
    return jnp.dot(left, right, preferred_element_type=F32)


def dot_first(left, right):
    return lax.dot_general(left, right, (((0,), (0,)), ((), ())), preferred_element_type=F32)


def dot_last(left, right):
    return lax.dot_general(left, right, (((1,), (1,)), ((), ())), preferred_element_type=F32)


def after(value, *deps):
    return lax.optimization_barrier((value,) + deps)[0]


def core_swap(value):
    count = lax.axis_size("dp")
    return lax.ppermute(value, "dp", [(k, k ^ 1) for k in range(count)])


def ring_shift(value, step):
    count = lax.axis_size("dp")
    return lax.ppermute(value, "dp", [(k, (k + 2 * step) % count) for k in range(count)])


def slot_owner(slot):
    count = lax.axis_size("dp")
    index = lax.axis_index("dp")
    chip = (index // 2 + count // 2 - slot // 2) % (count // 2)
    return chip * 2 + (index % 2 + slot % 2) % 2


def to_slots(rows):
    count = lax.axis_size("dp")
    width = rows.shape[1] // count
    return jnp.concatenate(
        [
            lax.dynamic_slice_in_dim(rows, slot_owner(slot) * width, width, 1)
            for slot in range(count)
        ],
        axis=1,
    )


def from_slots(rows):
    count = lax.axis_size("dp")
    width = rows.shape[1] // count
    index = lax.axis_index("dp")
    pieces = []
    for owner in range(count):
        lag = (index // 2 + count // 2 - owner // 2) % (count // 2)
        slot = lag * 2 + (index % 2 + owner % 2) % 2
        pieces.append(lax.dynamic_slice_in_dim(rows, slot * width, width, 1))
    return jnp.concatenate(pieces, axis=1)


def gather_slots(own, axis):
    chips = lax.axis_size("dp") // 2
    pieces = []
    for lag in range(chips):
        if lag:
            own = ring_shift(own, 1)
        pieces += [own, core_swap(own)]
    return jnp.concatenate(pieces, axis=axis), own


def scatter_slots(grad, axis):
    count = lax.axis_size("dp")
    chips = count // 2
    width = grad.shape[axis] // count

    def part(slot):
        return lax.slice_in_dim(grad, slot * width, (slot + 1) * width, axis=axis)

    def pair(lag):
        return part(2 * lag).astype(F32) + core_swap(part(2 * lag + 1)).astype(F32)

    total = pair(chips - 1).astype(BF16)
    for lag in range(chips - 2, -1, -1):
        total = ring_shift(total, -1).astype(F32) + pair(lag)
        if lag:
            total = total.astype(BF16)
    return total


def flip(value, bits):
    return lax.ppermute(value, "tensor", [(k, k ^ bits) for k in range(lax.axis_size("tensor"))])


def gather_rows(own):
    group = lax.axis_size("tensor")
    if group != 4:
        bits = 1
        while bits < group:
            own = jnp.concatenate([own, flip(own, bits)], axis=0)
            bits *= 2
        return own
    half = own.shape[0] // 2
    one = flip(own, 1)
    two = flip(own, 2)
    far_top = flip(one[:half], 2)
    far_low = flip(two[half:], 1)
    return jnp.concatenate([own, one, two, far_top, far_low], axis=0)


def scatter_rows(parts):
    group = lax.axis_size("tensor")
    if group != 4:
        while len(parts) > 1:
            bits = len(parts) // 2
            parts = [
                parts[j].astype(F32) + flip(parts[j + bits].astype(BF16), bits).astype(F32)
                for j in range(bits)
            ]
        return parts[0]
    half = parts[0].shape[0] // 2
    top = flip(parts[3][:half], 1)
    low = flip(parts[3][half:], 2)
    one_top = flip(parts[1][:half], 1)
    two_low = flip(parts[2][half:], 2)
    one_low = flip((parts[1][half:].astype(F32) + low.astype(F32)).astype(BF16), 1)
    two_top = flip((parts[2][:half].astype(F32) + top.astype(F32)).astype(BF16), 2)
    ones = jnp.concatenate([one_top, one_low], axis=0).astype(F32)
    twos = jnp.concatenate([two_top, two_low], axis=0).astype(F32)
    return parts[0].astype(F32) + ones + twos


def scores_of(q, k, seg_q, seg_k, row_base):
    s = lax.dot_general(q, k, (((1,), (1,)), ((), ())), preferred_element_type=F32) * (HD**-0.5)
    rows = lax.broadcasted_iota(jnp.int32, s.shape, 0) + row_base
    cols = lax.broadcasted_iota(jnp.int32, s.shape, 1)
    return jnp.where((seg_q == seg_k) & (rows >= cols), s, MASKED)


def softmax_of(s):
    peak = jnp.max(s, axis=-1, keepdims=True)
    e = jnp.exp(s - peak)
    return e * (1.0 / jnp.sum(e, axis=-1, keepdims=True))


def attend_kernel(blocks, t_ref, q_ref, k_ref, v_ref, segc_ref, segr_ref, out_ref, kt, vt):
    size = q_ref.shape[0] // blocks
    t = t_ref[0]

    def rows(block):
        return pl.ds(pl.multiple_of((block ^ t) * size, size), size)

    for b in range(blocks):
        kt[b * size : (b + 1) * size, :] = k_ref[rows(b), :]
        vt[b * size : (b + 1) * size, :] = v_ref[rows(b), :]
    for b in range(blocks):
        n = (b + 1) * size
        s = scores_of(
            q_ref[rows(b), :],
            kt[:n, :],
            segc_ref[b * size : n, :],
            segr_ref[:, :n],
            b * size,
        )
        p = softmax_of(s).astype(BF16)
        out_ref[rows(b), :] = jnp.dot(p, vt[:n, :], preferred_element_type=F32).astype(BF16)


def attend_forward(t, q, k, v, segc, segr):
    rows, width = q.shape
    blocks = lax.axis_size("tensor")
    head = pl.BlockSpec((rows, HD), lambda h, t: (0, h))

    def kernel(*refs):
        attend_kernel(blocks, *refs)

    return pl.pallas_call(
        kernel,
        out_shape=jax.ShapeDtypeStruct((rows, width), BF16),
        grid_spec=pltpu.PrefetchScalarGridSpec(
            num_scalar_prefetch=1,
            grid=(width // HD,),
            in_specs=[
                head,
                head,
                head,
                pl.BlockSpec((rows, 1), lambda h, t: (0, 0)),
                pl.BlockSpec((1, rows), lambda h, t: (0, 0)),
            ],
            out_specs=head,
            scratch_shapes=[pltpu.VMEM((rows, HD), BF16)] * 2,
        ),
        cost_estimate=pl.CostEstimate(
            flops=4 * rows * rows * width, bytes_accessed=8 * rows * width, transcendentals=rows * rows
        ),
    )(t, q, k, v, segc, segr)


def unattend_kernel(
    blocks, t_ref, q_ref, k_ref, v_ref, g_ref, segc_ref, segr_ref, cos_ref, sin_ref,
    dq_ref, dk_ref, dv_ref, kt, vt, dka, dva,
):
    size = q_ref.shape[0] // blocks
    t = t_ref[0]

    def rows(block):
        return pl.ds(pl.multiple_of((block ^ t) * size, size), size)

    def turn_back(grad, b):
        lo, hi = b * size, (b + 1) * size
        return grad * cos_ref[lo:hi, :] - pltpu.roll(grad, HD // 2, 1) * sin_ref[lo:hi, :]

    for b in range(blocks):
        kt[b * size : (b + 1) * size, :] = k_ref[rows(b), :]
        vt[b * size : (b + 1) * size, :] = v_ref[rows(b), :]
    for b in range(blocks - 1, -1, -1):
        n = (b + 1) * size
        q = q_ref[rows(b), :]
        g = g_ref[rows(b), :]
        s = scores_of(q, kt[:n, :], segc_ref[b * size : n, :], segr_ref[:, :n], b * size)
        p = softmax_of(s)
        dp = lax.dot_general(g, vt[:n, :], (((1,), (1,)), ((), ())), preferred_element_type=F32)
        pdp = p * dp
        delta = jnp.sum(pdp, axis=-1, keepdims=True)
        raw = ((pdp - p * delta) * (HD**-0.5)).astype(BF16)
        dq = jnp.dot(raw, kt[:n, :], preferred_element_type=F32)
        dq_ref[rows(b), :] = turn_back(dq, b).astype(BF16)
        dk = lax.dot_general(raw, q, (((0,), (0,)), ((), ())), preferred_element_type=F32)
        dv = lax.dot_general(
            p.astype(BF16), g, (((0,), (0,)), ((), ())), preferred_element_type=F32
        )
        if b == blocks - 1:
            dka[...] = dk
            dva[...] = dv
        else:
            dka[:n, :] += dk
            dva[:n, :] += dv
    for b in range(blocks):
        lo, hi = b * size, (b + 1) * size
        dk_ref[rows(b), :] = turn_back(dka[lo:hi, :], b).astype(BF16)
        dv_ref[rows(b), :] = dva[lo:hi, :].astype(BF16)


def attend_backward(t, q, k, v, g, segc, segr, cos, sin):
    rows, width = q.shape
    blocks = lax.axis_size("tensor")
    head = pl.BlockSpec((rows, HD), lambda h, t: (0, h))
    table = pl.BlockSpec((rows, HD), lambda h, t: (0, 0))

    def kernel(*refs):
        unattend_kernel(blocks, *refs)

    return pl.pallas_call(
        kernel,
        out_shape=[jax.ShapeDtypeStruct((rows, width), BF16)] * 3,
        grid_spec=pltpu.PrefetchScalarGridSpec(
            num_scalar_prefetch=1,
            grid=(width // HD,),
            in_specs=[
                head,
                head,
                head,
                head,
                pl.BlockSpec((rows, 1), lambda h, t: (0, 0)),
                pl.BlockSpec((1, rows), lambda h, t: (0, 0)),
                table,
                table,
            ],
            out_specs=[head, head, head],
            scratch_shapes=[pltpu.VMEM((rows, HD), BF16)] * 2 + [pltpu.VMEM((rows, HD), F32)] * 2,
        ),
        cost_estimate=pl.CostEstimate(
            flops=10 * rows * rows * width, bytes_accessed=14 * rows * width, transcendentals=rows * rows
        ),
    )(t, q, k, v, g, segc, segr, cos, sin)


def rotate(values, cos, sin):
    rows, width = values.shape
    heads = values.reshape(rows, width // HD, HD)
    swapped = jnp.concatenate([heads[..., HD // 2 :], heads[..., : HD // 2]], axis=-1)
    turned = heads * cos[:, None, :] + swapped * sin[:, None, :]
    return turned.reshape(rows, width).astype(BF16)


def per_device(
    tokens,
    lengths,
    query_weight,
    key_weight,
    value_weight,
    output_weight,
    gate_weight,
    up_weight,
    down_weight,
    cotangent,
):
    local = tokens.shape[0]
    group = lax.axis_size("tensor")
    t = lax.axis_index("tensor")
    slot_rows = local * group
    heads_width = query_weight.shape[1]
    hidden_width = gate_weight.shape[1]
    half_heads = heads_width // 2
    half_hidden = hidden_width // 2
    t_arg = t.astype(jnp.int32).reshape(1)

    segment, position, valid_all = slot_layout(lengths[0], slot_rows)
    valid = lax.dynamic_slice_in_dim(valid_all, t * local, local, 0).astype(F32)[:, None]
    cos, sin = rope_wide(position)
    segc, segr = segment[:, None], segment[None, :]

    def mine(table, j):
        return lax.dynamic_slice_in_dim(table, (t ^ j) * local, local, 0)

    cos_x = jnp.concatenate([mine(cos, j) for j in range(group)], axis=0)
    sin_x = jnp.concatenate([mine(sin, j) for j in range(group)], axis=0)

    heads_own = [
        jnp.concatenate(
            [w[:, a * half_heads : (a + 1) * half_heads] for w in (query_weight, key_weight, value_weight)],
            axis=1,
        )
        for a in range(2)
    ]
    gate_own = [gate_weight[:, a * half_hidden : (a + 1) * half_hidden] for a in range(2)]
    up_own = [up_weight[:, a * half_hidden : (a + 1) * half_hidden] for a in range(2)]
    down_own = [down_weight[a * half_hidden : (a + 1) * half_hidden, :] for a in range(2)]
    lanes = (
        [("a", heads_own[0], 0), ("o", output_weight, 1), ("u0", up_own[0], 0), ("g1", gate_own[1], 0), ("d1", down_own[1], 1)],
        [("b", heads_own[1], 0), ("g0", gate_own[0], 0), ("d0", down_own[0], 1), ("u1", up_own[1], 0)],
    )
    full = {}
    for lane in lanes:
        last = None
        for name, own, axis in lane:
            if last is not None:
                own = after(own, last)
            full[name], last = gather_slots(own, axis)

    residual = to_slots(tokens).astype(F32)
    grad_out = to_slots(cotangent).astype(F32) * valid
    normed_one, inverse_one = norm_forward(residual)
    h1 = gather_rows(normed_one.astype(BF16))
    g_rows = gather_rows(after(grad_out.astype(BF16), h1))

    q_parts, k_parts, v_parts, c_parts = [], [], [], []
    for name in ("a", "b"):
        pre = dot_plain(h1, full[name])
        q = rotate(pre[:, :half_heads], cos_x, sin_x)
        k = rotate(pre[:, half_heads : 2 * half_heads], cos_x, sin_x)
        v = pre[:, 2 * half_heads :].astype(BF16)
        q_parts.append(q)
        k_parts.append(k)
        v_parts.append(v)
        c_parts.append(attend_forward(t_arg, q, k, v, segc, segr))
    context = jnp.concatenate(c_parts, axis=1)

    def row_piece(value, j):
        return value[j * local : (j + 1) * local]

    attention = scatter_rows(
        [dot_plain(row_piece(context, j), full["o"]).astype(BF16) for j in range(group)]
    )
    middle = residual + attention
    normed_two, inverse_two = norm_forward(middle)
    h2 = gather_rows(normed_two.astype(BF16))

    feed = [None] * group
    d_normed = [None] * group
    sums = {}
    for a in range(2):
        gate_w, up_w, down_w = full[f"g{a}"], full[f"u{a}"], full[f"d{a}"]
        d_hidden = dot_last(g_rows, down_w)
        gate = dot_plain(h2, gate_w)
        up = dot_plain(h2, up_w)
        sg = jax.nn.sigmoid(gate)
        act = gate * sg
        hidden = (act * up).astype(BF16)
        d_gate = (d_hidden * up * sg * (1.0 + gate * (1.0 - sg))).astype(BF16)
        d_up = (d_hidden * act).astype(BF16)
        sums[f"d{a}"] = scatter_slots(dot_first(hidden, g_rows).astype(BF16), 1)
        sums[f"g{a}"] = scatter_slots(dot_first(h2, d_gate).astype(BF16), 0)
        sums[f"u{a}"] = scatter_slots(dot_first(h2, d_up).astype(BF16), 0)
        for j in range(group):
            f = dot_plain(row_piece(hidden, j), down_w)
            d = dot_last(row_piece(d_gate, j), gate_w) + dot_last(row_piece(d_up, j), up_w)
            feed[j] = f if a == 0 else feed[j] + f
            d_normed[j] = d if a == 0 else d_normed[j] + d
    d_normed_two = scatter_rows([d.astype(BF16) for d in d_normed])
    d_middle = grad_out + norm_backward(normed_two, inverse_two, d_normed_two)
    d_attention = gather_rows(d_middle.astype(BF16))

    feed_out = scatter_rows([f.astype(BF16) for f in feed])
    output = from_slots((valid * (middle + feed_out)).astype(BF16))

    d_context = dot_last(d_attention, full["o"]).astype(BF16)
    sums["o"] = scatter_slots(dot_first(context, d_attention).astype(BF16), 1)
    d_one = [None] * group
    for a, name in enumerate(("a", "b")):
        d_q, d_k, d_v = attend_backward(
            t_arg,
            q_parts[a],
            k_parts[a],
            v_parts[a],
            d_context[:, a * half_heads : (a + 1) * half_heads],
            segc,
            segr,
            cos,
            sin,
        )
        d_pre = jnp.concatenate([d_q, d_k, d_v], axis=1)
        sums[name] = scatter_slots(dot_first(h1, d_pre).astype(BF16), 0)
        for j in range(group):
            d = dot_last(row_piece(d_pre, j), full[name])
            d_one[j] = d if a == 0 else d_one[j] + d
    d_normed_one = scatter_rows([d.astype(BF16) for d in d_one])
    input_grad = from_slots(
        (d_middle + norm_backward(normed_one, inverse_one, d_normed_one)).astype(BF16)
    )

    def heads_grad(which):
        lo, hi = which * half_heads, (which + 1) * half_heads
        return jnp.concatenate([sums["a"][:, lo:hi], sums["b"][:, lo:hi]], axis=1)

    return (
        output,
        input_grad,
        heads_grad(0),
        heads_grad(1),
        heads_grad(2),
        sums["o"],
        jnp.concatenate([sums["g0"], sums["g1"]], axis=1),
        jnp.concatenate([sums["u0"], sums["u1"]], axis=1),
        jnp.concatenate([sums["d0"], sums["d1"]], axis=0),
    )


def solution(mesh):
    return jax.shard_map(
        per_device,
        mesh=mesh,
        in_specs=(
            P(("dp", "tensor"), None),
            P("dp", None),
            P("dp", "tensor"),
            P("dp", "tensor"),
            P("dp", "tensor"),
            P("tensor", "dp"),
            P("dp", "tensor"),
            P("dp", "tensor"),
            P("tensor", "dp"),
            P(("dp", "tensor"), None),
        ),
        out_specs=(
            P(("dp", "tensor"), None),
            P(("dp", "tensor"), None),
            P("dp", "tensor"),
            P("dp", "tensor"),
            P("dp", "tensor"),
            P("tensor", "dp"),
            P("dp", "tensor"),
            P("dp", "tensor"),
            P("tensor", "dp"),
        ),
        check_vma=False,
    )
```

time: 1310 us -> 1020 us (0.78)
  waiting for transfers between devices: 921 us -> 412 us
  starting transfers between devices: 1.43 us -> 146 us
  local copies, waits for them, and re-layouts: 16.4 us -> 146 us
  matrix products: 281 us -> 210 us
  Pallas kernels: 0 us -> 34.4 us
    reduce_scatter x11 -> x0, waiting for transfers between devices: 464 us -> none  [the longest x1 87.4 us: per_device(): lax.psum_scatter(down_part.astype(jnp.bfloat16), 'dp', scatter_dimension=...]
    all_gather x11 -> x0, waiting for transfers between devices: 452 us -> none  [the longest x1 84.1 us: per_device(): lax.all_gather(down_weight, 'dp', axis=1, tiled=True)]
    ppermute x0 -> x166, waiting for transfers between devices: none -> 412 us  [the longest x54 304 us: ring_shift(): lax.ppermute(value, 'dp', [(k, (k + 2 * step) % count) for k in range(cou...]
    ppermute x0 -> x166, starting transfers between devices: none -> 146 us  [the longest x54 92.7 us: ring_shift(): lax.ppermute(value, 'dp', [(k, (k + 2 * step) % count) for k in range(cou...]
    dot_general x19 -> x18, matrix products: 152 us -> 79.8 us  [dot_plain(): return jnp.dot(left, right, preferred_element_type=F32)]
    unnamed x138 -> x314, local copies, waits for them, and re-layouts: 13.6 us -> 85.3 us
    slice x7 -> x45, local copies, waits for them, and re-layouts: 0.39 us -> 38.6 us  [the longest x4 11.9 us: rotate(): heads[..., HD // 2:]]
    pallas_call x0 -> x4, Pallas kernels: none -> 34.4 us  [the longest x2 20.8 us: attend_backward(): pl.pallas_call(kernel, out_shape=[jax.ShapeDtypeStruct((rows, width), BF1...]
  transfers between devices with their start and end apart: 22 -> 166, of which waited for: 21 -> 57; matrix products, arithmetic and copies ran while one was open for 23% -> 30% of each run, Pallas kernels for 0% -> 2%
where the time goes in v1:
time: 1020 us; the launch traced here: 1010 us
  waiting for transfers between devices  412 us (40%)
  matrix products  210 us (21%)
  local copies, waits for them, and re-layouts  146 us (14%)
  starting transfers between devices  146 us (14%)
  other arithmetic  61 us (6%)
  Pallas kernels  34.4 us (3%)
    ppermute x54, waiting for transfers between devices, ring_shift(): lax.ppermute(value, 'dp', [(k, (k + 2 * step) % count) for k in range(cou...  304 us
    ppermute x40, waiting for transfers between devices, flip(): lax.ppermute(value, 'tensor', [(k, k ^ bits) for k in range(lax.axis_size...  108 us
    ppermute x54, starting transfers between devices, ring_shift(): lax.ppermute(value, 'dp', [(k, (k + 2 * step) % count) for k in range(cou...  92.7 us
    unnamed x314, local copies, waits for them, and re-layouts  85.3 us
    dot_general x18, matrix products, dot_plain(): return jnp.dot(left, right, preferred_element_type=F32)  79.8 us
    dot_general x27, matrix products, dot_last(): lax.dot_general(left, right, (((1,), (1,)), ((), ())), preferred_element_...  76.2 us
    dot_general x9, matrix products, dot_first(): lax.dot_general(left, right, (((0,), (0,)), ((), ())), preferred_element_...  53.5 us
    ppermute x40, starting transfers between devices, flip(): lax.ppermute(value, 'tensor', [(k, k ^ bits) for k in range(lax.axis_size...  40 us
  transfers between devices with their start and end apart: 166, of which 57 were waited for; matrix products, arithmetic and copies ran while one was open for 30% of the time, Pallas kernels for 2%

profile of v1, /device:TPU:0, one launch (start us, length us, event | category | flops | bytes accessed | tf_op | source)
XLA Modules:
  0.0 1012.4 jit_solution(11141713008300449958)
XLA Ops:
  104.2 7.4 collective-permute-done.19
  202.6 8.2 collective-permute-done.43
  219.0 8.4 collective-permute-done.40
  239.9 13.5 %collective-permute-done.86 = bf16[128,2048]{1,0:T(8,128)(2,1)S(1)} collective-permute-done((bf16[128,2048]{1,0:T(8,128)(2,1)S(1)}, bf16[128,2048]{1,0:T(8,128)(2,1)S(1)}, u32[]{:S(2)}, u32[]{:S(2)}) %collective-permute-start.86) | collective-permute-done | bytes 524320 | tf_op jit(solution)/shard_map/ppermute | solution.py:142
  270.3 11.1 %collective-permute-done.47 = bf16[256,1024]{1,0:T(8,128)(2,1)S(1)} collective-permute-done((bf16[256,1024]{1,0:T(8,128)(2,1)S(1)}, bf16[256,1024]{1,0:T(8,128)(2,1)S(1)}, u32[]{:S(2)}, u32[]{:S(2)}) %collective-permute-start.47) | collective-permute-done | bytes 524320 | tf_op jit(solution)/shard_map/ppermute | solution.py:78
  283.5 9.1 collective-permute-done.52
  292.7 11.2 %collective-permute-done.57 = bf16[256,1024]{1,0:T(8,128)(2,1)S(1)} collective-permute-done((bf16[256,1024]{1,0:T(8,128)(2,1)S(1)}, bf16[256,1024]{1,0:T(8,128)(2,1)S(1)}, u32[]{:S(2)}, u32[]{:S(2)}) %collective-permute-start.57) | collective-permute-done | bytes 524320 | tf_op jit(solution)/shard_map/ppermute | solution.py:78
  305.7 9.4 collective-permute-done.54
  316.9 11.2 %collective-permute-done.32 = bf16[256,2048]{1,0:T(8,128)(2,1)S(1)} collective-permute-done((bf16[256,2048]{1,0:T(8,128)(2,1)S(1)}, bf16[256,2048]{1,0:T(8,128)(2,1)S(1)}, u32[]{:S(2)}, u32[]{:S(2)}) %collective-permute-start.32) | collective-permute-done | bytes 1048608 | tf_op jit(solution)/shard_map/ppermute | solution.py:142
  352.8 9.8 multiply_convert_fusion.3
  398.1 14.2 %collective-permute-done.71 = bf16[1024,256]{1,0:T(8,128)(2,1)S(1)} collective-permute-done((bf16[1024,256]{1,0:T(8,128)(2,1)S(1)}, bf16[1024,256]{1,0:T(8,128)(2,1)S(1)}, u32[]{:S(2)}, u32[]{:S(2)}) %collective-permute-start.71) | collective-permute-done | bytes 524320 | tf_op jit(solution)/shard_map/ppermute | solution.py:78
  424.9 9.3 collective-permute-done.153
  434.2 14.1 %collective-permute-start.125 = (bf16[256,1024]{0,1:T(8,128)(2,1)S(1)}, bf16[256,1024]{0,1:T(8,128)(2,1)S(1)}, u32[]{:S(2)}, u32[]{:S(2)}) collective-permute-start(bf16[256,1024]{0,1:T(8,128)(2,1)S(1)} %add_convert_fusion.17), channel_id=1, source_target_pairs={{0,24},{4,28},{8,0},{12,4},{16,8},{20,12},{24,16},{28,20},{1,25},{... | collective-permute-start | bytes 1572872 | tf_op jit(solution)/shard_map/ppermute | solution.py:78
  449.5 11.2 %collective-permute-done.125 = bf16[256,1024]{0,1:T(8,128)(2,1)S(1)} collective-permute-done((bf16[256,1024]{0,1:T(8,128)(2,1)S(1)}, bf16[256,1024]{0,1:T(8,128)(2,1)S(1)}, u32[]{:S(2)}, u32[]{:S(2)}) %collective-permute-start.125) | collective-permute-done | bytes 524320 | tf_op jit(solution)/shard_map/ppermute | solution.py:78
  462.3 9.4 collective-permute-done.73
  475.9 8.3 fusion.157
  499.8 9.2 collective-permute-done.127
  533.4 10.0 collective-permute-done.143
  544.6 8.4 collective-permute-done.129
  555.1 8.4 fusion.159
  563.5 9.1 multiply_convert_fusion.1
  661.8 10.3 %collective-permute-done.80 = bf16[128,2048]{1,0:T(8,128)(2,1)S(1)} collective-permute-done((bf16[128,2048]{1,0:T(8,128)(2,1)S(1)}, bf16[128,2048]{1,0:T(8,128)(2,1)S(1)}, u32[]{:S(2)}, u32[]{:S(2)}) %collective-permute-start.80) | collective-permute-done | bytes 524320 | tf_op jit(solution)/shard_map/ppermute | solution.py:142
  682.6 15.6 %collective-permute-done.78 = bf16[128,2048]{1,0:T(8,128)(2,1)S(1)} collective-permute-done((bf16[128,2048]{1,0:T(8,128)(2,1)S(1)}, bf16[128,2048]{1,0:T(8,128)(2,1)S(1)}, u32[]{:S(2)}, u32[]{:S(2)}) %collective-permute-start.78) | collective-permute-done | bytes 524320 | tf_op jit(solution)/shard_map/ppermute | solution.py:142
  701.6 7.8 collective-permute-done.91
  721.2 8.3 collective-permute-done.81
  805.3 10.0 collective-permute-done.150
  816.3 10.3 %collective-permute-done.164 = bf16[1024,256]{1,0:T(8,128)(2,1)S(1)} collective-permute-done((bf16[1024,256]{1,0:T(8,128)(2,1)S(1)}, bf16[1024,256]{1,0:T(8,128)(2,1)S(1)}, u32[]{:S(2)}, u32[]{:S(2)}) %collective-permute-start.164) | collective-permute-done | bytes 524320 | tf_op jit(solution)/shard_map/ppermute | solution.py:78
  857.5 10.4 %shard_map.172 = (bf16[1024,256]{1,0:T(8,128)(2,1)}, bf16[1024,256]{1,0:T(8,128)(2,1)}, bf16[1024,256]{1,0:T(8,128)(2,1)}) custom-call(s32[1]{0:T(128)} %bitcast.2.refs_0_, bf16[1024,256]{1,0:T(8,128)(2,1)} %get-tuple-element.106.refs_1_, bf16[1024,256]{1,0:T(8,128)(2,1)} %get-tuple-element.105.refs_2_, bf16[1024,256]{1,0:T(8,128)(2,1)} %slice.1015.refs_3_, ...), custom_call_target="tpu_custom_call" | custom-call | flops 2684354560 | bytes 3670016 | tf_op jit(solution)/shard_map/pallas_call | solution.py:303
  871.1 7.4 convolution_convert_fusion.6
  888.1 10.4 %shard_map.171 = (bf16[1024,256]{1,0:T(8,128)(2,1)}, bf16[1024,256]{1,0:T(8,128)(2,1)}, bf16[1024,256]{1,0:T(8,128)(2,1)}) custom-call(s32[1]{0:T(128)} %bitcast.2.refs_0_, bf16[1024,256]{1,0:T(8,128)(2,1)} %get-tuple-element.141.refs_1_, bf16[1024,256]{1,0:T(8,128)(2,1)} %get-tuple-element.142.refs_2_, bf16[1024,256]{1,0:T(8,128)(2,1)} %slice.1016.refs_3_, ...), custom_call_target="tpu_custom_call" | custom-call | flops 2684354560 | bytes 3670016 | tf_op jit(solution)/shard_map/pallas_call | solution.py:303
  958.5 7.9 collective-permute-done.102
  966.6 7.5 collective-permute-done.101
  (827 shorter events, 691.7 us)
Async XLA Ops:
  3.7 58.0 %collective-permute-start.4 = (bf16[256,768]{1,0:T(8,128)(2,1)}, bf16[256,768]{1,0:T(8,128)(2,1)}, u32[]{:S(2)}, u32[]{:S(2)}) collective-permute-start(bf16[256,768]{1,0:T(8,128)(2,1)} %get-tuple-element.172), channel_id=1, source_target_pairs={{0,4},{4,0},{8,12},{12,8},{16,20},{20,16},{24,28},{28,24},{1,5},{5... | collective-permute-start | bytes 1179656 | tf_op jit(solution)/shard_map/ppermute | solution.py:73
  4.2 53.9 %collective-permute-start.5 = (bf16[256,768]{1,0:T(8,128)(2,1)}, bf16[256,768]{1,0:T(8,128)(2,1)}, u32[]{:S(2)}, u32[]{:S(2)}) collective-permute-start(bf16[256,768]{1,0:T(8,128)(2,1)} %get-tuple-element.172), channel_id=1, source_target_pairs={{0,8},{4,12},{8,16},{12,20},{16,24},{20,28},{24,0},{28,4},{1,9},{5... | collective-permute-start | bytes 1179656 | tf_op jit(solution)/shard_map/ppermute | solution.py:78
  7.6 57.7 %collective-permute-start.11 = (bf16[256,768]{1,0:T(8,128)(2,1)}, bf16[256,768]{1,0:T(8,128)(2,1)}, u32[]{:S(2)}, u32[]{:S(2)}) collective-permute-start(bf16[256,768]{1,0:T(8,128)(2,1)} %get-tuple-element.169), channel_id=1, source_target_pairs={{0,4},{4,0},{8,12},{12,8},{16,20},{20,16},{24,28},{28,24},{1,5},{5... | collective-permute-start | bytes 1179656 | tf_op jit(solution)/shard_map/ppermute | solution.py:73
  7.8 60.7 %collective-permute-start.12 = (bf16[256,768]{1,0:T(8,128)(2,1)}, bf16[256,768]{1,0:T(8,128)(2,1)}, u32[]{:S(2)}, u32[]{:S(2)}) collective-permute-start(bf16[256,768]{1,0:T(8,128)(2,1)} %get-tuple-element.169), channel_id=1, source_target_pairs={{0,8},{4,12},{8,16},{12,20},{16,24},{20,28},{24,0},{28,4},{1,9},{5... | collective-permute-start | bytes 1179656 | tf_op jit(solution)/shard_map/ppermute | solution.py:78
  28.1 56.1 %collective-permute-start = (bf16[256,2048]{1,0:T(8,128)(2,1)}, bf16[256,2048]{1,0:T(8,128)(2,1)}, u32[]{:S(2)}, u32[]{:S(2)}) collective-permute-start(bf16[256,2048]{1,0:T(8,128)(2,1)} %get-tuple-element.74), channel_id=1, source_target_pairs={{0,1},{1,0},{2,3},{3,2},{4,5},{5,4},{6,7},{7,6},{8,9},{9,8},{10,11... | collective-permute-start | bytes 3145736 | tf_op jit(solution)/shard_map/ppermute | solution.py:142
  103.3 76.4 %collective-permute-start.36 = (bf16[256,1024]{1,0:T(8,128)(2,1)}, bf16[256,1024]{1,0:T(8,128)(2,1)}, u32[]{:S(2)}, u32[]{:S(2)}) collective-permute-start(bf16[256,1024]{1,0:T(8,128)(2,1)} %get-tuple-element.24), channel_id=1, source_target_pairs={{0,8},{4,12},{8,16},{12,20},{16,24},{20,28},{24,0},{28,4},{1,9},{5... | collective-permute-start | bytes 1572872 | tf_op jit(solution)/shard_map/ppermute | solution.py:78
  103.4 77.8 %collective-permute-start.35 = (bf16[256,1024]{1,0:T(8,128)(2,1)}, bf16[256,1024]{1,0:T(8,128)(2,1)}, u32[]{:S(2)}, u32[]{:S(2)}) collective-permute-start(bf16[256,1024]{1,0:T(8,128)(2,1)} %get-tuple-element.24), channel_id=1, source_target_pairs={{0,4},{4,0},{8,12},{12,8},{16,20},{20,16},{24,28},{28,24},{1,5},{5... | collective-permute-start | bytes 1572872 | tf_op jit(solution)/shard_map/ppermute | solution.py:73
  113.9 62.3 %collective-permute-start.20 = (bf16[512,256]{1,0:T(8,128)(2,1)}, bf16[512,256]{1,0:T(8,128)(2,1)}, u32[]{:S(2)}, u32[]{:S(2)}) collective-permute-start(bf16[512,256]{1,0:T(8,128)(2,1)} %collective-permute-done.19), channel_id=1, source_target_pairs={{0,4},{4,0},{8,12},{12,8},{16,20},{20,16},{24,28},{28,24},{1,5},{5... | collective-permute-start | bytes 786440 | tf_op jit(solution)/shard_map/ppermute | solution.py:73
  117.3 58.7 %collective-permute-start.21 = (bf16[512,256]{1,0:T(8,128)(2,1)}, bf16[512,256]{1,0:T(8,128)(2,1)}, u32[]{:S(2)}, u32[]{:S(2)}) collective-permute-start(bf16[512,256]{1,0:T(8,128)(2,1)} %collective-permute-done.19), channel_id=1, source_target_pairs={{0,8},{4,12},{8,16},{12,20},{16,24},{20,28},{24,0},{28,4},{1,9},{5... | collective-permute-start | bytes 786440 | tf_op jit(solution)/shard_map/ppermute | solution.py:78
  136.8 75.4 %collective-permute-start.83 = (bf16[256,2048]{1,0:T(8,128)(2,1)}, bf16[256,2048]{1,0:T(8,128)(2,1)}, u32[]{:S(2)}, u32[]{:S(2)}) collective-permute-start(bf16[256,2048]{1,0:T(8,128)(2,1)} %fusion.44), channel_id=1, source_target_pairs={{0,1},{1,0},{2,3},{3,2},{4,5},{5,4},{6,7},{7,6},{8,9},{9,8},{10,11... | collective-permute-start | bytes 3145736 | tf_op jit(solution)/shard_map/ppermute | solution.py:142
  179.7 33.9 %collective-permute-start.84 = (bf16[256,2048]{1,0:T(8,128)(2,1)}, bf16[256,2048]{1,0:T(8,128)(2,1)S(1)}, u32[]{:S(2)}, u32[]{:S(2)}) collective-permute-start(bf16[256,2048]{1,0:T(8,128)(2,1)} %fusion.44), channel_id=1, source_target_pairs={{0,2},{1,3},{2,0},{3,1},{4,6},{5,7},{6,4},{7,5},{8,10},{9,11},{10,... | collective-permute-start | bytes 3145736 | tf_op jit(solution)/shard_map/ppermute | solution.py:142
  281.6 35.1 %collective-permute-start.31 = (bf16[256,2048]{1,0:T(8,128)(2,1)S(1)}, bf16[256,2048]{1,0:T(8,128)(2,1)S(1)}, u32[]{:S(2)}, u32[]{:S(2)}) collective-permute-start(bf16[256,2048]{1,0:T(8,128)(2,1)S(1)} %get-tuple-element.72), channel_id=1, source_target_pairs={{0,1},{1,0},{2,3},{3,2},{4,5},{5,4},{6,7},{7,6},{8,9},{9,8},{10,11... | collective-permute-start | bytes 3145736 | tf_op jit(solution)/shard_map/ppermute | solution.py:142
  331.5 60.8 %collective-permute-start.61 = (bf16[256,1024]{1,0:T(8,128)(2,1)S(1)}, bf16[256,1024]{1,0:T(8,128)(2,1)S(1)}, u32[]{:S(2)}, u32[]{:S(2)}) collective-permute-start(bf16[256,1024]{1,0:T(8,128)(2,1)S(1)} %collective-permute-done.59), channel_id=1, source_target_pairs={{0,8},{4,12},{8,16},{12,20},{16,24},{20,28},{24,0},{28,4},{1,9},{5... | collective-permute-start | bytes 1572872 | tf_op jit(solution)/shard_map/ppermute | solution.py:78
  337.9 56.2 %collective-permute-start.60 = (bf16[256,1024]{1,0:T(8,128)(2,1)S(1)}, bf16[256,1024]{1,0:T(8,128)(2,1)S(1)}, u32[]{:S(2)}, u32[]{:S(2)}) collective-permute-start(bf16[256,1024]{1,0:T(8,128)(2,1)S(1)} %collective-permute-done.59), channel_id=1, source_target_pairs={{0,4},{4,0},{8,12},{12,8},{16,20},{20,16},{24,28},{28,24},{1,5},{5... | collective-permute-start | bytes 1572872 | tf_op jit(solution)/shard_map/ppermute | solution.py:73
  344.7 49.5 %collective-permute-start.65 = (bf16[256,1024]{1,0:T(8,128)(2,1)S(1)}, bf16[256,1024]{1,0:T(8,128)(2,1)S(1)}, u32[]{:S(2)}, u32[]{:S(2)}) collective-permute-start(bf16[256,1024]{1,0:T(8,128)(2,1)S(1)} %collective-permute-done.64), channel_id=1, source_target_pairs={{0,4},{4,0},{8,12},{12,8},{16,20},{20,16},{24,28},{28,24},{1,5},{5... | collective-permute-start | bytes 1572872 | tf_op jit(solution)/shard_map/ppermute | solution.py:73
  346.4 49.2 %collective-permute-start.66 = (bf16[256,1024]{1,0:T(8,128)(2,1)S(1)}, bf16[256,1024]{1,0:T(8,128)(2,1)S(1)}, u32[]{:S(2)}, u32[]{:S(2)}) collective-permute-start(bf16[256,1024]{1,0:T(8,128)(2,1)S(1)} %collective-permute-done.64), channel_id=1, source_target_pairs={{0,8},{4,12},{8,16},{12,20},{16,24},{20,28},{24,0},{28,4},{1,9},{5... | collective-permute-start | bytes 1572872 | tf_op jit(solution)/shard_map/ppermute | solution.py:78
  415.7 32.8 %collective-permute-start.140 = (bf16[256,1024]{0,1:T(8,128)(2,1)S(1)}, bf16[256,1024]{0,1:T(8,128)(2,1)S(1)}, u32[]{:S(2)}, u32[]{:S(2)}) collective-permute-start(bf16[256,1024]{0,1:T(8,128)(2,1)S(1)} %get-tuple-element.92), channel_id=1, source_target_pairs={{0,4},{4,0},{8,12},{12,8},{16,20},{20,16},{24,28},{28,24},{1,5},{5... | collective-permute-start | bytes 1572872 | tf_op jit(solution)/shard_map/ppermute | solution.py:73
  415.8 32.9 %collective-permute-start.139 = (bf16[256,1024]{0,1:T(8,128)(2,1)S(1)}, bf16[256,1024]{0,1:T(8,128)(2,1)S(1)}, u32[]{:S(2)}, u32[]{:S(2)}) collective-permute-start(bf16[256,1024]{0,1:T(8,128)(2,1)S(1)} %add_convert_fusion.11), channel_id=1, source_target_pairs={{0,24},{4,28},{8,0},{12,4},{16,8},{20,12},{24,16},{28,20},{1,25},{... | collective-permute-start | bytes 1572872 | tf_op jit(solution)/shard_map/ppermute | solution.py:78
  423.5 60.7 %collective-permute-start.156 = (bf16[1024,256]{1,0:T(8,128)(2,1)S(1)}, bf16[1024,256]{1,0:T(8,128)(2,1)S(1)}, u32[]{:S(2)}, u32[]{:S(2)}) collective-permute-start(bf16[1024,256]{1,0:T(8,128)(2,1)S(1)} %get-tuple-element.83), channel_id=1, source_target_pairs={{0,4},{4,0},{8,12},{12,8},{16,20},{20,16},{24,28},{28,24},{1,5},{5... | collective-permute-start | bytes 1572872 | tf_op jit(solution)/shard_map/ppermute | solution.py:73
  449.0 72.6 %collective-permute-start.158 = (bf16[1024,256]{1,0:T(8,128)(2,1)S(1)}, bf16[1024,256]{1,0:T(8,128)(2,1)S(1)}, u32[]{:S(2)}, u32[]{:S(2)}) collective-permute-start(bf16[1024,256]{1,0:T(8,128)(2,1)S(1)} %get-tuple-element.82), channel_id=1, source_target_pairs={{0,4},{4,0},{8,12},{12,8},{16,20},{20,16},{24,28},{28,24},{1,5},{5... | collective-permute-start | bytes 1572872 | tf_op jit(solution)/shard_map/ppermute | solution.py:73
  499.7 33.6 %collective-permute-start.144 = (bf16[256,1024]{0,1:T(8,128)(2,1)S(1)}, bf16[256,1024]{0,1:T(8,128)(2,1)S(1)}, u32[]{:S(2)}, u32[]{:S(2)}) collective-permute-start(bf16[256,1024]{0,1:T(8,128)(2,1)S(1)} %get-tuple-element.90), channel_id=1, source_target_pairs={{0,4},{4,0},{8,12},{12,8},{16,20},{20,16},{24,28},{28,24},{1,5},{5... | collective-permute-start | bytes 1572872 | tf_op jit(solution)/shard_map/ppermute | solution.py:73
  614.8 58.8 %collective-permute-start.159 = (bf16[1024,256]{1,0:T(8,128)(2,1)}, bf16[1024,256]{1,0:T(8,128)(2,1)}, u32[]{:S(2)}, u32[]{:S(2)}) collective-permute-start(bf16[1024,256]{1,0:T(8,128)(2,1)} %get-tuple-element.85), channel_id=1, source_target_pairs={{0,4},{4,0},{8,12},{12,8},{16,20},{20,16},{24,28},{28,24},{1,5},{5... | collective-permute-start | bytes 1572872 | tf_op jit(solution)/shard_map/ppermute | solution.py:73
  616.3 61.1 %collective-permute-start.145 = (bf16[256,1024]{0,1:T(8,128)(2,1)}, bf16[256,1024]{0,1:T(8,128)(2,1)}, u32[]{:S(2)}, u32[]{:S(2)}) collective-permute-start(bf16[256,1024]{0,1:T(8,128)(2,1)} %get-tuple-element.93), channel_id=1, source_target_pairs={{0,4},{4,0},{8,12},{12,8},{16,20},{20,16},{24,28},{28,24},{1,5},{5... | collective-permute-start | bytes 1572872 | tf_op jit(solution)/shard_map/ppermute | solution.py:73
  625.6 54.2 %collective-permute-start.131 = (bf16[256,1024]{0,1:T(8,128)(2,1)}, bf16[256,1024]{0,1:T(8,128)(2,1)}, u32[]{:S(2)}, u32[]{:S(2)}) collective-permute-start(bf16[256,1024]{0,1:T(8,128)(2,1)} %get-tuple-element.101), channel_id=1, source_target_pairs={{0,4},{4,0},{8,12},{12,8},{16,20},{20,16},{24,28},{28,24},{1,5},{5... | collective-permute-start | bytes 1572872 | tf_op jit(solution)/shard_map/ppermute | solution.py:73
  659.0 40.1 %collective-permute-start.87 = (bf16[128,2048]{1,0:T(8,128)(2,1)S(1)}, bf16[128,2048]{1,0:T(8,128)(2,1)S(1)}, u32[]{:S(2)}, u32[]{:S(2)}) collective-permute-start(bf16[128,2048]{1,0:T(8,128)(2,1)S(1)} %slice.759), channel_id=1, source_target_pairs={{0,1},{1,0},{2,3},{3,2},{4,5},{5,4},{6,7},{7,6},{8,9},{9,8},{10,11... | collective-permute-start | bytes 1572872 | tf_op jit(solution)/shard_map/ppermute | solution.py:142
  698.2 41.3 %collective-permute-start.161 = (bf16[1024,256]{1,0:T(8,128)(2,1)}, bf16[1024,256]{1,0:T(8,128)(2,1)}, u32[]{:S(2)}, u32[]{:S(2)}) collective-permute-start(bf16[1024,256]{1,0:T(8,128)(2,1)} %get-tuple-element.88), channel_id=1, source_target_pairs={{0,4},{4,0},{8,12},{12,8},{16,20},{20,16},{24,28},{28,24},{1,5},{5... | collective-permute-start | bytes 1572872 | tf_op jit(solution)/shard_map/ppermute | solution.py:73
  720.7 41.0 %collective-permute-start.163 = (bf16[1024,256]{1,0:T(8,128)(2,1)}, bf16[1024,256]{1,0:T(8,128)(2,1)S(1)}, u32[]{:S(2)}, u32[]{:S(2)}) collective-permute-start(bf16[1024,256]{1,0:T(8,128)(2,1)} %get-tuple-element.87), channel_id=1, source_target_pairs={{0,4},{4,0},{8,12},{12,8},{16,20},{20,16},{24,28},{28,24},{1,5},{5... | collective-permute-start | bytes 1572872 | tf_op jit(solution)/shard_map/ppermute | solution.py:73
  761.7 41.6 %collective-permute-start.93 = (bf16[256,2048]{1,0:T(8,128)(2,1)S(1)}, bf16[256,2048]{1,0:T(8,128)(2,1)S(1)}, u32[]{:S(2)}, u32[]{:S(2)}) collective-permute-start(bf16[256,2048]{1,0:T(8,128)(2,1)S(1)} %get-tuple-element.69), channel_id=1, source_target_pairs={{0,1},{1,0},{2,3},{3,2},{4,5},{5,4},{6,7},{7,6},{8,9},{9,8},{10,11... | collective-permute-start | bytes 3145736 | tf_op jit(solution)/shard_map/ppermute | solution.py:142
  761.9 42.3 %collective-permute-start.94 = (bf16[256,2048]{1,0:T(8,128)(2,1)S(1)}, bf16[256,2048]{1,0:T(8,128)(2,1)S(1)}, u32[]{:S(2)}, u32[]{:S(2)}) collective-permute-start(bf16[256,2048]{1,0:T(8,128)(2,1)S(1)} %get-tuple-element.69), channel_id=1, source_target_pairs={{0,2},{1,3},{2,0},{3,1},{4,6},{5,7},{6,4},{7,5},{8,10},{9,11},{10,... | collective-permute-start | bytes 3145736 | tf_op jit(solution)/shard_map/ppermute | solution.py:142
  888.1 54.7 %collective-permute-start.121 = (bf16[512,256]{1,0:T(8,128)(2,1)S(1)}, bf16[512,256]{1,0:T(8,128)(2,1)S(1)}, u32[]{:S(2)}, u32[]{:S(2)}) collective-permute-start(bf16[512,256]{1,0:T(8,128)(2,1)S(1)} %get-tuple-element.123), channel_id=1, source_target_pairs={{0,4},{4,0},{8,12},{12,8},{16,20},{20,16},{24,28},{28,24},{1,5},{5... | collective-permute-start | bytes 786440 | tf_op jit(solution)/shard_map/ppermute | solution.py:73
  919.2 32.3 %collective-permute-start.105 = (bf16[256,768]{0,1:T(8,128)(2,1)S(1)}, bf16[256,768]{0,1:T(8,128)(2,1)S(1)}, u32[]{:S(2)}, u32[]{:S(2)}) collective-permute-start(bf16[256,768]{0,1:T(8,128)(2,1)S(1)} %get-tuple-element.112), channel_id=1, source_target_pairs={{0,4},{4,0},{8,12},{12,8},{16,20},{20,16},{24,28},{28,24},{1,5},{5... | collective-permute-start | bytes 1179656 | tf_op jit(solution)/shard_map/ppermute | solution.py:73
  919.5 33.2 %collective-permute-start.112 = (bf16[256,768]{0,1:T(8,128)(2,1)S(1)}, bf16[256,768]{0,1:T(8,128)(2,1)S(1)}, u32[]{:S(2)}, u32[]{:S(2)}) collective-permute-start(bf16[256,768]{0,1:T(8,128)(2,1)S(1)} %get-tuple-element.116), channel_id=1, source_target_pairs={{0,4},{4,0},{8,12},{12,8},{16,20},{20,16},{24,28},{28,24},{1,5},{5... | collective-permute-start | bytes 1179656 | tf_op jit(solution)/shard_map/ppermute | solution.py:73
  (236 other events, 4051.6 us)

commit v2 on v1

v2 whole, which is shorter than its diff:
```python
import math

import jax
import jax.numpy as jnp
from jax import lax
from jax.experimental import pallas as pl
from jax.experimental.pallas import tpu as pltpu
from jax.sharding import PartitionSpec as P

HD = 128
EPSILON = 1e-05
ROPE_BASE = 10000.0
MASKED = -1e30
F32 = jnp.float32
BF16 = jnp.bfloat16


def norm_forward(rows):
    centre = jnp.mean(rows, axis=-1, keepdims=True)
    centered = rows - centre
    spread = jnp.mean(centered * centered, axis=-1, keepdims=True)
    inverse = lax.rsqrt(spread + EPSILON)
    return centered * inverse, inverse


def norm_backward(normed, inverse, grad):
    mean_grad = jnp.mean(grad, axis=-1, keepdims=True)
    mean_both = jnp.mean(grad * normed, axis=-1, keepdims=True)
    return (grad - mean_grad - normed * mean_both) * inverse


def slot_layout(lengths_row, row_total):
    ends = jnp.cumsum(lengths_row)
    places = jnp.arange(row_total, dtype=jnp.int32)
    segment = jnp.sum((places[:, None] >= ends[None, :]).astype(jnp.int32), axis=1)
    starts = jnp.concatenate([jnp.zeros((1,), jnp.int32), ends])
    picks = jnp.arange(starts.shape[0], dtype=jnp.int32)
    begins = jnp.sum(jnp.where(segment[:, None] == picks[None, :], starts[None, :], 0), axis=1)
    valid = (places < ends[-1]).astype(jnp.int32)
    return segment, places - begins, valid


def rope_wide(position):
    half = HD // 2
    steps = jnp.arange(half, dtype=F32)
    freqs = jnp.exp(steps * (-2.0 * math.log(ROPE_BASE) / HD))
    angles = position.astype(F32)[:, None] * freqs[None, :]
    cosine, sine = jnp.cos(angles), jnp.sin(angles)
    return (
        jnp.concatenate([cosine, cosine], axis=1),
        jnp.concatenate([-sine, sine], axis=1),
    )


def dot_plain(left, right):
    return jnp.dot(left, right, preferred_element_type=F32)


def dot_first(left, right):
    return lax.dot_general(left, right, (((0,), (0,)), ((), ())), preferred_element_type=F32)


def dot_last(left, right):
    return lax.dot_general(left, right, (((1,), (1,)), ((), ())), preferred_element_type=F32)


def after(value, *deps):
    return lax.optimization_barrier((value,) + deps)[0]


def gather_dp(own, axis):
    return lax.all_gather(own, "dp", axis=axis, tiled=True)


def scatter_dp(grad, axis):
    total = lax.psum_scatter(grad.astype(BF16), "dp", scatter_dimension=axis, tiled=True)
    return total.astype(F32)


def flip(value, bits):
    return lax.ppermute(value, "tensor", [(k, k ^ bits) for k in range(lax.axis_size("tensor"))])


def join_kernel(*refs):
    out = refs[-1]
    start = 0
    for ref in refs[:-1]:
        out[start : start + ref.shape[0], :] = ref[...]
        start += ref.shape[0]


def join(pieces):
    rows = sum(piece.shape[0] for piece in pieces)
    width = pieces[0].shape[1]
    tile = min(width, 512)
    return pl.pallas_call(
        join_kernel,
        out_shape=jax.ShapeDtypeStruct((rows, width), pieces[0].dtype),
        grid=(width // tile,),
        in_specs=[pl.BlockSpec((piece.shape[0], tile), lambda n: (0, n)) for piece in pieces],
        out_specs=pl.BlockSpec((rows, tile), lambda n: (0, n)),
        cost_estimate=pl.CostEstimate(flops=0, bytes_accessed=4 * rows * width, transcendentals=0),
    )(*pieces)


def gather_rows(own):
    return gather_steps(own)[0]


def gather_steps(own):
    group = lax.axis_size("tensor")
    if group != 4:
        bits = 1
        while bits < group:
            own = jnp.concatenate([own, flip(own, bits)], axis=0)
            bits *= 2
        return own, own
    half = own.shape[0] // 2
    one = flip(own, 1)
    two = flip(own, 2)
    far_top = flip(one[:half], 2)
    far_low = flip(two[half:], 1)
    return join([own, one, two, far_top, far_low]), one


def scatter_rows(piece):
    group = lax.axis_size("tensor")
    if group != 4:
        parts = [piece(j, None).astype(BF16) for j in range(group)]
        while len(parts) > 1:
            bits = len(parts) // 2
            parts = [
                parts[j].astype(F32) + flip(parts[j + bits].astype(BF16), bits).astype(F32)
                for j in range(bits)
            ]
        return parts[0]
    far = piece(3, None).astype(BF16)
    half = far.shape[0] // 2
    top = flip(far[:half], 1)
    low = flip(far[half:], 2)
    one = piece(1, far).astype(BF16)
    one_top = flip(one[:half], 1)
    two = piece(2, one).astype(BF16)
    two_low = flip(two[half:], 2)
    one_low = flip((one[half:].astype(F32) + low.astype(F32)).astype(BF16), 1)
    two_top = flip((two[:half].astype(F32) + top.astype(F32)).astype(BF16), 2)
    own = piece(0, two)
    ones = jnp.concatenate([one_top, one_low], axis=0).astype(F32)
    twos = jnp.concatenate([two_top, two_low], axis=0).astype(F32)
    return own + ones + twos


def feed_kernel(h_ref, g_ref, gate_ref, up_ref, down_ref, hidden_ref, d_ref):
    tile = gate_ref.shape[1]
    lo = pl.program_id(0) * tile
    gate = jnp.dot(h_ref[...], gate_ref[...], preferred_element_type=F32)
    up = jnp.dot(h_ref[...], up_ref[...], preferred_element_type=F32)
    d_hidden = jnp.dot(g_ref[...], down_ref[...], preferred_element_type=F32)
    sg = jax.nn.sigmoid(gate)
    act = gate * sg
    hidden_ref[...] = (act * up).astype(BF16)
    d_gate = d_hidden * up * (sg + act * (1.0 - sg))
    d_ref[:, pl.ds(pl.multiple_of(lo, tile), tile)] = d_gate.astype(BF16)
    d_ref[:, pl.ds(pl.multiple_of(lo + d_ref.shape[1] // 2, tile), tile)] = (d_hidden * act).astype(BF16)


def feed(h2, g_rows, wide):
    rows, depth = h2.shape
    width = wide.shape[1] // 3
    tile = 256
    tiles = width // tile
    return pl.pallas_call(
        feed_kernel,
        out_shape=[
            jax.ShapeDtypeStruct((rows, width), BF16),
            jax.ShapeDtypeStruct((rows, 2 * width), BF16),
        ],
        grid=(tiles,),
        in_specs=[
            pl.BlockSpec((rows, depth), lambda n: (0, 0)),
            pl.BlockSpec((rows, depth), lambda n: (0, 0)),
            pl.BlockSpec((depth, tile), lambda n: (0, n)),
            pl.BlockSpec((depth, tile), lambda n: (0, tiles + n)),
            pl.BlockSpec((depth, tile), lambda n: (0, 2 * tiles + n)),
        ],
        out_specs=[
            pl.BlockSpec((rows, tile), lambda n: (0, n)),
            pl.BlockSpec((rows, 2 * width), lambda n: (0, 0)),
        ],
        cost_estimate=pl.CostEstimate(
            flops=6 * rows * depth * width,
            bytes_accessed=4 * rows * depth + 6 * depth * width + 6 * rows * width,
            transcendentals=rows * width,
        ),
    )(h2, g_rows, wide, wide, wide)


def scores_of(q, k, seg_q, seg_k, row_base):
    s = lax.dot_general(q, k, (((1,), (1,)), ((), ())), preferred_element_type=F32) * (HD**-0.5)
    rows = lax.broadcasted_iota(jnp.int32, s.shape, 0) + row_base
    cols = lax.broadcasted_iota(jnp.int32, s.shape, 1)
    return jnp.where((seg_q == seg_k) & (rows >= cols), s, MASKED)


def softmax_of(s):
    peak = jnp.max(s, axis=-1, keepdims=True)
    e = jnp.exp(s - peak)
    return e * (1.0 / jnp.sum(e, axis=-1, keepdims=True))


def turn(values, cos, sin):
    return values * cos + pltpu.roll(values, HD // 2, 1) * sin


def attend_kernel(
    blocks, t_ref, q_ref, k_ref, v_ref, segc_ref, segr_ref, cos_ref, sin_ref,
    out_ref, saved_ref, kt, vt,
):
    size = q_ref.shape[0] // blocks
    width = saved_ref.shape[1] // 3
    head = pl.program_id(0) * HD
    t = t_ref[0]

    def rows(block):
        return pl.ds(pl.multiple_of((block ^ t) * size, size), size)

    def lanes(which):
        return pl.ds(pl.multiple_of(which * width + head, HD), HD)

    for b in range(blocks):
        lo, hi = b * size, (b + 1) * size
        cos, sin = cos_ref[lo:hi, :], sin_ref[lo:hi, :]
        q = turn(q_ref[rows(b), :], cos, sin).astype(BF16)
        k = turn(k_ref[rows(b), :], cos, sin).astype(BF16)
        v = v_ref[rows(b), :].astype(BF16)
        saved_ref[rows(b), lanes(0)] = q
        saved_ref[rows(b), lanes(1)] = k
        saved_ref[rows(b), lanes(2)] = v
        kt[lo:hi, :] = k
        vt[lo:hi, :] = v
        s = scores_of(q, kt[:hi, :], segc_ref[lo:hi, :], segr_ref[:, :hi], lo)
        p = softmax_of(s).astype(BF16)
        out_ref[rows(b), :] = jnp.dot(p, vt[:hi, :], preferred_element_type=F32).astype(BF16)


def attend_forward(t, pre, segc, segr, cos, sin):
    rows, width = pre.shape[0], pre.shape[1] // 3
    heads = width // HD
    blocks = lax.axis_size("tensor")
    table = pl.BlockSpec((rows, HD), lambda h, t: (0, 0))

    def kernel(*refs):
        attend_kernel(blocks, *refs)

    return pl.pallas_call(
        kernel,
        out_shape=[
            jax.ShapeDtypeStruct((rows, width), BF16),
            jax.ShapeDtypeStruct((rows, 3 * width), BF16),
        ],
        grid_spec=pltpu.PrefetchScalarGridSpec(
            num_scalar_prefetch=1,
            grid=(heads,),
            in_specs=[
                pl.BlockSpec((rows, HD), lambda h, t: (0, h)),
                pl.BlockSpec((rows, HD), lambda h, t: (0, heads + h)),
                pl.BlockSpec((rows, HD), lambda h, t: (0, 2 * heads + h)),
                pl.BlockSpec((rows, 1), lambda h, t: (0, 0)),
                pl.BlockSpec((1, rows), lambda h, t: (0, 0)),
                table,
                table,
            ],
            out_specs=[
                pl.BlockSpec((rows, HD), lambda h, t: (0, h)),
                pl.BlockSpec((rows, 3 * width), lambda h, t: (0, 0)),
            ],
            scratch_shapes=[pltpu.VMEM((rows, HD), BF16)] * 2,
        ),
        cost_estimate=pl.CostEstimate(
            flops=4 * rows * rows * width,
            bytes_accessed=20 * rows * width,
            transcendentals=rows * rows * heads,
        ),
    )(t, pre, pre, pre, segc, segr, cos, sin)


def unattend_kernel(
    blocks, t_ref, q_ref, k_ref, v_ref, g_ref, segc_ref, segr_ref, cos_ref, sin_ref,
    out_ref, kt, vt, dka, dva,
):
    size = q_ref.shape[0] // blocks
    width = out_ref.shape[1] // 3
    head = pl.program_id(0) * HD
    t = t_ref[0]

    def rows(block):
        return pl.ds(pl.multiple_of((block ^ t) * size, size), size)

    def lanes(which):
        return pl.ds(pl.multiple_of(which * width + head, HD), HD)

    def turn_back(grad, b):
        lo, hi = b * size, (b + 1) * size
        return grad * cos_ref[lo:hi, :] - pltpu.roll(grad, HD // 2, 1) * sin_ref[lo:hi, :]

    for b in range(blocks):
        kt[b * size : (b + 1) * size, :] = k_ref[rows(b), :]
        vt[b * size : (b + 1) * size, :] = v_ref[rows(b), :]
    for b in range(blocks - 1, -1, -1):
        n = (b + 1) * size
        q = q_ref[rows(b), :]
        g = g_ref[rows(b), :]
        s = scores_of(q, kt[:n, :], segc_ref[b * size : n, :], segr_ref[:, :n], b * size)
        p = softmax_of(s)
        dp = lax.dot_general(g, vt[:n, :], (((1,), (1,)), ((), ())), preferred_element_type=F32)
        pdp = p * dp
        delta = jnp.sum(pdp, axis=-1, keepdims=True)
        raw = ((pdp - p * delta) * (HD**-0.5)).astype(BF16)
        dq = jnp.dot(raw, kt[:n, :], preferred_element_type=F32)
        out_ref[rows(b), lanes(0)] = turn_back(dq, b).astype(BF16)
        dk = lax.dot_general(raw, q, (((0,), (0,)), ((), ())), preferred_element_type=F32)
        dv = lax.dot_general(
            p.astype(BF16), g, (((0,), (0,)), ((), ())), preferred_element_type=F32
        )
        if b == blocks - 1:
            dka[...] = dk
            dva[...] = dv
        else:
            dka[:n, :] += dk
            dva[:n, :] += dv
    for b in range(blocks):
        lo, hi = b * size, (b + 1) * size
        out_ref[rows(b), lanes(1)] = turn_back(dka[lo:hi, :], b).astype(BF16)
        out_ref[rows(b), lanes(2)] = dva[lo:hi, :].astype(BF16)


def attend_backward(t, saved, g, segc, segr, cos, sin):
    rows, width = g.shape
    heads = width // HD
    blocks = lax.axis_size("tensor")
    table = pl.BlockSpec((rows, HD), lambda h, t: (0, 0))

    def kernel(*refs):
        unattend_kernel(blocks, *refs)

    return pl.pallas_call(
        kernel,
        out_shape=jax.ShapeDtypeStruct((rows, 3 * width), BF16),
        grid_spec=pltpu.PrefetchScalarGridSpec(
            num_scalar_prefetch=1,
            grid=(heads,),
            in_specs=[
                pl.BlockSpec((rows, HD), lambda h, t: (0, h)),
                pl.BlockSpec((rows, HD), lambda h, t: (0, heads + h)),
                pl.BlockSpec((rows, HD), lambda h, t: (0, 2 * heads + h)),
                pl.BlockSpec((rows, HD), lambda h, t: (0, h)),
                pl.BlockSpec((rows, 1), lambda h, t: (0, 0)),
                pl.BlockSpec((1, rows), lambda h, t: (0, 0)),
                table,
                table,
            ],
            out_specs=pl.BlockSpec((rows, 3 * width), lambda h, t: (0, 0)),
            scratch_shapes=[pltpu.VMEM((rows, HD), BF16)] * 2 + [pltpu.VMEM((rows, HD), F32)] * 2,
        ),
        cost_estimate=pl.CostEstimate(
            flops=10 * rows * rows * width,
            bytes_accessed=14 * rows * width,
            transcendentals=rows * rows * heads,
        ),
    )(t, saved, saved, saved, g, segc, segr, cos, sin)


def per_device(
    tokens,
    lengths,
    query_weight,
    key_weight,
    value_weight,
    output_weight,
    gate_weight,
    up_weight,
    down_weight,
    cotangent,
):
    local = tokens.shape[0]
    group = lax.axis_size("tensor")
    t = lax.axis_index("tensor")
    slot_rows = local * group
    heads_width = query_weight.shape[1]
    hidden_width = gate_weight.shape[1]
    t_arg = t.astype(jnp.int32).reshape(1)

    half = hidden_width // 2

    mixed = gather_dp(
        jnp.concatenate([query_weight, key_weight, value_weight, output_weight.T], axis=1), 0
    )
    heads_full, out_full = mixed[:, : 3 * heads_width], mixed[:, 3 * heads_width :]
    wide = [
        gather_dp(
            jnp.concatenate(
                [w[:, a * half : (a + 1) * half] for w in (gate_weight, up_weight)]
                + [down_weight[a * half : (a + 1) * half].T],
                axis=1,
            ),
            0,
        )
        for a in range(2)
    ]

    segment, position, valid_all = slot_layout(lengths[0], slot_rows)
    valid = lax.dynamic_slice_in_dim(valid_all, t * local, local, 0).astype(F32)[:, None]
    cos, sin = rope_wide(position)
    segc, segr = segment[:, None], segment[None, :]

    residual = tokens.astype(F32)
    grad_out = cotangent.astype(F32) * valid
    normed_one, inverse_one = norm_forward(residual)
    h1 = gather_rows(normed_one.astype(BF16))
    g_rows = gather_rows(after(grad_out.astype(BF16), h1))

    def rows_of(value, j):
        return value[j * local : (j + 1) * local]

    context, saved = attend_forward(t_arg, dot_plain(h1, heads_full), segc, segr, cos, sin)

    def attention_piece(j, earlier):
        rows = rows_of(context, j)
        return dot_last(rows if earlier is None else after(rows, earlier), out_full)

    middle = residual + scatter_rows(attention_piece)
    normed_two, inverse_two = norm_forward(middle)
    h2 = gather_rows(normed_two.astype(BF16))

    hidden_0, d_wide_0 = feed(h2, g_rows, wide[0])
    first_grad = jnp.concatenate(
        [dot_first(h2, d_wide_0).astype(BF16), dot_first(g_rows, hidden_0).astype(BF16)], axis=1
    )
    first_sum = scatter_dp(first_grad, 0)
    d_first = dot_last(d_wide_0, wide[0][:, : 2 * half])
    wide_1, first_grad, d_first = lax.optimization_barrier((wide[1], first_grad, d_first))
    hidden_1, d_wide_1 = feed(h2, g_rows, wide_1)

    def feed_back_piece(j, earlier):
        rows = rows_of(d_wide_1, j)
        rows = rows if earlier is None else after(rows, earlier)
        return rows_of(d_first, j) + dot_last(rows, wide_1[:, : 2 * half])

    d_normed_two = scatter_rows(feed_back_piece)
    d_middle = grad_out + norm_backward(normed_two, inverse_two, d_normed_two)
    second_grad = jnp.concatenate(
        [dot_first(h2, d_wide_1).astype(BF16), dot_first(g_rows, hidden_1).astype(BF16)], axis=1
    )
    d_attention = gather_rows(d_middle.astype(BF16))
    d_context = dot_plain(d_attention, out_full).astype(BF16)
    second_sum = scatter_dp(after(second_grad, first_sum, d_context), 0)

    def feed_piece(j, earlier):
        rows = after(rows_of(hidden_0, j), d_attention if earlier is None else earlier)
        return dot_last(rows, wide[0][:, 2 * half :]) + dot_last(
            rows_of(hidden_1, j), wide_1[:, 2 * half :]
        )

    feed_out = scatter_rows(feed_piece)

    d_pre = attend_backward(t_arg, saved, d_context, segc, segr, cos, sin)
    d_pre = after(d_pre, feed_out)
    output = (valid * (middle + feed_out)).astype(BF16)
    mixed_grad = jnp.concatenate(
        [dot_first(h1, d_pre).astype(BF16), dot_first(d_attention, context).astype(BF16)], axis=1
    )
    mixed_sum = scatter_dp(after(mixed_grad, second_sum), 0)

    def heads_back_piece(j, earlier):
        rows = rows_of(d_pre, j)
        return dot_last(rows if earlier is None else after(rows, earlier), heads_full)

    d_normed_one = scatter_rows(heads_back_piece)
    input_grad = (d_middle + norm_backward(normed_one, inverse_one, d_normed_one)).astype(BF16)
    wide_sum = [first_sum, second_sum]

    return (
        output,
        input_grad,
        mixed_sum[:, :heads_width],
        mixed_sum[:, heads_width : 2 * heads_width],
        mixed_sum[:, 2 * heads_width : 3 * heads_width],
        mixed_sum[:, 3 * heads_width :].T,
        jnp.concatenate([part[:, :half] for part in wide_sum], axis=1),
        jnp.concatenate([part[:, half : 2 * half] for part in wide_sum], axis=1),
        jnp.concatenate([part[:, 2 * half :].T for part in wide_sum], axis=0),
    )


def solution(mesh):
    return jax.shard_map(
        per_device,
        mesh=mesh,
        in_specs=(
            P(("dp", "tensor"), None),
            P("dp", None),
            P("dp", "tensor"),
            P("dp", "tensor"),
            P("dp", "tensor"),
            P("tensor", "dp"),
            P("dp", "tensor"),
            P("dp", "tensor"),
            P("tensor", "dp"),
            P(("dp", "tensor"), None),
        ),
        out_specs=(
            P(("dp", "tensor"), None),
            P(("dp", "tensor"), None),
            P("dp", "tensor"),
            P("dp", "tensor"),
            P("dp", "tensor"),
            P("tensor", "dp"),
            P("dp", "tensor"),
            P("dp", "tensor"),
            P("tensor", "dp"),
        ),
        check_vma=False,
    )
```

time: 1020 us -> 712 us (0.70)
  waiting for transfers between devices: 412 us -> 285 us
  local copies, waits for them, and re-layouts: 146 us -> 42 us
  starting transfers between devices: 146 us -> 48.4 us
  Pallas kernels: 34.4 us -> 95.6 us
  matrix products: 210 us -> 157 us
  between operations: 3.73 us -> 15.5 us
    ppermute x126 -> x0, waiting for transfers between devices: 304 us -> none  [the longest x54 304 us: ring_shift(): lax.ppermute(value, 'dp', [(k, (k + 2 * step) % count) for k in range(cou...]
    ppermute x126 -> x0, starting transfers between devices: 106 us -> none  [the longest x54 92.7 us: ring_shift(): lax.ppermute(value, 'dp', [(k, (k + 2 * step) % count) for k in range(cou...]
    reduce_scatter x0 -> x3, waiting for transfers between devices: none -> 70.5 us  [scatter_dp(): lax.psum_scatter(grad.astype(BF16), 'dp', scatter_dimension=axis, tiled=T...]
    unnamed x314 -> x100, local copies, waits for them, and re-layouts: 85.3 us -> 17.3 us
    dot_general x18 -> x2, matrix products: 79.8 us -> 18.1 us  [dot_plain(): return jnp.dot(left, right, preferred_element_type=F32)]
    pallas_call x4 -> x8, Pallas kernels: 34.4 us -> 95.6 us  [the longest x2 42.9 us: feed(): pl.pallas_call(feed_kernel, out_shape=[jax.ShapeDtypeStruct((rows, width)...]
    ppermute x40, waiting for transfers between devices: 108 us -> 161 us  [flip(): lax.ppermute(value, 'tensor', [(k, k ^ bits) for k in range(lax.axis_size...]
    all_gather x0 -> x3, waiting for transfers between devices: none -> 52.7 us  [gather_dp(): return lax.all_gather(own, 'dp', axis=axis, tiled=True)]
  transfers between devices with their start and end apart: 166 -> 46, of which waited for: 57 -> 24; matrix products, arithmetic and copies ran while one was open for 30% -> 34% of each run, Pallas kernels for 2% -> 14%
where the time goes in v2:
time: 712 us; the launch traced here: 706 us
  waiting for transfers between devices  285 us (40%)
  matrix products  157 us (22%)
  Pallas kernels  95.6 us (13%)
  other arithmetic  63.5 us (9%)
  starting transfers between devices  48.4 us (7%)
  local copies, waits for them, and re-layouts  42 us (6%)
  between operations  15.5 us (2%)
    ppermute x40, waiting for transfers between devices, flip(): lax.ppermute(value, 'tensor', [(k, k ^ bits) for k in range(lax.axis_size...  161 us
    dot_general x21, matrix products, dot_last(): lax.dot_general(left, right, (((1,), (1,)), ((), ())), preferred_element_...  91.6 us
    reduce_scatter x3, waiting for transfers between devices, scatter_dp(): lax.psum_scatter(grad.astype(BF16), 'dp', scatter_dimension=axis, tiled=T...  70.5 us
    all_gather x3, waiting for transfers between devices, gather_dp(): return lax.all_gather(own, 'dp', axis=axis, tiled=True)  52.7 us
    ppermute x40, starting transfers between devices, flip(): lax.ppermute(value, 'tensor', [(k, k ^ bits) for k in range(lax.axis_size...  48 us
    dot_general x6, matrix products, dot_first(): lax.dot_general(left, right, (((0,), (0,)), ((), ())), preferred_element_...  46.8 us
    pallas_call x2, Pallas kernels, feed(): pl.pallas_call(feed_kernel, out_shape=[jax.ShapeDtypeStruct((rows, width)...  42.9 us
    pallas_call x4, Pallas kernels, join(): pl.pallas_call(join_kernel, out_shape=jax.ShapeDtypeStruct((rows, width),...  19.4 us
  transfers between devices with their start and end apart: 46, of which 24 were waited for; matrix products, arithmetic and copies ran while one was open for 34% of the time, Pallas kernels for 14%

profile of v2, /device:TPU:0, one launch (start us, length us, event | category | flops | bytes accessed | tf_op | source)
XLA Modules:
  0.0 706.2 jit_solution(11893120804650442361)
XLA Ops:
  24.6 21.2 %collective-permute-done.refs_1_ = bf16[256,2048]{1,0:T(8,128)(2,1)S(1)} collective-permute-done((bf16[256,2048]{1,0:T(8,128)(2,1)S(1)}, bf16[256,2048]{1,0:T(8,128)(2,1)S(1)}, u32[]{:S(2)}, u32[]{:S(2)}) %collective-permute-start) | collective-permute-done | bytes 1048608 | tf_op jit(solution)/shard_map/ppermute | solution.py:81
  68.3 29.7 %all-gather.4.cloned.1.call-done = bf16[2048,2048]{0,1:T(8,128)(2,1)} async-done(((bf16[256,2048]{0,1:T(8,128)(2,1)}), bf16[2048,2048]{0,1:T(8,128)(2,1)}) %all-gather.4.cloned.1.call-update) | async-done | bytes 8388624 | tf_op jit(solution)/shard_map/all_gather | solution.py:72
  98.0 11.9 %fusion.18.refs_1_.refs_2_.refs_3_ = f32[1024,1536]{1,0:T(8,128)} fusion(bf16[1024,2048]{1,0:T(8,128)(2,1)} %shard_map.169, bf16[2048,2048]{0,1:T(8,128)(2,1)} %all-gather.4.cloned.1.call-done), kind=kOutput, calls=%fused_computation.26 | convolution fusion | flops 6442450944 | bytes 16777216 | tf_op jit(solution)/shard_map/dot_general | solution.py:56
  110.0 14.6 %shard_map.170 = (bf16[1024,512]{1,0:T(8,128)(2,1)}, bf16[1024,1536]{1,0:T(8,128)(2,1)}) custom-call(s32[1]{0:T(128)} %bitcast.2.refs_0_, f32[1024,1536]{1,0:T(8,128)} %fusion.18.refs_1_.refs_2_.refs_3_, f32[1024,1536]{1,0:T(8,128)} %fusion.18.refs_1_.refs_2_.refs_3_, f32[1024,1536]{1,0:T(8,128)} %fusion.18.refs_1_.refs_2_.refs_3_, ...), custom_call_target="tpu_custom_call" | custom-call | flops 2147483648 | bytes 10485760 | tf_op jit(solution)/shard_map/pallas_call | solution.py:255
  135.8 7.4 %collective-permute-done.7 = bf16[128,2048]{1,0:T(8,128)(2,1)S(1)} collective-permute-done((bf16[128,2048]{1,0:T(8,128)(2,1)S(1)}, bf16[128,2048]{1,0:T(8,128)(2,1)S(1)}, u32[]{:S(2)}, u32[]{:S(2)}) %collective-permute-start.7) | collective-permute-done | bytes 524320 | tf_op jit(solution)/shard_map/ppermute | solution.py:81
  149.7 8.6 %collective-permute-done.9 = bf16[128,2048]{1,0:T(8,128)(2,1)S(1)} collective-permute-done((bf16[128,2048]{1,0:T(8,128)(2,1)S(1)}, bf16[128,2048]{1,0:T(8,128)(2,1)S(1)}, u32[]{:S(2)}, u32[]{:S(2)}) %collective-permute-start.9) | collective-permute-done | bytes 524320 | tf_op jit(solution)/shard_map/ppermute | solution.py:81
  159.8 9.8 %collective-permute-done.8 = bf16[128,2048]{1,0:T(8,128)(2,1)S(1)} collective-permute-done((bf16[128,2048]{1,0:T(8,128)(2,1)S(1)}, bf16[128,2048]{1,0:T(8,128)(2,1)S(1)}, u32[]{:S(2)}, u32[]{:S(2)}) %collective-permute-start.8) | collective-permute-done | bytes 524320 | tf_op jit(solution)/shard_map/ppermute | solution.py:81
  173.7 14.5 %collective-permute-done.14.refs_1_ = bf16[256,2048]{1,0:T(8,128)(2,1)S(1)} collective-permute-done((bf16[256,2048]{1,0:T(8,128)(2,1)S(1)}, bf16[256,2048]{1,0:T(8,128)(2,1)S(1)}, u32[]{:S(2)}, u32[]{:S(2)}) %collective-permute-start.14) | collective-permute-done | bytes 1048608 | tf_op jit(solution)/shard_map/ppermute | solution.py:81
  192.8 17.9 %collective-permute-done.10.refs_1_ = bf16[256,2048]{1,0:T(8,128)(2,1)S(1)} collective-permute-done((bf16[256,2048]{1,0:T(8,128)(2,1)S(1)}, bf16[256,2048]{1,0:T(8,128)(2,1)S(1)}, u32[]{:S(2)}, u32[]{:S(2)}) %collective-permute-start.10) | collective-permute-done | bytes 1048608 | tf_op jit(solution)/shard_map/ppermute | solution.py:81
  216.0 9.7 %collective-permute-done.16.refs_3_ = bf16[128,2048]{1,0:T(8,128)(2,1)S(1)} collective-permute-done((bf16[128,2048]{1,0:T(8,128)(2,1)S(1)}, bf16[128,2048]{1,0:T(8,128)(2,1)S(1)}, u32[]{:S(2)}, u32[]{:S(2)}) %collective-permute-start.16) | collective-permute-done | bytes 524320 | tf_op jit(solution)/shard_map/ppermute | solution.py:81
  240.9 21.7 %shard_map.173 = (bf16[1024,1024]{1,0:T(8,128)(2,1)}, bf16[1024,2048]{1,0:T(8,128)(2,1)}) custom-call(bf16[1024,2048]{1,0:T(8,128)(2,1)} %shard_map.171.h_ref, bf16[1024,2048]{1,0:T(8,128)(2,1)} %shard_map.172.g_ref, bf16[2048,3072]{1,0:T(8,128)(2,1)} %all-gather.6.cloned.1.call-done.gate_ref.up_ref.down_ref, ...), custom_call_target="tpu_custom_call" | custom-call | flops 12884901888 | bytes 27262976 | tf_op jit(solution)/shard_map/pallas_call | solution.py:172
  262.6 7.7 %convolution_convert_fusion.4 = bf16[2048,1024]{0,1:T(8,128)(2,1)S(1)} fusion(bf16[1024,2048]{1,0:T(8,128)(2,1)} %shard_map.172.g_ref, bf16[1024,1024]{1,0:T(8,128)(2,1)} %get-tuple-element.39), kind=kOutput, calls=%fused_computation.17 | convolution fusion | flops 4297064448 | bytes 10485760 | tf_op jit(solution)/shard_map/dot_general | solution.py:60
  270.3 9.7 %convolution_convert_fusion.2 = bf16[2048,2048]{0,1:T(8,128)(2,1)S(1)} fusion(bf16[1024,2048]{1,0:T(8,128)(2,1)S(1)} %copy-done.10, bf16[1024,2048]{1,0:T(8,128)(2,1)S(1)} %copy-done.39), kind=kOutput, calls=%fused_computation.7 | convolution fusion | flops 8594128896 | bytes 16777216 | tf_op jit(solution)/shard_map/dot_general | solution.py:60
  280.0 14.4 %pad_maximum_fusion = bf16[2048,3072]{0,1:T(8,128)(2,1)} fusion(bf16[2048,1024]{0,1:T(8,128)(2,1)S(1)} %convolution_convert_fusion.4, bf16[2048,2048]{0,1:T(8,128)(2,1)S(1)} %convolution_convert_fusion.2), kind=kLoop, calls=%fused_computation | loop fusion | flops 25165824 | bytes 25165824 | tf_op jit(solution)/shard_map/concatenate | solution.py:436
  294.5 14.8 %fusion = f32[1024,2048]{1,0:T(8,128)} fusion(bf16[1024,2048]{1,0:T(8,128)(2,1)} %get-tuple-element.40, bf16[2048,3072]{1,0:T(8,128)(2,1)} %all-gather.6.cloned.1.call-done.gate_ref.up_ref.down_ref), kind=kOutput, calls=%fused_computation.2 | convolution fusion | flops 8589934592 | bytes 20971520 | tf_op jit(solution)/shard_map/dot_general | solution.py:64
  309.3 23.0 %all-gather.8.cloned.1.call-done.gate_ref.up_ref.down_ref = bf16[2048,3072]{1,0:T(8,128)(2,1)} async-done(((bf16[256,3072]{1,0:T(8,128)(2,1)}), bf16[2048,3072]{1,0:T(8,128)(2,1)}) %all-gather.8.cloned.1.call-update) | async-done | bytes 12582928 | tf_op jit(solution)/shard_map/all_gather | solution.py:72
  332.3 21.2 %shard_map.174 = (bf16[1024,1024]{1,0:T(8,128)(2,1)}, bf16[1024,2048]{1,0:T(8,128)(2,1)}) custom-call(bf16[1024,2048]{1,0:T(8,128)(2,1)} %shard_map.171.h_ref, bf16[1024,2048]{1,0:T(8,128)(2,1)} %shard_map.172.g_ref, bf16[2048,3072]{1,0:T(8,128)(2,1)} %all-gather.8.cloned.1.call-done.gate_ref.up_ref.down_ref, ...), custom_call_target="tpu_custom_call" | custom-call | flops 12884901888 | bytes 27262976 | tf_op jit(solution)/shard_map/pallas_call | solution.py:172
  363.0 6.5 fusion.69
  387.8 9.4 %collective-permute-done.23 = bf16[128,2048]{1,0:T(8,128)(2,1)S(1)} collective-permute-done((bf16[128,2048]{1,0:T(8,128)(2,1)S(1)}, bf16[128,2048]{1,0:T(8,128)(2,1)S(1)}, u32[]{:S(2)}, u32[]{:S(2)}) %collective-permute-start.23) | collective-permute-done | bytes 524320 | tf_op jit(solution)/shard_map/ppermute | solution.py:81
  397.2 10.3 %collective-permute-done.22 = bf16[128,2048]{1,0:T(8,128)(2,1)S(1)} collective-permute-done((bf16[128,2048]{1,0:T(8,128)(2,1)S(1)}, bf16[128,2048]{1,0:T(8,128)(2,1)S(1)}, u32[]{:S(2)}, u32[]{:S(2)}) %collective-permute-start.22) | collective-permute-done | bytes 524320 | tf_op jit(solution)/shard_map/ppermute | solution.py:81
  407.5 7.1 %fusion.121 = (f32[256]{0:T(256)S(1)}, f32[256]{0:T(256)S(1)}, f32[256,2048]{1,0:T(8,128)S(1)}) fusion(bf16[128,2048]{1,0:T(8,128)(2,1)S(1)} %collective-permute-done.23, bf16[128,2048]{1,0:T(8,128)(2,1)S(1)} %collective-permute-done.22, bf16[128,2048]{1,0:T(8,128)(2,1)S(1)} %collective-permute-done.20, bf16[128,2048]{1,0:T(8,128)(2,1)S(1)} %collective-permute-done.18, ...), kind=kOutput, calls=%fused_computation.145 | convolution fusion | flops 2155871744 | bytes 17829888 | tf_op jit(solution)/shard_map/dot_general | solution.py:64
  419.7 10.1 %convolution_convert_fusion = bf16[2048,2048]{0,1:T(8,128)(2,1)S(1)} fusion(bf16[1024,2048]{1,0:T(8,128)(2,1)S(1)} %copy-done.11, bf16[1024,2048]{1,0:T(8,128)(2,1)S(1)} %copy-done.17), kind=kOutput, calls=%fused_computation.5 | convolution fusion | flops 8594128896 | bytes 16777216 | tf_op jit(solution)/shard_map/dot_general | solution.py:60
  446.1 14.5 %pad_maximum_fusion.1 = bf16[2048,3072]{0,1:T(8,128)(2,1)} fusion(bf16[2048,1024]{0,1:T(8,128)(2,1)S(1)} %convolution_convert_fusion.3, bf16[2048,2048]{0,1:T(8,128)(2,1)S(1)} %convolution_convert_fusion), kind=kLoop, calls=%fused_computation.1 | loop fusion | flops 25165824 | bytes 25165824 | tf_op jit(solution)/shard_map/concatenate | solution.py:451
  512.7 18.7 %shard_map.176 = bf16[1024,1536]{1,0:T(8,128)(2,1)} custom-call(s32[1]{0:T(128)} %bitcast.2.refs_0_, bf16[1024,1536]{1,0:T(8,128)(2,1)} %get-tuple-element.52.refs_1_.refs_2_.refs_3_, bf16[1024,1536]{1,0:T(8,128)(2,1)} %get-tuple-element.52.refs_1_.refs_2_.refs_3_, bf16[1024,1536]{1,0:T(8,128)(2,1)} %get-tuple-element.52.refs_1_.refs_2_.refs_3_, ...), custom_call_target="tpu_custom_call" | custom-call | flops 5368709120 | bytes 7340032 | tf_op jit(solution)/shard_map/pallas_call | solution.py:346
  531.4 6.5 multiply_convert_fusion
  537.9 9.2 %convolution_convert_fusion.1 = bf16[2048,1536]{0,1:T(8,128)(2,1)} fusion(bf16[1024,2048]{1,0:T(8,128)(2,1)S(1)} %copy-done.8, bf16[1024,1536]{1,0:T(8,128)(2,1)S(1)} %copy-done.25), kind=kOutput, calls=%fused_computation.6 | convolution fusion | flops 6445596672 | bytes 13631488 | tf_op jit(solution)/shard_map/dot_general | solution.py:60
  547.2 7.8 %pad_maximum_fusion.2 = bf16[2048,2048]{0,1:T(8,128)(2,1)} fusion(bf16[2048,512]{0,1:T(8,128)(2,1)S(1)} %copy-done.24, bf16[2048,1536]{0,1:T(8,128)(2,1)} %convolution_convert_fusion.1), kind=kLoop, calls=%fused_computation.4 | loop fusion | flops 16777216 | bytes 16777216 | tf_op jit(solution)/shard_map/concatenate | solution.py:469
  554.9 47.3 %reduce-scatter.6.cloned.1.call-done = bf16[256,3072]{0,1:T(8,128)(2,1)} async-done(((bf16[2048,3072]{0,1:T(8,128)(2,1)}), bf16[256,3072]{0,1:T(8,128)(2,1)}) %reduce-scatter.6.cloned.1.call-update) | async-done | bytes 1572880 | tf_op jit(solution)/shard_map/reduce_scatter | solution.py:76
  623.9 8.6 %collective-permute-done.37 = bf16[128,2048]{1,0:T(8,128)(2,1)S(1)} collective-permute-done((bf16[128,2048]{1,0:T(8,128)(2,1)S(1)}, bf16[128,2048]{1,0:T(8,128)(2,1)S(1)}, u32[]{:S(2)}, u32[]{:S(2)}) %collective-permute-start.37) | collective-permute-done | bytes 524320 | tf_op jit(solution)/shard_map/ppermute | solution.py:81
  635.5 9.3 %collective-permute-done.39 = bf16[128,2048]{1,0:T(8,128)(2,1)S(1)} collective-permute-done((bf16[128,2048]{1,0:T(8,128)(2,1)S(1)}, bf16[128,2048]{1,0:T(8,128)(2,1)S(1)}, u32[]{:S(2)}, u32[]{:S(2)}) %collective-permute-start.39) | collective-permute-done | bytes 524320 | tf_op jit(solution)/shard_map/ppermute | solution.py:81
  644.8 8.2 %collective-permute-done.38 = bf16[128,2048]{1,0:T(8,128)(2,1)S(1)} collective-permute-done((bf16[128,2048]{1,0:T(8,128)(2,1)S(1)}, bf16[128,2048]{1,0:T(8,128)(2,1)S(1)}, u32[]{:S(2)}, u32[]{:S(2)}) %collective-permute-start.38) | collective-permute-done | bytes 524320 | tf_op jit(solution)/shard_map/ppermute | solution.py:81
  670.4 23.2 %reduce-scatter.8.cloned.1.call-done = bf16[256,2048]{0,1:T(8,128)(2,1)} async-done(((bf16[2048,2048]{0,1:T(8,128)(2,1)}), bf16[256,2048]{0,1:T(8,128)(2,1)}) %reduce-scatter.8.cloned.1.call-update) | async-done | bytes 1048592 | tf_op jit(solution)/shard_map/reduce_scatter | solution.py:76
  (285 shorter events, 236.3 us)
Async XLA Ops:
  7.2 90.8 %all-gather.4.cloned.1.call-start = ((), (), s32[]{:S(2)}) async-start(), calls=%async_computation.3 | async-start | bytes 9437184 | tf_op jit(solution)/shard_map/all_gather | solution.py:72
  12.6 228.3 %all-gather.6.cloned.1.call-start = ((), (), s32[]{:S(2)}) async-start(), calls=%async_computation.4 | async-start | bytes 14155776 | tf_op jit(solution)/shard_map/all_gather | solution.py:72
  15.9 316.3 %all-gather.8.cloned.1.call-start = ((), (), s32[]{:S(2)}) async-start(), calls=%async_computation.5 | async-start | bytes 14155776 | tf_op jit(solution)/shard_map/all_gather | solution.py:72
  17.5 455.0 %reduce-scatter.4.cloned.1.call-start = ((), (), s32[]{:S(2)}) async-start(), calls=%async_computation.6 | async-start | bytes 14155776 | tf_op jit(solution)/shard_map/reduce_scatter | solution.py:76
  19.6 26.2 %collective-permute-start = (bf16[256,2048]{1,0:T(8,128)(2,1)S(1)}, bf16[256,2048]{1,0:T(8,128)(2,1)S(1)}, u32[]{:S(2)}, u32[]{:S(2)}) collective-permute-start(bf16[256,2048]{1,0:T(8,128)(2,1)S(1)} %fusion.97.refs_0_), channel_id=1, source_target_pairs={{0,1},{1,0},{2,3},{3,2},{4,5},{5,4},{6,7},{7,6},{8,9},{9,8},{10,11... | collective-permute-start | bytes 3145736 | tf_op jit(solution)/shard_map/ppermute | solution.py:81
  22.7 25.8 %collective-permute-start.1 = (bf16[256,2048]{1,0:T(8,128)(2,1)S(1)}, bf16[256,2048]{1,0:T(8,128)(2,1)}, u32[]{:S(2)}, u32[]{:S(2)}) collective-permute-start(bf16[256,2048]{1,0:T(8,128)(2,1)S(1)} %fusion.97.refs_0_), channel_id=1, source_target_pairs={{0,2},{1,3},{2,0},{3,1},{4,6},{5,7},{6,4},{7,5},{8,10},{9,11},{10,... | collective-permute-start | bytes 3145736 | tf_op jit(solution)/shard_map/ppermute | solution.py:81
  134.6 23.7 %collective-permute-start.9 = (bf16[128,2048]{1,0:T(8,128)(2,1)S(1)}, bf16[128,2048]{1,0:T(8,128)(2,1)S(1)}, u32[]{:S(2)}, u32[]{:S(2)}) collective-permute-start(bf16[128,2048]{1,0:T(8,128)(2,1)S(1)} %slice.335), channel_id=1, source_target_pairs={{0,2},{1,3},{2,0},{3,1},{4,6},{5,7},{6,4},{7,5},{8,10},{9,11},{10,... | collective-permute-start | bytes 1572872 | tf_op jit(solution)/shard_map/ppermute | solution.py:81
  135.2 24.6 %collective-permute-start.4 = (bf16[128,2048]{1,0:T(8,128)(2,1)S(1)}, bf16[128,2048]{1,0:T(8,128)(2,1)S(1)}, u32[]{:S(2)}, u32[]{:S(2)}) collective-permute-start(bf16[128,2048]{1,0:T(8,128)(2,1)S(1)} %slice.330), channel_id=1, source_target_pairs={{0,1},{1,0},{2,3},{3,2},{4,5},{5,4},{6,7},{7,6},{8,9},{9,8},{10,11... | collective-permute-start | bytes 1572872 | tf_op jit(solution)/shard_map/ppermute | solution.py:81
  143.4 26.2 %collective-permute-start.8 = (bf16[128,2048]{1,0:T(8,128)(2,1)S(1)}, bf16[128,2048]{1,0:T(8,128)(2,1)S(1)}, u32[]{:S(2)}, u32[]{:S(2)}) collective-permute-start(bf16[128,2048]{1,0:T(8,128)(2,1)S(1)} %add_convert_fusion.6), channel_id=1, source_target_pairs={{0,2},{1,3},{2,0},{3,1},{4,6},{5,7},{6,4},{7,5},{8,10},{9,11},{10,... | collective-permute-start | bytes 1572872 | tf_op jit(solution)/shard_map/ppermute | solution.py:81
  147.3 22.3 %collective-permute-start.6 = (bf16[128,2048]{1,0:T(8,128)(2,1)S(1)}, bf16[128,2048]{1,0:T(8,128)(2,1)S(1)}, u32[]{:S(2)}, u32[]{:S(2)}) collective-permute-start(bf16[128,2048]{1,0:T(8,128)(2,1)S(1)} %add_convert_fusion.7), channel_id=1, source_target_pairs={{0,1},{1,0},{2,3},{3,2},{4,5},{5,4},{6,7},{7,6},{8,9},{9,8},{10,11... | collective-permute-start | bytes 1572872 | tf_op jit(solution)/shard_map/ppermute | solution.py:81
  148.2 39.9 %collective-permute-start.14 = (bf16[256,2048]{1,0:T(8,128)(2,1)S(1)}, bf16[256,2048]{1,0:T(8,128)(2,1)S(1)}, u32[]{:S(2)}, u32[]{:S(2)}) collective-permute-start(bf16[256,2048]{1,0:T(8,128)(2,1)S(1)} %fusion.104.refs_0_), channel_id=1, source_target_pairs={{0,1},{1,0},{2,3},{3,2},{4,5},{5,4},{6,7},{7,6},{8,9},{9,8},{10,11... | collective-permute-start | bytes 3145736 | tf_op jit(solution)/shard_map/ppermute | solution.py:81
  158.4 33.7 %collective-permute-start.15 = (bf16[256,2048]{1,0:T(8,128)(2,1)S(1)}, bf16[256,2048]{1,0:T(8,128)(2,1)S(1)}, u32[]{:S(2)}, u32[]{:S(2)}) collective-permute-start(bf16[256,2048]{1,0:T(8,128)(2,1)S(1)} %fusion.104.refs_0_), channel_id=1, source_target_pairs={{0,2},{1,3},{2,0},{3,1},{4,6},{5,7},{6,4},{7,5},{8,10},{9,11},{10,... | collective-permute-start | bytes 3145736 | tf_op jit(solution)/shard_map/ppermute | solution.py:81
  171.6 39.1 %collective-permute-start.10 = (bf16[256,2048]{1,0:T(8,128)(2,1)S(1)}, bf16[256,2048]{1,0:T(8,128)(2,1)S(1)}, u32[]{:S(2)}, u32[]{:S(2)}) collective-permute-start(bf16[256,2048]{1,0:T(8,128)(2,1)S(1)} %fusion.105.refs_0_), channel_id=1, source_target_pairs={{0,1},{1,0},{2,3},{3,2},{4,5},{5,4},{6,7},{7,6},{8,9},{9,8},{10,11... | collective-permute-start | bytes 3145736 | tf_op jit(solution)/shard_map/ppermute | solution.py:81
  172.2 42.3 %collective-permute-start.11 = (bf16[256,2048]{1,0:T(8,128)(2,1)S(1)}, bf16[256,2048]{1,0:T(8,128)(2,1)S(1)}, u32[]{:S(2)}, u32[]{:S(2)}) collective-permute-start(bf16[256,2048]{1,0:T(8,128)(2,1)S(1)} %fusion.105.refs_0_), channel_id=1, source_target_pairs={{0,2},{1,3},{2,0},{3,1},{4,6},{5,7},{6,4},{7,5},{8,10},{9,11},{10,... | collective-permute-start | bytes 3145736 | tf_op jit(solution)/shard_map/ppermute | solution.py:81
  188.2 37.5 %collective-permute-start.16 = (bf16[128,2048]{1,0:T(8,128)(2,1)S(1)}, bf16[128,2048]{1,0:T(8,128)(2,1)S(1)}, u32[]{:S(2)}, u32[]{:S(2)}) collective-permute-start(bf16[128,2048]{1,0:T(8,128)(2,1)S(1)} %slice.338), channel_id=1, source_target_pairs={{0,2},{1,3},{2,0},{3,1},{4,6},{5,7},{6,4},{7,5},{8,10},{9,11},{10,... | collective-permute-start | bytes 1572872 | tf_op jit(solution)/shard_map/ppermute | solution.py:81
  192.1 34.5 %collective-permute-start.17 = (bf16[128,2048]{1,0:T(8,128)(2,1)S(1)}, bf16[128,2048]{1,0:T(8,128)(2,1)}, u32[]{:S(2)}, u32[]{:S(2)}) collective-permute-start(bf16[128,2048]{1,0:T(8,128)(2,1)S(1)} %slice.339), channel_id=1, source_target_pairs={{0,1},{1,0},{2,3},{3,2},{4,5},{5,4},{6,7},{7,6},{8,9},{9,8},{10,11... | collective-permute-start | bytes 1572872 | tf_op jit(solution)/shard_map/ppermute | solution.py:81
  211.6 24.6 %collective-permute-start.12 = (bf16[128,2048]{1,0:T(8,128)(2,1)}, bf16[128,2048]{1,0:T(8,128)(2,1)}, u32[]{:S(2)}, u32[]{:S(2)}) collective-permute-start(bf16[128,2048]{1,0:T(8,128)(2,1)} %slice.336), channel_id=1, source_target_pairs={{0,2},{1,3},{2,0},{3,1},{4,6},{5,7},{6,4},{7,5},{8,10},{9,11},{10,... | collective-permute-start | bytes 1572872 | tf_op jit(solution)/shard_map/ppermute | solution.py:81
  215.4 20.7 %collective-permute-start.13 = (bf16[128,2048]{1,0:T(8,128)(2,1)}, bf16[128,2048]{1,0:T(8,128)(2,1)}, u32[]{:S(2)}, u32[]{:S(2)}) collective-permute-start(bf16[128,2048]{1,0:T(8,128)(2,1)} %slice.337), channel_id=1, source_target_pairs={{0,1},{1,0},{2,3},{3,2},{4,5},{5,4},{6,7},{7,6},{8,9},{9,8},{10,11... | collective-permute-start | bytes 1572872 | tf_op jit(solution)/shard_map/ppermute | solution.py:81
  294.4 307.8 %reduce-scatter.6.cloned.1.call-start = ((), (), s32[]{:S(2)}) async-start(), calls=%async_computation.7 | async-start | bytes 14155776 | tf_op jit(solution)/shard_map/reduce_scatter | solution.py:76
  384.6 22.9 %collective-permute-start.22 = (bf16[128,2048]{1,0:T(8,128)(2,1)S(1)}, bf16[128,2048]{1,0:T(8,128)(2,1)S(1)}, u32[]{:S(2)}, u32[]{:S(2)}) collective-permute-start(bf16[128,2048]{1,0:T(8,128)(2,1)S(1)} %add_convert_fusion.4), channel_id=1, source_target_pairs={{0,2},{1,3},{2,0},{3,1},{4,6},{5,7},{6,4},{7,5},{8,10},{9,11},{10,... | collective-permute-start | bytes 1572872 | tf_op jit(solution)/shard_map/ppermute | solution.py:81
  386.3 21.2 %collective-permute-start.20 = (bf16[128,2048]{1,0:T(8,128)(2,1)S(1)}, bf16[128,2048]{1,0:T(8,128)(2,1)S(1)}, u32[]{:S(2)}, u32[]{:S(2)}) collective-permute-start(bf16[128,2048]{1,0:T(8,128)(2,1)S(1)} %add_convert_fusion.5), channel_id=1, source_target_pairs={{0,1},{1,0},{2,3},{3,2},{4,5},{5,4},{6,7},{7,6},{8,9},{9,8},{10,11... | collective-permute-start | bytes 1572872 | tf_op jit(solution)/shard_map/ppermute | solution.py:81
  417.6 24.3 %collective-permute-start.24 = (bf16[256,2048]{1,0:T(8,128)(2,1)S(1)}, bf16[256,2048]{1,0:T(8,128)(2,1)S(1)}, u32[]{:S(2)}, u32[]{:S(2)}) collective-permute-start(bf16[256,2048]{1,0:T(8,128)(2,1)S(1)} %get-tuple-element.90.refs_0_), channel_id=1, source_target_pairs={{0,1},{1,0},{2,3},{3,2},{4,5},{5,4},{6,7},{7,6},{8,9},{9,8},{10,11... | collective-permute-start | bytes 3145736 | tf_op jit(solution)/shard_map/ppermute | solution.py:81
  418.2 26.1 %collective-permute-start.25 = (bf16[256,2048]{1,0:T(8,128)(2,1)S(1)}, bf16[256,2048]{1,0:T(8,128)(2,1)}, u32[]{:S(2)}, u32[]{:S(2)}) collective-permute-start(bf16[256,2048]{1,0:T(8,128)(2,1)S(1)} %get-tuple-element.90.refs_0_), channel_id=1, source_target_pairs={{0,2},{1,3},{2,0},{3,1},{4,6},{5,7},{6,4},{7,5},{8,10},{9,11},{10,... | collective-permute-start | bytes 3145736 | tf_op jit(solution)/shard_map/ppermute | solution.py:81
  475.8 217.9 %reduce-scatter.8.cloned.1.call-start = ((), (), s32[]{:S(2)}) async-start(), calls=%async_computation.8 | async-start | bytes 9437184 | tf_op jit(solution)/shard_map/reduce_scatter | solution.py:76
  503.4 28.0 %collective-permute-start.33 = (bf16[128,2048]{1,0:T(8,128)(2,1)}, bf16[128,2048]{1,0:T(8,128)(2,1)}, u32[]{:S(2)}, u32[]{:S(2)}) collective-permute-start(bf16[128,2048]{1,0:T(8,128)(2,1)} %slice.355), channel_id=1, source_target_pairs={{0,2},{1,3},{2,0},{3,1},{4,6},{5,7},{6,4},{7,5},{8,10},{9,11},{10,... | collective-permute-start | bytes 1572872 | tf_op jit(solution)/shard_map/ppermute | solution.py:81
  505.4 26.0 %collective-permute-start.28 = (bf16[128,2048]{1,0:T(8,128)(2,1)}, bf16[128,2048]{1,0:T(8,128)(2,1)}, u32[]{:S(2)}, u32[]{:S(2)}) collective-permute-start(bf16[128,2048]{1,0:T(8,128)(2,1)} %slice.350), channel_id=1, source_target_pairs={{0,1},{1,0},{2,3},{3,2},{4,5},{5,4},{6,7},{7,6},{8,9},{9,8},{10,11... | collective-permute-start | bytes 1572872 | tf_op jit(solution)/shard_map/ppermute | solution.py:81
  506.0 25.4 %collective-permute-start.32 = (bf16[128,2048]{1,0:T(8,128)(2,1)S(1)}, bf16[128,2048]{1,0:T(8,128)(2,1)}, u32[]{:S(2)}, u32[]{:S(2)}) collective-permute-start(bf16[128,2048]{1,0:T(8,128)(2,1)S(1)} %add_convert_fusion.2), channel_id=1, source_target_pairs={{0,2},{1,3},{2,0},{3,1},{4,6},{5,7},{6,4},{7,5},{8,10},{9,11},{10,... | collective-permute-start | bytes 1572872 | tf_op jit(solution)/shard_map/ppermute | solution.py:81
  507.0 24.4 %collective-permute-start.30 = (bf16[128,2048]{1,0:T(8,128)(2,1)S(1)}, bf16[128,2048]{1,0:T(8,128)(2,1)}, u32[]{:S(2)}, u32[]{:S(2)}) collective-permute-start(bf16[128,2048]{1,0:T(8,128)(2,1)S(1)} %add_convert_fusion.3), channel_id=1, source_target_pairs={{0,1},{1,0},{2,3},{3,2},{4,5},{5,4},{6,7},{7,6},{8,9},{9,8},{10,11... | collective-permute-start | bytes 1572872 | tf_op jit(solution)/shard_map/ppermute | solution.py:81
  622.3 22.5 %collective-permute-start.39 = (bf16[128,2048]{1,0:T(8,128)(2,1)S(1)}, bf16[128,2048]{1,0:T(8,128)(2,1)S(1)}, u32[]{:S(2)}, u32[]{:S(2)}) collective-permute-start(bf16[128,2048]{1,0:T(8,128)(2,1)S(1)} %slice.361), channel_id=1, source_target_pairs={{0,2},{1,3},{2,0},{3,1},{4,6},{5,7},{6,4},{7,5},{8,10},{9,11},{10,... | collective-permute-start | bytes 1572872 | tf_op jit(solution)/shard_map/ppermute | solution.py:81
  622.9 21.9 %collective-permute-start.34 = (bf16[128,2048]{1,0:T(8,128)(2,1)S(1)}, bf16[128,2048]{1,0:T(8,128)(2,1)S(1)}, u32[]{:S(2)}, u32[]{:S(2)}) collective-permute-start(bf16[128,2048]{1,0:T(8,128)(2,1)S(1)} %slice.356), channel_id=1, source_target_pairs={{0,1},{1,0},{2,3},{3,2},{4,5},{5,4},{6,7},{7,6},{8,9},{9,8},{10,11... | collective-permute-start | bytes 1572872 | tf_op jit(solution)/shard_map/ppermute | solution.py:81
  632.6 20.4 %collective-permute-start.38 = (bf16[128,2048]{1,0:T(8,128)(2,1)S(1)}, bf16[128,2048]{1,0:T(8,128)(2,1)S(1)}, u32[]{:S(2)}, u32[]{:S(2)}) collective-permute-start(bf16[128,2048]{1,0:T(8,128)(2,1)S(1)} %add_convert_fusion), channel_id=1, source_target_pairs={{0,2},{1,3},{2,0},{3,1},{4,6},{5,7},{6,4},{7,5},{8,10},{9,11},{10,... | collective-permute-start | bytes 1572872 | tf_op jit(solution)/shard_map/ppermute | solution.py:81
  633.9 19.1 %collective-permute-start.36 = (bf16[128,2048]{1,0:T(8,128)(2,1)S(1)}, bf16[128,2048]{1,0:T(8,128)(2,1)S(1)}, u32[]{:S(2)}, u32[]{:S(2)}) collective-permute-start(bf16[128,2048]{1,0:T(8,128)(2,1)S(1)} %add_convert_fusion.1), channel_id=1, source_target_pairs={{0,1},{1,0},{2,3},{3,2},{4,5},{5,4},{6,7},{7,6},{8,9},{9,8},{10,11... | collective-permute-start | bytes 1572872 | tf_op jit(solution)/shard_map/ppermute | solution.py:81
  (59 other events, 745.9 us)
Sparse Core Ops, SparseCore 0:
  12.7 85.2 all-gather.3
  100.2 114.8 all-gather.5
  217.3 114.8 all-gather.7
  334.4 127.2 reduce-scatter.3
  475.9 126.2 reduce-scatter.5
  605.6 87.9 reduce-scatter.7

commit v3 on v2

--- a/solution.py
+++ b/solution.py
@@ -72,8 +72,26 @@
     return lax.all_gather(own, "dp", axis=axis, tiled=True)
 
 
-def scatter_dp(grad, axis):
-    total = lax.psum_scatter(grad.astype(BF16), "dp", scatter_dimension=axis, tiled=True)
+def core_swap(value):
+    count = lax.axis_size("dp")
+    return lax.ppermute(value, "dp", [(k, k ^ 1) for k in range(count)])
+
+
+def pair_sum(terms):
+    others = [core_swap(dot_first(peer, right).astype(BF16)) for own, peer, right in terms]
+    sums = [
+        (dot_first(own, right) + other.astype(F32)).astype(BF16)
+        for (own, peer, right), other in zip(terms, others)
+    ]
+    return jnp.concatenate(sums, axis=1)
+
+
+def scatter_dp(pairs):
+    count = lax.axis_size("dp")
+    groups = [list(range(core, count, 2)) for core in range(2)]
+    total = lax.psum_scatter(
+        pairs, "dp", scatter_dimension=0, tiled=True, axis_index_groups=groups
+    )
     return total.astype(F32)
 
 
@@ -81,26 +99,42 @@
     return lax.ppermute(value, "tensor", [(k, k ^ bits) for k in range(lax.axis_size("tensor"))])
 
 
-def join_kernel(*refs):
-    out = refs[-1]
+def join_kernel(core_ref, *refs):
+    out, own, peer = refs[-3:]
+    width = own.shape[1]
+    mine = pl.multiple_of(core_ref[0] * width, width)
+    other = pl.multiple_of((1 - core_ref[0]) * width, width)
     start = 0
-    for ref in refs[:-1]:
-        out[start : start + ref.shape[0], :] = ref[...]
+    for ref in refs[:-3]:
+        rows = slice(start, start + ref.shape[0])
+        out[rows, :] = ref[...]
+        own[rows, :] = ref[:, pl.ds(mine, width)]
+        peer[rows, :] = ref[:, pl.ds(other, width)]
         start += ref.shape[0]
 
 
 def join(pieces):
     rows = sum(piece.shape[0] for piece in pieces)
     width = pieces[0].shape[1]
-    tile = min(width, 512)
+    count = lax.axis_size("dp")
+    tile = 2 * width // count
+    core = (lax.axis_index("dp") % 2).astype(jnp.int32).reshape(1)
+    half = pl.BlockSpec((rows, tile // 2), lambda n, c: (0, n))
     return pl.pallas_call(
         join_kernel,
-        out_shape=jax.ShapeDtypeStruct((rows, width), pieces[0].dtype),
-        grid=(width // tile,),
-        in_specs=[pl.BlockSpec((piece.shape[0], tile), lambda n: (0, n)) for piece in pieces],
-        out_specs=pl.BlockSpec((rows, tile), lambda n: (0, n)),
-        cost_estimate=pl.CostEstimate(flops=0, bytes_accessed=4 * rows * width, transcendentals=0),
-    )(*pieces)
+        out_shape=[
+            jax.ShapeDtypeStruct((rows, width), pieces[0].dtype),
+            jax.ShapeDtypeStruct((rows, width // 2), pieces[0].dtype),
+            jax.ShapeDtypeStruct((rows, width // 2), pieces[0].dtype),
+        ],
+        grid_spec=pltpu.PrefetchScalarGridSpec(
+            num_scalar_prefetch=1,
+            grid=(count // 2,),
+            in_specs=[pl.BlockSpec((piece.shape[0], tile), lambda n, c: (0, n)) for piece in pieces],
+            out_specs=[pl.BlockSpec((rows, tile), lambda n, c: (0, n)), half, half],
+        ),
+        cost_estimate=pl.CostEstimate(flops=0, bytes_accessed=6 * rows * width, transcendentals=0),
+    )(core, *pieces)
 
 
 def gather_rows(own):
@@ -114,7 +148,7 @@
         while bits < group:
             own = jnp.concatenate([own, flip(own, bits)], axis=0)
             bits *= 2
-        return own, own
+        return join([own]), own
     half = own.shape[0] // 2
     one = flip(own, 1)
     two = flip(own, 2)
@@ -416,8 +450,8 @@
     residual = tokens.astype(F32)
     grad_out = cotangent.astype(F32) * valid
     normed_one, inverse_one = norm_forward(residual)
-    h1 = gather_rows(normed_one.astype(BF16))
-    g_rows = gather_rows(after(grad_out.astype(BF16), h1))
+    h1, h1_own, h1_peer = gather_rows(normed_one.astype(BF16))
+    g_rows, g_own, g_peer = gather_rows(after(grad_out.astype(BF16), h1))
 
     def rows_of(value, j):
         return value[j * local : (j + 1) * local]
@@ -430,13 +464,11 @@
 
     middle = residual + scatter_rows(attention_piece)
     normed_two, inverse_two = norm_forward(middle)
-    h2 = gather_rows(normed_two.astype(BF16))
+    h2, h2_own, h2_peer = gather_rows(normed_two.astype(BF16))
 
     hidden_0, d_wide_0 = feed(h2, g_rows, wide[0])
-    first_grad = jnp.concatenate(
-        [dot_first(h2, d_wide_0).astype(BF16), dot_first(g_rows, hidden_0).astype(BF16)], axis=1
-    )
-    first_sum = scatter_dp(first_grad, 0)
+    first_grad = pair_sum([(h2_own, h2_peer, d_wide_0), (g_own, g_peer, hidden_0)])
+    first_sum = scatter_dp(first_grad)
     d_first = dot_last(d_wide_0, wide[0][:, : 2 * half])
     wide_1, first_grad, d_first = lax.optimization_barrier((wide[1], first_grad, d_first))
     hidden_1, d_wide_1 = feed(h2, g_rows, wide_1)
@@ -448,32 +480,27 @@
 
     d_normed_two = scatter_rows(feed_back_piece)
     d_middle = grad_out + norm_backward(normed_two, inverse_two, d_normed_two)
-    second_grad = jnp.concatenate(
-        [dot_first(h2, d_wide_1).astype(BF16), dot_first(g_rows, hidden_1).astype(BF16)], axis=1
-    )
-    d_attention = gather_rows(d_middle.astype(BF16))
+    second_grad = pair_sum([(h2_own, h2_peer, d_wide_1), (g_own, g_peer, hidden_1)])
+    (d_attention, d_attention_own, d_attention_peer), neighbour = gather_steps(d_middle.astype(BF16))
+    second_sum = scatter_dp(after(second_grad, first_sum, neighbour))
+
     d_context = dot_plain(d_attention, out_full).astype(BF16)
-    second_sum = scatter_dp(after(second_grad, first_sum, d_context), 0)
+    d_pre = attend_backward(t_arg, saved, d_context, segc, segr, cos, sin)
+    mixed_grad = pair_sum([(h1_own, h1_peer, d_pre), (d_attention_own, d_attention_peer, context)])
+    mixed_sum = scatter_dp(after(mixed_grad, second_sum))
 
     def feed_piece(j, earlier):
-        rows = after(rows_of(hidden_0, j), d_attention if earlier is None else earlier)
+        rows = after(rows_of(hidden_0, j), d_pre if earlier is None else earlier)
         return dot_last(rows, wide[0][:, 2 * half :]) + dot_last(
             rows_of(hidden_1, j), wide_1[:, 2 * half :]
         )
 
     feed_out = scatter_rows(feed_piece)
-
-    d_pre = attend_backward(t_arg, saved, d_context, segc, segr, cos, sin)
-    d_pre = after(d_pre, feed_out)
     output = (valid * (middle + feed_out)).astype(BF16)
-    mixed_grad = jnp.concatenate(
-        [dot_first(h1, d_pre).astype(BF16), dot_first(d_attention, context).astype(BF16)], axis=1
-    )
-    mixed_sum = scatter_dp(after(mixed_grad, second_sum), 0)
 
     def heads_back_piece(j, earlier):
-        rows = rows_of(d_pre, j)
-        return dot_last(rows if earlier is None else after(rows, earlier), heads_full)
+        rows = after(rows_of(d_pre, j), mixed_grad if earlier is None else earlier)
+        return dot_last(rows, heads_full)
 
     d_normed_one = scatter_rows(heads_back_piece)
     input_grad = (d_middle + norm_backward(normed_one, inverse_one, d_normed_one)).astype(BF16)

time: 712 us -> 669 us (0.940)
  waiting for transfers between devices: 285 us -> 255 us
  other arithmetic: 63.5 us -> 40.9 us
    reduce_scatter x3, waiting for transfers between devices: 70.5 us -> 5.29 us  [scatter_dp(): lax.psum_scatter(pairs, 'dp', scatter_dimension=0, tiled=True, axis_index...]
    ppermute x40, waiting for transfers between devices: 161 us -> 190 us  [flip(): lax.ppermute(value, 'tensor', [(k, k ^ bits) for k in range(lax.axis_size...]
    concatenate x3, other arithmetic: 36.7 us -> 8.86 us  [pair_sum(): return jnp.concatenate(sums, axis=1)]
    dot_general x6 -> x12, matrix products: 46.8 us -> 56.3 us  [dot_first(): lax.dot_general(left, right, (((0,), (0,)), ((), ())), preferred_element_...]
    ppermute x0 -> x6, waiting for transfers between devices: none -> 7.77 us  [core_swap(): return lax.ppermute(value, 'dp', [(k, k ^ 1) for k in range(count)])]
    unnamed x100 -> x133, local copies, waits for them, and re-layouts: 17.3 us -> 14.3 us
  transfers between devices with their start and end apart: 46 -> 52, of which waited for: 24 -> 32; matrix products, arithmetic and copies ran while one was open for 34% -> 34% of each run, Pallas kernels for 14% -> 15%
where the time goes in v3:
time: 669 us; the launch traced here: 663 us
  waiting for transfers between devices  255 us (38%)
  matrix products  163 us (24%)
  Pallas kernels  100 us (15%)
  starting transfers between devices  50.2 us (8%)
  other arithmetic  40.9 us (6%)
  local copies, waits for them, and re-layouts  38 us (6%)
  between operations  15.5 us (2%)
    ppermute x40, waiting for transfers between devices, flip(): lax.ppermute(value, 'tensor', [(k, k ^ bits) for k in range(lax.axis_size...  190 us
    dot_general x21, matrix products, dot_last(): lax.dot_general(left, right, (((1,), (1,)), ((), ())), preferred_element_...  88.8 us
    dot_general x12, matrix products, dot_first(): lax.dot_general(left, right, (((0,), (0,)), ((), ())), preferred_element_...  56.3 us
    all_gather x3, waiting for transfers between devices, gather_dp(): return lax.all_gather(own, 'dp', axis=axis, tiled=True)  51.8 us
    ppermute x40, starting transfers between devices, flip(): lax.ppermute(value, 'tensor', [(k, k ^ bits) for k in range(lax.axis_size...  48.5 us
    pallas_call x2, Pallas kernels, feed(): pl.pallas_call(feed_kernel, out_shape=[jax.ShapeDtypeStruct((rows, width)...  42.8 us
    pallas_call x4, Pallas kernels, join(): pl.pallas_call(join_kernel, out_shape=[jax.ShapeDtypeStruct((rows, width)...  24.3 us
    pallas_call x1, Pallas kernels, attend_backward(): pl.pallas_call(kernel, out_shape=jax.ShapeDtypeStruct((rows, 3 * width),...  18.7 us
  transfers between devices with their start and end apart: 52, of which 32 were waited for; matrix products, arithmetic and copies ran while one was open for 34% of the time, Pallas kernels for 15%

profile of v3, /device:TPU:0, one launch (start us, length us, event | category | flops | bytes accessed | tf_op | source)
XLA Modules:
  0.0 663.3 jit_solution(14434727740983381297)
XLA Ops:
  24.6 21.2 %collective-permute-done.refs_1_ = bf16[256,2048]{1,0:T(8,128)(2,1)S(1)} collective-permute-done((bf16[256,2048]{1,0:T(8,128)(2,1)S(1)}, bf16[256,2048]{1,0:T(8,128)(2,1)S(1)}, u32[]{:S(2)}, u32[]{:S(2)}) %collective-permute-start) | collective-permute-done | bytes 1048608 | tf_op jit(solution)/shard_map/ppermute | solution.py:99
  63.4 6.4 shard_map.169
  69.7 28.2 %all-gather.4.cloned.1.call-done = bf16[2048,2048]{0,1:T(8,128)(2,1)} async-done(((bf16[256,2048]{0,1:T(8,128)(2,1)}), bf16[2048,2048]{0,1:T(8,128)(2,1)}) %all-gather.4.cloned.1.call-update) | async-done | bytes 8388624 | tf_op jit(solution)/shard_map/all_gather | solution.py:72
  98.0 11.7 %fusion.18.refs_1_.refs_2_.refs_3_ = f32[1024,1536]{1,0:T(8,128)} fusion(bf16[1024,2048]{1,0:T(8,128)(2,1)} %get-tuple-element.46, bf16[2048,2048]{0,1:T(8,128)(2,1)} %all-gather.4.cloned.1.call-done), kind=kOutput, calls=%fused_computation.29 | convolution fusion | flops 6442450944 | bytes 16777216 | tf_op jit(solution)/shard_map/dot_general | solution.py:56
  109.7 14.6 %shard_map.170 = (bf16[1024,512]{1,0:T(8,128)(2,1)}, bf16[1024,1536]{1,0:T(8,128)(2,1)}) custom-call(s32[1]{0:T(128)} %bitcast.2.refs_0_, f32[1024,1536]{1,0:T(8,128)} %fusion.18.refs_1_.refs_2_.refs_3_, f32[1024,1536]{1,0:T(8,128)} %fusion.18.refs_1_.refs_2_.refs_3_, f32[1024,1536]{1,0:T(8,128)} %fusion.18.refs_1_.refs_2_.refs_3_, ...), custom_call_target="tpu_custom_call" | custom-call | flops 2147483648 | bytes 10485760 | tf_op jit(solution)/shard_map/pallas_call | solution.py:289
  135.6 7.4 %collective-permute-done.5 = bf16[128,2048]{1,0:T(8,128)(2,1)S(1)} collective-permute-done((bf16[128,2048]{1,0:T(8,128)(2,1)S(1)}, bf16[128,2048]{1,0:T(8,128)(2,1)S(1)}, u32[]{:S(2)}, u32[]{:S(2)}) %collective-permute-start.5) | collective-permute-done | bytes 524320 | tf_op jit(solution)/shard_map/ppermute | solution.py:99
  158.2 11.2 %collective-permute-done.6 = bf16[128,2048]{1,0:T(8,128)(2,1)S(1)} collective-permute-done((bf16[128,2048]{1,0:T(8,128)(2,1)S(1)}, bf16[128,2048]{1,0:T(8,128)(2,1)S(1)}, u32[]{:S(2)}, u32[]{:S(2)}) %collective-permute-start.6) | collective-permute-done | bytes 524320 | tf_op jit(solution)/shard_map/ppermute | solution.py:99
  173.6 18.3 %collective-permute-done.14.refs_1_ = bf16[256,2048]{1,0:T(8,128)(2,1)S(1)} collective-permute-done((bf16[256,2048]{1,0:T(8,128)(2,1)S(1)}, bf16[256,2048]{1,0:T(8,128)(2,1)S(1)}, u32[]{:S(2)}, u32[]{:S(2)}) %collective-permute-start.14) | collective-permute-done | bytes 1048608 | tf_op jit(solution)/shard_map/ppermute | solution.py:99
  194.2 20.2 %collective-permute-done.10.refs_1_ = bf16[256,2048]{1,0:T(8,128)(2,1)S(1)} collective-permute-done((bf16[256,2048]{1,0:T(8,128)(2,1)S(1)}, bf16[256,2048]{1,0:T(8,128)(2,1)S(1)}, u32[]{:S(2)}, u32[]{:S(2)}) %collective-permute-start.10) | collective-permute-done | bytes 1048608 | tf_op jit(solution)/shard_map/ppermute | solution.py:99
  225.7 6.1 shard_map.172
  235.9 5.9 shard_map.171
  241.8 21.3 %shard_map.173 = (bf16[1024,1024]{1,0:T(8,128)(2,1)}, bf16[1024,2048]{1,0:T(8,128)(2,1)}) custom-call(bf16[1024,2048]{1,0:T(8,128)(2,1)} %get-tuple-element.51.h_ref, bf16[1024,2048]{1,0:T(8,128)(2,1)} %get-tuple-element.53.g_ref, bf16[2048,3072]{1,0:T(8,128)(2,1)} %all-gather.6.cloned.1.call-done.gate_ref.up_ref.down_ref, ...), custom_call_target="tpu_custom_call" | custom-call | flops 12884901888 | bytes 27262976 | tf_op jit(solution)/shard_map/pallas_call | solution.py:206
  263.1 7.7 %convolution_convert_fusion.2 = bf16[1024,2048]{1,0:T(8,128)(2,1)S(1)} fusion(bf16[1024,1024]{1,0:T(8,128)(2,1)} %get-tuple-element.58, bf16[1024,2048]{1,0:T(8,128)(2,1)} %get-tuple-element.57), kind=kOutput, calls=%fused_computation.20 | convolution fusion | flops 4297064448 | bytes 10485760 | tf_op jit(solution)/shard_map/dot_general | solution.py:60
  273.9 7.8 %collective-permute-done.19 = bf16[1024,1024]{1,0:T(8,128)(2,1)S(1)} collective-permute-done((bf16[1024,1024]{1,0:T(8,128)(2,1)S(1)}, bf16[1024,1024]{1,0:T(8,128)(2,1)S(1)}, u32[]{:S(2)}, u32[]{:S(2)}) %collective-permute-start.19) | collective-permute-done | bytes 2097184 | tf_op jit(solution)/shard_map/ppermute | solution.py:77
  293.0 14.6 %fusion = f32[1024,2048]{1,0:T(8,128)} fusion(bf16[1024,2048]{1,0:T(8,128)(2,1)} %get-tuple-element.57, bf16[2048,3072]{1,0:T(8,128)(2,1)} %all-gather.6.cloned.1.call-done.gate_ref.up_ref.down_ref), kind=kOutput, calls=%fused_computation | convolution fusion | flops 8589934592 | bytes 20971520 | tf_op jit(solution)/shard_map/dot_general | solution.py:64
  307.6 23.5 %all-gather.8.cloned.1.call-done.gate_ref.up_ref.down_ref = bf16[2048,3072]{1,0:T(8,128)(2,1)} async-done(((bf16[256,3072]{1,0:T(8,128)(2,1)}), bf16[2048,3072]{1,0:T(8,128)(2,1)}) %all-gather.8.cloned.1.call-update) | async-done | bytes 12582928 | tf_op jit(solution)/shard_map/all_gather | solution.py:72
  331.1 21.5 %shard_map.174 = (bf16[1024,1024]{1,0:T(8,128)(2,1)}, bf16[1024,2048]{1,0:T(8,128)(2,1)}) custom-call(bf16[1024,2048]{1,0:T(8,128)(2,1)} %get-tuple-element.51.h_ref, bf16[1024,2048]{1,0:T(8,128)(2,1)} %get-tuple-element.53.g_ref, bf16[2048,3072]{1,0:T(8,128)(2,1)} %all-gather.8.cloned.1.call-done.gate_ref.up_ref.down_ref, ...), custom_call_target="tpu_custom_call" | custom-call | flops 12884901888 | bytes 27262976 | tf_op jit(solution)/shard_map/pallas_call | solution.py:206
  352.6 7.5 %convolution_convert_fusion.1 = bf16[1024,2048]{1,0:T(8,128)(2,1)S(1)} fusion(bf16[1024,1024]{1,0:T(8,128)(2,1)} %get-tuple-element.58, bf16[1024,2048]{1,0:T(8,128)(2,1)} %get-tuple-element.63), kind=kOutput, calls=%fused_computation.19 | convolution fusion | flops 4297064448 | bytes 10485760 | tf_op jit(solution)/shard_map/dot_general | solution.py:60
  360.9 6.3 fusion.66
  367.2 6.3 fusion.63
  376.8 6.3 fusion.60
  401.3 10.3 %collective-permute-done.22 = bf16[128,2048]{1,0:T(8,128)(2,1)S(1)} collective-permute-done((bf16[128,2048]{1,0:T(8,128)(2,1)S(1)}, bf16[128,2048]{1,0:T(8,128)(2,1)S(1)}, u32[]{:S(2)}, u32[]{:S(2)}) %collective-permute-start.22) | collective-permute-done | bytes 524320 | tf_op jit(solution)/shard_map/ppermute | solution.py:99
  411.6 7.2 %fusion.118 = (f32[256]{0:T(256)S(1)}, f32[256]{0:T(256)S(1)}, f32[256,2048]{1,0:T(8,128)S(1)}) fusion(bf16[128,2048]{1,0:T(8,128)(2,1)S(1)} %collective-permute-done.25, bf16[128,2048]{1,0:T(8,128)(2,1)S(1)} %collective-permute-done.24, bf16[128,2048]{1,0:T(8,128)(2,1)S(1)} %collective-permute-done.22, bf16[128,2048]{1,0:T(8,128)(2,1)S(1)} %collective-permute-done.20, ...), kind=kOutput, calls=%fused_computation.148 | convolution fusion | flops 2155871744 | bytes 17829888 | tf_op jit(solution)/shard_map/dot_general | solution.py:64
  427.3 6.5 add_convert_fusion
  449.5 22.9 %collective-permute-done.27.refs_2_ = bf16[256,2048]{1,0:T(8,128)(2,1)S(1)} collective-permute-done((bf16[256,2048]{1,0:T(8,128)(2,1)S(1)}, bf16[256,2048]{1,0:T(8,128)(2,1)S(1)}, u32[]{:S(2)}, u32[]{:S(2)}) %collective-permute-start.27) | collective-permute-done | bytes 1048608 | tf_op jit(solution)/shard_map/ppermute | solution.py:99
  490.9 6.2 convolution_convert_fusion.9.refs_4_
  497.1 18.7 %shard_map.176 = bf16[1024,1536]{1,0:T(8,128)(2,1)} custom-call(s32[1]{0:T(128)} %bitcast.2.refs_0_, bf16[1024,1536]{1,0:T(8,128)(2,1)} %get-tuple-element.55.refs_1_.refs_2_.refs_3_, bf16[1024,1536]{1,0:T(8,128)(2,1)} %get-tuple-element.55.refs_1_.refs_2_.refs_3_, bf16[1024,1536]{1,0:T(8,128)(2,1)} %get-tuple-element.55.refs_1_.refs_2_.refs_3_, ...), custom_call_target="tpu_custom_call" | custom-call | flops 5368709120 | bytes 7340032 | tf_op jit(solution)/shard_map/pallas_call | solution.py:380
  515.9 7.8 %convolution_convert_fusion = bf16[1024,1536]{1,0:T(8,128)(2,1)} fusion(bf16[1024,1024]{1,0:T(8,128)(2,1)} %get-tuple-element.74, bf16[1024,1536]{1,0:T(8,128)(2,1)} %shard_map.176), kind=kOutput, calls=%fused_computation.18 | convolution fusion | flops 3222798336 | bytes 8388608 | tf_op jit(solution)/shard_map/dot_general | solution.py:60
  592.1 7.8 %collective-permute-done.39 = bf16[128,2048]{1,0:T(8,128)(2,1)S(1)} collective-permute-done((bf16[128,2048]{1,0:T(8,128)(2,1)S(1)}, bf16[128,2048]{1,0:T(8,128)(2,1)S(1)}, u32[]{:S(2)}, u32[]{:S(2)}) %collective-permute-start.39) | collective-permute-done | bytes 524320 | tf_op jit(solution)/shard_map/ppermute | solution.py:99
  606.7 8.1 %collective-permute-done.32 = bf16[128,2048]{1,0:T(8,128)(2,1)S(1)} collective-permute-done((bf16[128,2048]{1,0:T(8,128)(2,1)S(1)}, bf16[128,2048]{1,0:T(8,128)(2,1)S(1)}, u32[]{:S(2)}, u32[]{:S(2)}) %collective-permute-start.32) | collective-permute-done | bytes 524320 | tf_op jit(solution)/shard_map/ppermute | solution.py:99
  620.0 6.0 collective-permute-done.38
  626.0 9.0 %collective-permute-done.40 = bf16[128,2048]{1,0:T(8,128)(2,1)S(1)} collective-permute-done((bf16[128,2048]{1,0:T(8,128)(2,1)S(1)}, bf16[128,2048]{1,0:T(8,128)(2,1)S(1)}, u32[]{:S(2)}, u32[]{:S(2)}) %collective-permute-start.40) | collective-permute-done | bytes 524320 | tf_op jit(solution)/shard_map/ppermute | solution.py:99
  (337 shorter events, 263.2 us)
Async XLA Ops:
  7.2 90.8 %all-gather.4.cloned.1.call-start = ((), (), s32[]{:S(2)}) async-start(), calls=%async_computation.3 | async-start | bytes 9437184 | tf_op jit(solution)/shard_map/all_gather | solution.py:72
  12.6 229.2 %all-gather.6.cloned.1.call-start = ((), (), s32[]{:S(2)}) async-start(), calls=%async_computation.4 | async-start | bytes 14155776 | tf_op jit(solution)/shard_map/all_gather | solution.py:72
  15.9 315.2 %all-gather.8.cloned.1.call-start = ((), (), s32[]{:S(2)}) async-start(), calls=%async_computation.5 | async-start | bytes 14155776 | tf_op jit(solution)/shard_map/all_gather | solution.py:72
  17.5 424.8 %reduce-scatter.4.cloned.1.call-start = ((), (), s32[]{:S(2)}) async-start(), calls=%async_computation.6 | async-start | bytes 7864320 | tf_op jit(solution)/shard_map/reduce_scatter | solution.py:92
  19.6 26.2 %collective-permute-start = (bf16[256,2048]{1,0:T(8,128)(2,1)S(1)}, bf16[256,2048]{1,0:T(8,128)(2,1)S(1)}, u32[]{:S(2)}, u32[]{:S(2)}) collective-permute-start(bf16[256,2048]{1,0:T(8,128)(2,1)S(1)} %fusion.91.refs_0_), channel_id=1, source_target_pairs={{0,1},{1,0},{2,3},{3,2},{4,5},{5,4},{6,7},{7,6},{8,9},{9,8},{10,11... | collective-permute-start | bytes 3145736 | tf_op jit(solution)/shard_map/ppermute | solution.py:99
  22.7 25.8 %collective-permute-start.1 = (bf16[256,2048]{1,0:T(8,128)(2,1)S(1)}, bf16[256,2048]{1,0:T(8,128)(2,1)}, u32[]{:S(2)}, u32[]{:S(2)}) collective-permute-start(bf16[256,2048]{1,0:T(8,128)(2,1)S(1)} %fusion.91.refs_0_), channel_id=1, source_target_pairs={{0,2},{1,3},{2,0},{3,1},{4,6},{5,7},{6,4},{7,5},{8,10},{9,11},{10,... | collective-permute-start | bytes 3145736 | tf_op jit(solution)/shard_map/ppermute | solution.py:99
  135.1 23.0 %collective-permute-start.4 = (bf16[128,2048]{1,0:T(8,128)(2,1)S(1)}, bf16[128,2048]{1,0:T(8,128)(2,1)S(1)}, u32[]{:S(2)}, u32[]{:S(2)}) collective-permute-start(bf16[128,2048]{1,0:T(8,128)(2,1)S(1)} %slice.330), channel_id=1, source_target_pairs={{0,1},{1,0},{2,3},{3,2},{4,5},{5,4},{6,7},{7,6},{8,9},{9,8},{10,11... | collective-permute-start | bytes 1572872 | tf_op jit(solution)/shard_map/ppermute | solution.py:99
  143.1 26.3 %collective-permute-start.6 = (bf16[128,2048]{1,0:T(8,128)(2,1)S(1)}, bf16[128,2048]{1,0:T(8,128)(2,1)S(1)}, u32[]{:S(2)}, u32[]{:S(2)}) collective-permute-start(bf16[128,2048]{1,0:T(8,128)(2,1)S(1)} %add_convert_fusion.13), channel_id=1, source_target_pairs={{0,1},{1,0},{2,3},{3,2},{4,5},{5,4},{6,7},{7,6},{8,9},{9,8},{10,11... | collective-permute-start | bytes 1572872 | tf_op jit(solution)/shard_map/ppermute | solution.py:99
  147.1 22.3 %collective-permute-start.8 = (bf16[128,2048]{1,0:T(8,128)(2,1)S(1)}, bf16[128,2048]{1,0:T(8,128)(2,1)S(1)}, u32[]{:S(2)}, u32[]{:S(2)}) collective-permute-start(bf16[128,2048]{1,0:T(8,128)(2,1)S(1)} %add_convert_fusion.12), channel_id=1, source_target_pairs={{0,2},{1,3},{2,0},{3,1},{4,6},{5,7},{6,4},{7,5},{8,10},{9,11},{10,... | collective-permute-start | bytes 1572872 | tf_op jit(solution)/shard_map/ppermute | solution.py:99
  148.0 43.9 %collective-permute-start.14 = (bf16[256,2048]{1,0:T(8,128)(2,1)S(1)}, bf16[256,2048]{1,0:T(8,128)(2,1)S(1)}, u32[]{:S(2)}, u32[]{:S(2)}) collective-permute-start(bf16[256,2048]{1,0:T(8,128)(2,1)S(1)} %fusion.98.refs_0_), channel_id=1, source_target_pairs={{0,1},{1,0},{2,3},{3,2},{4,5},{5,4},{6,7},{7,6},{8,9},{9,8},{10,11... | collective-permute-start | bytes 3145736 | tf_op jit(solution)/shard_map/ppermute | solution.py:99
  154.2 38.3 %collective-permute-start.15 = (bf16[256,2048]{1,0:T(8,128)(2,1)S(1)}, bf16[256,2048]{1,0:T(8,128)(2,1)S(1)}, u32[]{:S(2)}, u32[]{:S(2)}) collective-permute-start(bf16[256,2048]{1,0:T(8,128)(2,1)S(1)} %fusion.98.refs_0_), channel_id=1, source_target_pairs={{0,2},{1,3},{2,0},{3,1},{4,6},{5,7},{6,4},{7,5},{8,10},{9,11},{10,... | collective-permute-start | bytes 3145736 | tf_op jit(solution)/shard_map/ppermute | solution.py:99
  171.4 42.9 %collective-permute-start.10 = (bf16[256,2048]{1,0:T(8,128)(2,1)S(1)}, bf16[256,2048]{1,0:T(8,128)(2,1)S(1)}, u32[]{:S(2)}, u32[]{:S(2)}) collective-permute-start(bf16[256,2048]{1,0:T(8,128)(2,1)S(1)} %fusion.99.refs_0_), channel_id=1, source_target_pairs={{0,1},{1,0},{2,3},{3,2},{4,5},{5,4},{6,7},{7,6},{8,9},{9,8},{10,11... | collective-permute-start | bytes 3145736 | tf_op jit(solution)/shard_map/ppermute | solution.py:99
  173.0 42.8 %collective-permute-start.11 = (bf16[256,2048]{1,0:T(8,128)(2,1)S(1)}, bf16[256,2048]{1,0:T(8,128)(2,1)S(1)}, u32[]{:S(2)}, u32[]{:S(2)}) collective-permute-start(bf16[256,2048]{1,0:T(8,128)(2,1)S(1)} %fusion.99.refs_0_), channel_id=1, source_target_pairs={{0,2},{1,3},{2,0},{3,1},{4,6},{5,7},{6,4},{7,5},{8,10},{9,11},{10,... | collective-permute-start | bytes 3145736 | tf_op jit(solution)/shard_map/ppermute | solution.py:99
  191.9 29.7 %collective-permute-start.16 = (bf16[128,2048]{1,0:T(8,128)(2,1)S(1)}, bf16[128,2048]{1,0:T(8,128)(2,1)S(1)}, u32[]{:S(2)}, u32[]{:S(2)}) collective-permute-start(bf16[128,2048]{1,0:T(8,128)(2,1)S(1)} %slice.338), channel_id=1, source_target_pairs={{0,2},{1,3},{2,0},{3,1},{4,6},{5,7},{6,4},{7,5},{8,10},{9,11},{10,... | collective-permute-start | bytes 1572872 | tf_op jit(solution)/shard_map/ppermute | solution.py:99
  192.6 33.1 %collective-permute-start.17 = (bf16[128,2048]{1,0:T(8,128)(2,1)S(1)}, bf16[128,2048]{1,0:T(8,128)(2,1)}, u32[]{:S(2)}, u32[]{:S(2)}) collective-permute-start(bf16[128,2048]{1,0:T(8,128)(2,1)S(1)} %slice.339), channel_id=1, source_target_pairs={{0,1},{1,0},{2,3},{3,2},{4,5},{5,4},{6,7},{7,6},{8,9},{9,8},{10,11... | collective-permute-start | bytes 1572872 | tf_op jit(solution)/shard_map/ppermute | solution.py:99
  293.0 274.5 %reduce-scatter.6.cloned.1.call-start = ((), (), s32[]{:S(2)}) async-start(), calls=%async_computation.7 | async-start | bytes 7864320 | tf_op jit(solution)/shard_map/reduce_scatter | solution.py:92
  360.2 67.1 %collective-permute-start.44 = (bf16[1024,2048]{1,0:T(8,128)(2,1)S(1)}, bf16[1024,2048]{1,0:T(8,128)(2,1)}, u32[]{:S(2)}, u32[]{:S(2)}) collective-permute-start(bf16[1024,2048]{1,0:T(8,128)(2,1)S(1)} %convolution_convert_fusion.1), channel_id=1, source_target_pairs={{0,4},{4,0},{8,12},{12,8},{16,20},{20,16},{24,28},{28,24},{1,5},{5... | collective-permute-start | bytes 12582920 | tf_op jit(solution)/shard_map/ppermute | solution.py:77
  388.7 22.8 %collective-permute-start.22 = (bf16[128,2048]{1,0:T(8,128)(2,1)S(1)}, bf16[128,2048]{1,0:T(8,128)(2,1)S(1)}, u32[]{:S(2)}, u32[]{:S(2)}) collective-permute-start(bf16[128,2048]{1,0:T(8,128)(2,1)S(1)} %add_convert_fusion.11), channel_id=1, source_target_pairs={{0,1},{1,0},{2,3},{3,2},{4,5},{5,4},{6,7},{7,6},{8,9},{9,8},{10,11... | collective-permute-start | bytes 1572872 | tf_op jit(solution)/shard_map/ppermute | solution.py:99
  399.8 23.4 %collective-permute-start.45 = (bf16[1024,1024]{1,0:T(8,128)(2,1)}, bf16[1024,1024]{1,0:T(8,128)(2,1)}, u32[]{:S(2)}, u32[]{:S(2)}) collective-permute-start(bf16[1024,1024]{1,0:T(8,128)(2,1)} %convolution_convert_fusion.6), channel_id=1, source_target_pairs={{0,4},{4,0},{8,12},{12,8},{16,20},{20,16},{24,28},{28,24},{1,5},{5... | collective-permute-start | bytes 6291464 | tf_op jit(solution)/shard_map/ppermute | solution.py:77
  421.8 24.4 %collective-permute-start.26 = (bf16[256,2048]{1,0:T(8,128)(2,1)S(1)}, bf16[256,2048]{1,0:T(8,128)(2,1)}, u32[]{:S(2)}, u32[]{:S(2)}) collective-permute-start(bf16[256,2048]{1,0:T(8,128)(2,1)S(1)} %get-tuple-element.114.refs_0_), channel_id=1, source_target_pairs={{0,1},{1,0},{2,3},{3,2},{4,5},{5,4},{6,7},{7,6},{8,9},{9,8},{10,11... | collective-permute-start | bytes 3145736 | tf_op jit(solution)/shard_map/ppermute | solution.py:99
  446.2 206.3 %reduce-scatter.8.cloned.1.call-start = ((), (), s32[]{:S(2)}) async-start(), calls=%async_computation.8 | async-start | bytes 5242880 | tf_op jit(solution)/shard_map/reduce_scatter | solution.py:92
  446.3 26.1 %collective-permute-start.27 = (bf16[256,2048]{1,0:T(8,128)(2,1)S(1)}, bf16[256,2048]{1,0:T(8,128)(2,1)S(1)}, u32[]{:S(2)}, u32[]{:S(2)}) collective-permute-start(bf16[256,2048]{1,0:T(8,128)(2,1)S(1)} %get-tuple-element.114.refs_0_), channel_id=1, source_target_pairs={{0,2},{1,3},{2,0},{3,1},{4,6},{5,7},{6,4},{7,5},{8,10},{9,11},{10,... | collective-permute-start | bytes 3145736 | tf_op jit(solution)/shard_map/ppermute | solution.py:99
  448.4 33.6 %collective-permute-start.28 = (bf16[128,2048]{1,0:T(8,128)(2,1)S(1)}, bf16[128,2048]{1,0:T(8,128)(2,1)}, u32[]{:S(2)}, u32[]{:S(2)}) collective-permute-start(bf16[128,2048]{1,0:T(8,128)(2,1)S(1)} %slice.347), channel_id=1, source_target_pairs={{0,2},{1,3},{2,0},{3,1},{4,6},{5,7},{6,4},{7,5},{8,10},{9,11},{10,... | collective-permute-start | bytes 1572872 | tf_op jit(solution)/shard_map/ppermute | solution.py:99
  523.7 37.2 %collective-permute-start.36 = (bf16[1024,1536]{1,0:T(8,128)(2,1)}, bf16[1024,1536]{1,0:T(8,128)(2,1)S(1)}, u32[]{:S(2)}, u32[]{:S(2)}) collective-permute-start(bf16[1024,1536]{1,0:T(8,128)(2,1)} %convolution_convert_fusion), channel_id=1, source_target_pairs={{0,4},{4,0},{8,12},{12,8},{16,20},{20,16},{24,28},{28,24},{1,5},{5... | collective-permute-start | bytes 9437192 | tf_op jit(solution)/shard_map/ppermute | solution.py:77
  526.0 31.2 %collective-permute-start.37 = (bf16[1024,512]{1,0:T(8,128)(2,1)}, bf16[1024,512]{1,0:T(8,128)(2,1)}, u32[]{:S(2)}, u32[]{:S(2)}) collective-permute-start(bf16[1024,512]{1,0:T(8,128)(2,1)} %convolution_convert_fusion.8), channel_id=1, source_target_pairs={{0,4},{4,0},{8,12},{12,8},{16,20},{20,16},{24,28},{28,24},{1,5},{5... | collective-permute-start | bytes 3145736 | tf_op jit(solution)/shard_map/ppermute | solution.py:77
  548.8 22.2 %collective-permute-start.33 = (bf16[128,2048]{1,0:T(8,128)(2,1)}, bf16[128,2048]{1,0:T(8,128)(2,1)}, u32[]{:S(2)}, u32[]{:S(2)}) collective-permute-start(bf16[128,2048]{1,0:T(8,128)(2,1)} %get-tuple-element.138), channel_id=1, source_target_pairs={{0,1},{1,0},{2,3},{3,2},{4,5},{5,4},{6,7},{7,6},{8,9},{9,8},{10,11... | collective-permute-start | bytes 1572872 | tf_op jit(solution)/shard_map/ppermute | solution.py:99
  550.3 52.2 %collective-permute-start.35 = (bf16[128,2048]{1,0:T(8,128)(2,1)}, bf16[128,2048]{1,0:T(8,128)(2,1)}, u32[]{:S(2)}, u32[]{:S(2)}) collective-permute-start(bf16[128,2048]{1,0:T(8,128)(2,1)} %slice.355), channel_id=1, source_target_pairs={{0,2},{1,3},{2,0},{3,1},{4,6},{5,7},{6,4},{7,5},{8,10},{9,11},{10,... | collective-permute-start | bytes 1572872 | tf_op jit(solution)/shard_map/ppermute | solution.py:99
  552.2 51.9 %collective-permute-start.30 = (bf16[128,2048]{1,0:T(8,128)(2,1)}, bf16[128,2048]{1,0:T(8,128)(2,1)}, u32[]{:S(2)}, u32[]{:S(2)}) collective-permute-start(bf16[128,2048]{1,0:T(8,128)(2,1)} %slice.350), channel_id=1, source_target_pairs={{0,1},{1,0},{2,3},{3,2},{4,5},{5,4},{6,7},{7,6},{8,9},{9,8},{10,11... | collective-permute-start | bytes 1572872 | tf_op jit(solution)/shard_map/ppermute | solution.py:99
  572.4 32.3 %collective-permute-start.34 = (bf16[128,2048]{1,0:T(8,128)(2,1)S(1)}, bf16[128,2048]{1,0:T(8,128)(2,1)S(1)}, u32[]{:S(2)}, u32[]{:S(2)}) collective-permute-start(bf16[128,2048]{1,0:T(8,128)(2,1)S(1)} %add_convert_fusion.8), channel_id=1, source_target_pairs={{0,2},{1,3},{2,0},{3,1},{4,6},{5,7},{6,4},{7,5},{8,10},{9,11},{10,... | collective-permute-start | bytes 1572872 | tf_op jit(solution)/shard_map/ppermute | solution.py:99
  602.6 23.4 %collective-permute-start.38 = (bf16[128,2048]{1,0:T(8,128)(2,1)S(1)}, bf16[128,2048]{1,0:T(8,128)(2,1)S(1)}, u32[]{:S(2)}, u32[]{:S(2)}) collective-permute-start(bf16[128,2048]{1,0:T(8,128)(2,1)S(1)} %slice.360), channel_id=1, source_target_pairs={{0,1},{1,0},{2,3},{3,2},{4,5},{5,4},{6,7},{7,6},{8,9},{9,8},{10,11... | collective-permute-start | bytes 1572872 | tf_op jit(solution)/shard_map/ppermute | solution.py:99
  604.1 30.9 %collective-permute-start.40 = (bf16[128,2048]{1,0:T(8,128)(2,1)S(1)}, bf16[128,2048]{1,0:T(8,128)(2,1)S(1)}, u32[]{:S(2)}, u32[]{:S(2)}) collective-permute-start(bf16[128,2048]{1,0:T(8,128)(2,1)S(1)} %add_convert_fusion.7), channel_id=1, source_target_pairs={{0,1},{1,0},{2,3},{3,2},{4,5},{5,4},{6,7},{7,6},{8,9},{9,8},{10,11... | collective-permute-start | bytes 1572872 | tf_op jit(solution)/shard_map/ppermute | solution.py:99
  604.7 30.4 %collective-permute-start.42 = (bf16[128,2048]{1,0:T(8,128)(2,1)S(1)}, bf16[128,2048]{1,0:T(8,128)(2,1)S(1)}, u32[]{:S(2)}, u32[]{:S(2)}) collective-permute-start(bf16[128,2048]{1,0:T(8,128)(2,1)S(1)} %add_convert_fusion.6), channel_id=1, source_target_pairs={{0,2},{1,3},{2,0},{3,1},{4,6},{5,7},{6,4},{7,5},{8,10},{9,11},{10,... | collective-permute-start | bytes 1572872 | tf_op jit(solution)/shard_map/ppermute | solution.py:99
  (83 other events, 1020.1 us)
Sparse Core Ops, SparseCore 0:
  12.7 85.1 all-gather.3
  99.6 114.8 all-gather.5
  216.2 114.8 all-gather.7
  333.3 108.9 reduce-scatter.3
  446.3 110.7 reduce-scatter.5
  571.1 76.8 reduce-scatter.7

commit v4 on v3

--- a/solution.py
+++ b/solution.py
@@ -148,13 +148,13 @@
         while bits < group:
             own = jnp.concatenate([own, flip(own, bits)], axis=0)
             bits *= 2
-        return join([own]), own
+        return join([own]), (own,)
     half = own.shape[0] // 2
     one = flip(own, 1)
     two = flip(own, 2)
     far_top = flip(one[:half], 2)
     far_low = flip(two[half:], 1)
-    return join([own, one, two, far_top, far_low]), one
+    return join([own, one, two, far_top, far_low]), (one, two)
 
 
 def scatter_rows(piece):
@@ -178,7 +178,7 @@
     two_low = flip(two[half:], 2)
     one_low = flip((one[half:].astype(F32) + low.astype(F32)).astype(BF16), 1)
     two_top = flip((two[:half].astype(F32) + top.astype(F32)).astype(BF16), 2)
-    own = piece(0, two)
+    own = lax.optimization_barrier(piece(0, two))
     ones = jnp.concatenate([one_top, one_low], axis=0).astype(F32)
     twos = jnp.concatenate([two_top, two_low], axis=0).astype(F32)
     return own + ones + twos
@@ -473,16 +473,20 @@
     wide_1, first_grad, d_first = lax.optimization_barrier((wide[1], first_grad, d_first))
     hidden_1, d_wide_1 = feed(h2, g_rows, wide_1)
 
+    pieces = []
+
     def feed_back_piece(j, earlier):
         rows = rows_of(d_wide_1, j)
         rows = rows if earlier is None else after(rows, earlier)
-        return rows_of(d_first, j) + dot_last(rows, wide_1[:, : 2 * half])
+        pieces.append(rows_of(d_first, j) + dot_last(rows, wide_1[:, : 2 * half]))
+        return pieces[-1]
 
     d_normed_two = scatter_rows(feed_back_piece)
     d_middle = grad_out + norm_backward(normed_two, inverse_two, d_normed_two)
+    d_wide_1, hidden_1, _ = lax.optimization_barrier((d_wide_1, hidden_1, pieces[-1]))
     second_grad = pair_sum([(h2_own, h2_peer, d_wide_1), (g_own, g_peer, hidden_1)])
-    (d_attention, d_attention_own, d_attention_peer), neighbour = gather_steps(d_middle.astype(BF16))
-    second_sum = scatter_dp(after(second_grad, first_sum, neighbour))
+    (d_attention, d_attention_own, d_attention_peer), neighbours = gather_steps(d_middle.astype(BF16))
+    second_sum = scatter_dp(after(second_grad, first_sum, *neighbours))
 
     d_context = dot_plain(d_attention, out_full).astype(BF16)
     d_pre = attend_backward(t_arg, saved, d_context, segc, segr, cos, sin)

time: 669 us -> 655 us (0.979)
  matrix products: 163 us -> 138 us
  local copies, waits for them, and re-layouts: 38 us -> 45.3 us
    ppermute x40, waiting for transfers between devices: 190 us -> 158 us  [flip(): lax.ppermute(value, 'tensor', [(k, k ^ bits) for k in range(lax.axis_size...]
    reduce_scatter x3, waiting for transfers between devices: 5.29 us -> 36.9 us  [scatter_dp(): lax.psum_scatter(pairs, 'dp', scatter_dimension=0, tiled=True, axis_index...]
    dot_general x21, matrix products: 88.8 us -> 73.9 us  [dot_last(): lax.dot_general(left, right, (((1,), (1,)), ((), ())), preferred_element_...]
    dot_general x12, matrix products: 56.3 us -> 46.3 us  [dot_first(): lax.dot_general(left, right, (((0,), (0,)), ((), ())), preferred_element_...]
    unnamed x133 -> x121, local copies, waits for them, and re-layouts: 14.3 us -> 15.2 us
  transfers between devices with their start and end apart: 52 -> 52, of which waited for: 32 -> 28; matrix products, arithmetic and copies ran while one was open for 34% -> 32% of each run, Pallas kernels for 15% -> 15%
where the time goes in v4:
time: 655 us; the launch traced here: 649 us
  waiting for transfers between devices  255 us (39%)
  matrix products  138 us (21%)
  Pallas kernels  100 us (15%)
  starting transfers between devices  51.2 us (8%)
  local copies, waits for them, and re-layouts  45.3 us (7%)
  other arithmetic  44.1 us (7%)
  between operations  15.8 us (2%)
    ppermute x40, waiting for transfers between devices, flip(): lax.ppermute(value, 'tensor', [(k, k ^ bits) for k in range(lax.axis_size...  158 us
    dot_general x21, matrix products, dot_last(): lax.dot_general(left, right, (((1,), (1,)), ((), ())), preferred_element_...  73.9 us
    all_gather x3, waiting for transfers between devices, gather_dp(): return lax.all_gather(own, 'dp', axis=axis, tiled=True)  51.6 us
    ppermute x40, starting transfers between devices, flip(): lax.ppermute(value, 'tensor', [(k, k ^ bits) for k in range(lax.axis_size...  49.7 us
    dot_general x12, matrix products, dot_first(): lax.dot_general(left, right, (((0,), (0,)), ((), ())), preferred_element_...  46.3 us
    pallas_call x2, Pallas kernels, feed(): pl.pallas_call(feed_kernel, out_shape=[jax.ShapeDtypeStruct((rows, width)...  42.9 us
    reduce_scatter x3, waiting for transfers between devices, scatter_dp(): lax.psum_scatter(pairs, 'dp', scatter_dimension=0, tiled=True, axis_index...  36.9 us
    pallas_call x4, Pallas kernels, join(): pl.pallas_call(join_kernel, out_shape=[jax.ShapeDtypeStruct((rows, width)...  24.1 us
  transfers between devices with their start and end apart: 52, of which 28 were waited for; matrix products, arithmetic and copies ran while one was open for 32% of the time, Pallas kernels for 15%

profile of v4, /device:TPU:0, one launch (start us, length us, event | category | flops | bytes accessed | tf_op | source)
XLA Modules:
  0.0 649.3 jit_solution(7868103250806278977)
XLA Ops:
  25.9 20.0 %collective-permute-done.refs_1_ = bf16[256,2048]{1,0:T(8,128)(2,1)S(1)} collective-permute-done((bf16[256,2048]{1,0:T(8,128)(2,1)S(1)}, bf16[256,2048]{1,0:T(8,128)(2,1)S(1)}, u32[]{:S(2)}, u32[]{:S(2)}) %collective-permute-start) | collective-permute-done | bytes 1048608 | tf_op jit(solution)/shard_map/ppermute | solution.py:99
  63.4 6.1 shard_map.169
  69.5 28.5 %all-gather.4.cloned.1.call-done = bf16[2048,2048]{0,1:T(8,128)(2,1)} async-done(((bf16[256,2048]{0,1:T(8,128)(2,1)}), bf16[2048,2048]{0,1:T(8,128)(2,1)}) %all-gather.4.cloned.1.call-update) | async-done | bytes 8388624 | tf_op jit(solution)/shard_map/all_gather | solution.py:72
  98.0 11.7 %fusion.18.refs_1_.refs_2_.refs_3_ = f32[1024,1536]{1,0:T(8,128)} fusion(bf16[1024,2048]{1,0:T(8,128)(2,1)} %get-tuple-element.48, bf16[2048,2048]{0,1:T(8,128)(2,1)} %all-gather.4.cloned.1.call-done), kind=kOutput, calls=%fused_computation.29 | convolution fusion | flops 6442450944 | bytes 16777216 | tf_op jit(solution)/shard_map/dot_general | solution.py:56
  109.7 14.6 %shard_map.170 = (bf16[1024,512]{1,0:T(8,128)(2,1)}, bf16[1024,1536]{1,0:T(8,128)(2,1)}) custom-call(s32[1]{0:T(128)} %bitcast.2.refs_0_, f32[1024,1536]{1,0:T(8,128)} %fusion.18.refs_1_.refs_2_.refs_3_, f32[1024,1536]{1,0:T(8,128)} %fusion.18.refs_1_.refs_2_.refs_3_, f32[1024,1536]{1,0:T(8,128)} %fusion.18.refs_1_.refs_2_.refs_3_, ...), custom_call_target="tpu_custom_call" | custom-call | flops 2147483648 | bytes 10485760 | tf_op jit(solution)/shard_map/pallas_call | solution.py:289
  135.6 7.3 %collective-permute-done.7 = bf16[128,2048]{1,0:T(8,128)(2,1)S(1)} collective-permute-done((bf16[128,2048]{1,0:T(8,128)(2,1)S(1)}, bf16[128,2048]{1,0:T(8,128)(2,1)S(1)}, u32[]{:S(2)}, u32[]{:S(2)}) %collective-permute-start.7) | collective-permute-done | bytes 524320 | tf_op jit(solution)/shard_map/ppermute | solution.py:99
  150.3 7.9 %collective-permute-done.9 = bf16[128,2048]{1,0:T(8,128)(2,1)S(1)} collective-permute-done((bf16[128,2048]{1,0:T(8,128)(2,1)S(1)}, bf16[128,2048]{1,0:T(8,128)(2,1)S(1)}, u32[]{:S(2)}, u32[]{:S(2)}) %collective-permute-start.9) | collective-permute-done | bytes 524320 | tf_op jit(solution)/shard_map/ppermute | solution.py:99
  159.7 9.7 %collective-permute-done.8 = bf16[128,2048]{1,0:T(8,128)(2,1)S(1)} collective-permute-done((bf16[128,2048]{1,0:T(8,128)(2,1)S(1)}, bf16[128,2048]{1,0:T(8,128)(2,1)S(1)}, u32[]{:S(2)}, u32[]{:S(2)}) %collective-permute-start.8) | collective-permute-done | bytes 524320 | tf_op jit(solution)/shard_map/ppermute | solution.py:99
  173.0 14.9 %collective-permute-done.14.refs_1_ = bf16[256,2048]{1,0:T(8,128)(2,1)S(1)} collective-permute-done((bf16[256,2048]{1,0:T(8,128)(2,1)S(1)}, bf16[256,2048]{1,0:T(8,128)(2,1)S(1)}, u32[]{:S(2)}, u32[]{:S(2)}) %collective-permute-start.14) | collective-permute-done | bytes 1048608 | tf_op jit(solution)/shard_map/ppermute | solution.py:99
  192.5 17.8 %collective-permute-done.10.refs_1_ = bf16[256,2048]{1,0:T(8,128)(2,1)S(1)} collective-permute-done((bf16[256,2048]{1,0:T(8,128)(2,1)S(1)}, bf16[256,2048]{1,0:T(8,128)(2,1)S(1)}, u32[]{:S(2)}, u32[]{:S(2)}) %collective-permute-start.10) | collective-permute-done | bytes 1048608 | tf_op jit(solution)/shard_map/ppermute | solution.py:99
  215.8 9.8 %collective-permute-done.16.refs_3_ = bf16[128,2048]{1,0:T(8,128)(2,1)S(1)} collective-permute-done((bf16[128,2048]{1,0:T(8,128)(2,1)S(1)}, bf16[128,2048]{1,0:T(8,128)(2,1)S(1)}, u32[]{:S(2)}, u32[]{:S(2)}) %collective-permute-start.16) | collective-permute-done | bytes 524320 | tf_op jit(solution)/shard_map/ppermute | solution.py:99
  226.4 5.9 shard_map.172
  235.9 5.9 shard_map.171
  241.8 21.6 %shard_map.173 = (bf16[1024,1024]{1,0:T(8,128)(2,1)}, bf16[1024,2048]{1,0:T(8,128)(2,1)}) custom-call(bf16[1024,2048]{1,0:T(8,128)(2,1)} %get-tuple-element.53.h_ref, bf16[1024,2048]{1,0:T(8,128)(2,1)} %get-tuple-element.55.g_ref, bf16[2048,3072]{1,0:T(8,128)(2,1)} %all-gather.6.cloned.1.call-done.gate_ref.up_ref.down_ref, ...), custom_call_target="tpu_custom_call" | custom-call | flops 12884901888 | bytes 27262976 | tf_op jit(solution)/shard_map/pallas_call | solution.py:206
  263.5 7.7 %convolution_convert_fusion.2 = bf16[1024,2048]{1,0:T(8,128)(2,1)S(1)} fusion(bf16[1024,1024]{1,0:T(8,128)(2,1)} %get-tuple-element.60, bf16[1024,2048]{1,0:T(8,128)(2,1)} %get-tuple-element.59), kind=kOutput, calls=%fused_computation.20 | convolution fusion | flops 4297064448 | bytes 10485760 | tf_op jit(solution)/shard_map/dot_general | solution.py:60
  274.2 8.0 %collective-permute-done.19 = bf16[1024,1024]{1,0:T(8,128)(2,1)S(1)} collective-permute-done((bf16[1024,1024]{1,0:T(8,128)(2,1)S(1)}, bf16[1024,1024]{1,0:T(8,128)(2,1)S(1)}, u32[]{:S(2)}, u32[]{:S(2)}) %collective-permute-start.19) | collective-permute-done | bytes 2097184 | tf_op jit(solution)/shard_map/ppermute | solution.py:77
  293.5 14.6 %fusion = f32[1024,2048]{1,0:T(8,128)} fusion(bf16[1024,2048]{1,0:T(8,128)(2,1)} %get-tuple-element.59, bf16[2048,3072]{1,0:T(8,128)(2,1)} %all-gather.6.cloned.1.call-done.gate_ref.up_ref.down_ref), kind=kOutput, calls=%fused_computation | convolution fusion | flops 8589934592 | bytes 20971520 | tf_op jit(solution)/shard_map/dot_general | solution.py:64
  308.1 23.1 %all-gather.8.cloned.1.call-done.gate_ref.up_ref.down_ref = bf16[2048,3072]{1,0:T(8,128)(2,1)} async-done(((bf16[256,3072]{1,0:T(8,128)(2,1)}), bf16[2048,3072]{1,0:T(8,128)(2,1)}) %all-gather.8.cloned.1.call-update) | async-done | bytes 12582928 | tf_op jit(solution)/shard_map/all_gather | solution.py:72
  331.1 21.2 %shard_map.174 = (bf16[1024,1024]{1,0:T(8,128)(2,1)}, bf16[1024,2048]{1,0:T(8,128)(2,1)}) custom-call(bf16[1024,2048]{1,0:T(8,128)(2,1)} %get-tuple-element.53.h_ref, bf16[1024,2048]{1,0:T(8,128)(2,1)} %get-tuple-element.55.g_ref, bf16[2048,3072]{1,0:T(8,128)(2,1)} %all-gather.8.cloned.1.call-done.gate_ref.up_ref.down_ref, ...), custom_call_target="tpu_custom_call" | custom-call | flops 12884901888 | bytes 27262976 | tf_op jit(solution)/shard_map/pallas_call | solution.py:206
  355.6 6.6 %fusion.66 = bf16[256,2048]{1,0:T(8,128)(2,1)S(1)} fusion(bf16[2048,3072]{1,0:T(8,128)(2,1)} %all-gather.8.cloned.1.call-done.gate_ref.up_ref.down_ref, f32[1024,2048]{1,0:T(8,128)} %fusion, bf16[1024,2048]{1,0:T(8,128)(2,1)S(1)} %copy-done.20), kind=kOutput, calls=%fused_computation.60 | convolution fusion | flops 2148532224 | bytes 12582912 | tf_op jit(solution)/shard_map/dot_general | solution.py:64
  382.3 7.0 %convolution_convert_fusion.1 = bf16[1024,2048]{1,0:T(8,128)(2,1)S(1)} fusion(bf16[1024,1024]{1,0:T(8,128)(2,1)} %get-tuple-element.60, bf16[1024,2048]{1,0:T(8,128)(2,1)S(1)} %copy-done.20), kind=kOutput, calls=%fused_computation.19 | convolution fusion | flops 4297064448 | bytes 10485760 | tf_op jit(solution)/shard_map/dot_general | solution.py:60
  401.6 10.2 %collective-permute-done.24 = bf16[128,2048]{1,0:T(8,128)(2,1)S(1)} collective-permute-done((bf16[128,2048]{1,0:T(8,128)(2,1)S(1)}, bf16[128,2048]{1,0:T(8,128)(2,1)S(1)}, u32[]{:S(2)}, u32[]{:S(2)}) %collective-permute-start.24) | collective-permute-done | bytes 524320 | tf_op jit(solution)/shard_map/ppermute | solution.py:99
  429.4 12.9 %reduce-scatter.4.cloned.1.call-done = bf16[256,3072]{1,0:T(8,128)(2,1)} async-done(((bf16[1024,3072]{1,0:T(8,128)(2,1)}), bf16[256,3072]{1,0:T(8,128)(2,1)}) %reduce-scatter.4.cloned.1.call-update) | async-done | bytes 1572880 | tf_op jit(solution)/shard_map/reduce_scatter | solution.py:92
  454.3 6.3 collective-permute-done.28.refs_3_
  463.7 6.1 shard_map.175
  469.8 6.2 convolution_convert_fusion.9.refs_4_
  476.0 18.6 %shard_map.176 = bf16[1024,1536]{1,0:T(8,128)(2,1)} custom-call(s32[1]{0:T(128)} %bitcast.2.refs_0_, bf16[1024,1536]{1,0:T(8,128)(2,1)} %get-tuple-element.57.refs_1_.refs_2_.refs_3_, bf16[1024,1536]{1,0:T(8,128)(2,1)} %get-tuple-element.57.refs_1_.refs_2_.refs_3_, bf16[1024,1536]{1,0:T(8,128)(2,1)} %get-tuple-element.57.refs_1_.refs_2_.refs_3_, ...), custom_call_target="tpu_custom_call" | custom-call | flops 5368709120 | bytes 7340032 | tf_op jit(solution)/shard_map/pallas_call | solution.py:380
  544.2 13.0 %reduce-scatter.6.cloned.1.call-done = bf16[256,3072]{1,0:T(8,128)(2,1)} async-done(((bf16[1024,3072]{1,0:T(8,128)(2,1)}), bf16[256,3072]{1,0:T(8,128)(2,1)}) %reduce-scatter.6.cloned.1.call-update) | async-done | bytes 1572880 | tf_op jit(solution)/shard_map/reduce_scatter | solution.py:92
  580.1 8.7 %collective-permute-done.41 = bf16[128,2048]{1,0:T(8,128)(2,1)S(1)} collective-permute-done((bf16[128,2048]{1,0:T(8,128)(2,1)S(1)}, bf16[128,2048]{1,0:T(8,128)(2,1)S(1)}, u32[]{:S(2)}, u32[]{:S(2)}) %collective-permute-start.41) | collective-permute-done | bytes 524320 | tf_op jit(solution)/shard_map/ppermute | solution.py:99
  594.2 7.4 %collective-permute-done.43 = bf16[128,2048]{1,0:T(8,128)(2,1)S(1)} collective-permute-done((bf16[128,2048]{1,0:T(8,128)(2,1)S(1)}, bf16[128,2048]{1,0:T(8,128)(2,1)S(1)}, u32[]{:S(2)}, u32[]{:S(2)}) %collective-permute-start.43) | collective-permute-done | bytes 524320 | tf_op jit(solution)/shard_map/ppermute | solution.py:99
  601.6 9.8 %collective-permute-done.42 = bf16[128,2048]{1,0:T(8,128)(2,1)S(1)} collective-permute-done((bf16[128,2048]{1,0:T(8,128)(2,1)S(1)}, bf16[128,2048]{1,0:T(8,128)(2,1)S(1)}, u32[]{:S(2)}, u32[]{:S(2)}) %collective-permute-start.42) | collective-permute-done | bytes 524320 | tf_op jit(solution)/shard_map/ppermute | solution.py:99
  627.1 11.0 %reduce-scatter.8.cloned.1.call-done = bf16[256,2048]{1,0:T(8,128)(2,1)} async-done(((bf16[1024,2048]{1,0:T(8,128)(2,1)}), bf16[256,2048]{1,0:T(8,128)(2,1)}) %reduce-scatter.8.cloned.1.call-update) | async-done | bytes 1048592 | tf_op jit(solution)/shard_map/reduce_scatter | solution.py:92
  (328 shorter events, 253.2 us)
Async XLA Ops:
  7.2 90.8 %all-gather.4.cloned.1.call-start = ((), (), s32[]{:S(2)}) async-start(), calls=%async_computation.3 | async-start | bytes 9437184 | tf_op jit(solution)/shard_map/all_gather | solution.py:72
  12.6 229.2 %all-gather.6.cloned.1.call-start = ((), (), s32[]{:S(2)}) async-start(), calls=%async_computation.4 | async-start | bytes 14155776 | tf_op jit(solution)/shard_map/all_gather | solution.py:72
  16.0 315.2 %all-gather.8.cloned.1.call-start = ((), (), s32[]{:S(2)}) async-start(), calls=%async_computation.5 | async-start | bytes 14155776 | tf_op jit(solution)/shard_map/all_gather | solution.py:72
  17.5 424.8 %reduce-scatter.4.cloned.1.call-start = ((), (), s32[]{:S(2)}) async-start(), calls=%async_computation.6 | async-start | bytes 7864320 | tf_op jit(solution)/shard_map/reduce_scatter | solution.py:92
  19.7 26.2 %collective-permute-start = (bf16[256,2048]{1,0:T(8,128)(2,1)S(1)}, bf16[256,2048]{1,0:T(8,128)(2,1)S(1)}, u32[]{:S(2)}, u32[]{:S(2)}) collective-permute-start(bf16[256,2048]{1,0:T(8,128)(2,1)S(1)} %fusion.91.refs_0_), channel_id=1, source_target_pairs={{0,1},{1,0},{2,3},{3,2},{4,5},{5,4},{6,7},{7,6},{8,9},{9,8},{10,11... | collective-permute-start | bytes 3145736 | tf_op jit(solution)/shard_map/ppermute | solution.py:99
  22.7 25.8 %collective-permute-start.1 = (bf16[256,2048]{1,0:T(8,128)(2,1)S(1)}, bf16[256,2048]{1,0:T(8,128)(2,1)}, u32[]{:S(2)}, u32[]{:S(2)}) collective-permute-start(bf16[256,2048]{1,0:T(8,128)(2,1)S(1)} %fusion.91.refs_0_), channel_id=1, source_target_pairs={{0,2},{1,3},{2,0},{3,1},{4,6},{5,7},{6,4},{7,5},{8,10},{9,11},{10,... | collective-permute-start | bytes 3145736 | tf_op jit(solution)/shard_map/ppermute | solution.py:99
  134.5 23.7 %collective-permute-start.9 = (bf16[128,2048]{1,0:T(8,128)(2,1)S(1)}, bf16[128,2048]{1,0:T(8,128)(2,1)S(1)}, u32[]{:S(2)}, u32[]{:S(2)}) collective-permute-start(bf16[128,2048]{1,0:T(8,128)(2,1)S(1)} %slice.335), channel_id=1, source_target_pairs={{0,2},{1,3},{2,0},{3,1},{4,6},{5,7},{6,4},{7,5},{8,10},{9,11},{10,... | collective-permute-start | bytes 1572872 | tf_op jit(solution)/shard_map/ppermute | solution.py:99
  135.1 24.6 %collective-permute-start.4 = (bf16[128,2048]{1,0:T(8,128)(2,1)S(1)}, bf16[128,2048]{1,0:T(8,128)(2,1)S(1)}, u32[]{:S(2)}, u32[]{:S(2)}) collective-permute-start(bf16[128,2048]{1,0:T(8,128)(2,1)S(1)} %slice.330), channel_id=1, source_target_pairs={{0,1},{1,0},{2,3},{3,2},{4,5},{5,4},{6,7},{7,6},{8,9},{9,8},{10,11... | collective-permute-start | bytes 1572872 | tf_op jit(solution)/shard_map/ppermute | solution.py:99
  143.1 26.4 %collective-permute-start.8 = (bf16[128,2048]{1,0:T(8,128)(2,1)S(1)}, bf16[128,2048]{1,0:T(8,128)(2,1)S(1)}, u32[]{:S(2)}, u32[]{:S(2)}) collective-permute-start(bf16[128,2048]{1,0:T(8,128)(2,1)S(1)} %add_convert_fusion.12), channel_id=1, source_target_pairs={{0,2},{1,3},{2,0},{3,1},{4,6},{5,7},{6,4},{7,5},{8,10},{9,11},{10,... | collective-permute-start | bytes 1572872 | tf_op jit(solution)/shard_map/ppermute | solution.py:99
  147.1 22.3 %collective-permute-start.6 = (bf16[128,2048]{1,0:T(8,128)(2,1)S(1)}, bf16[128,2048]{1,0:T(8,128)(2,1)S(1)}, u32[]{:S(2)}, u32[]{:S(2)}) collective-permute-start(bf16[128,2048]{1,0:T(8,128)(2,1)S(1)} %add_convert_fusion.13), channel_id=1, source_target_pairs={{0,1},{1,0},{2,3},{3,2},{4,5},{5,4},{6,7},{7,6},{8,9},{9,8},{10,11... | collective-permute-start | bytes 1572872 | tf_op jit(solution)/shard_map/ppermute | solution.py:99
  147.9 40.0 %collective-permute-start.14 = (bf16[256,2048]{1,0:T(8,128)(2,1)S(1)}, bf16[256,2048]{1,0:T(8,128)(2,1)S(1)}, u32[]{:S(2)}, u32[]{:S(2)}) collective-permute-start(bf16[256,2048]{1,0:T(8,128)(2,1)S(1)} %fusion.98.refs_0_), channel_id=1, source_target_pairs={{0,1},{1,0},{2,3},{3,2},{4,5},{5,4},{6,7},{7,6},{8,9},{9,8},{10,11... | collective-permute-start | bytes 3145736 | tf_op jit(solution)/shard_map/ppermute | solution.py:99
  158.2 33.7 %collective-permute-start.15 = (bf16[256,2048]{1,0:T(8,128)(2,1)S(1)}, bf16[256,2048]{1,0:T(8,128)(2,1)S(1)}, u32[]{:S(2)}, u32[]{:S(2)}) collective-permute-start(bf16[256,2048]{1,0:T(8,128)(2,1)S(1)} %fusion.98.refs_0_), channel_id=1, source_target_pairs={{0,2},{1,3},{2,0},{3,1},{4,6},{5,7},{6,4},{7,5},{8,10},{9,11},{10,... | collective-permute-start | bytes 3145736 | tf_op jit(solution)/shard_map/ppermute | solution.py:99
  170.8 39.6 %collective-permute-start.10 = (bf16[256,2048]{1,0:T(8,128)(2,1)S(1)}, bf16[256,2048]{1,0:T(8,128)(2,1)S(1)}, u32[]{:S(2)}, u32[]{:S(2)}) collective-permute-start(bf16[256,2048]{1,0:T(8,128)(2,1)S(1)} %fusion.99.refs_0_), channel_id=1, source_target_pairs={{0,1},{1,0},{2,3},{3,2},{4,5},{5,4},{6,7},{7,6},{8,9},{9,8},{10,11... | collective-permute-start | bytes 3145736 | tf_op jit(solution)/shard_map/ppermute | solution.py:99
  171.3 43.0 %collective-permute-start.11 = (bf16[256,2048]{1,0:T(8,128)(2,1)S(1)}, bf16[256,2048]{1,0:T(8,128)(2,1)S(1)}, u32[]{:S(2)}, u32[]{:S(2)}) collective-permute-start(bf16[256,2048]{1,0:T(8,128)(2,1)S(1)} %fusion.99.refs_0_), channel_id=1, source_target_pairs={{0,2},{1,3},{2,0},{3,1},{4,6},{5,7},{6,4},{7,5},{8,10},{9,11},{10,... | collective-permute-start | bytes 3145736 | tf_op jit(solution)/shard_map/ppermute | solution.py:99
  187.9 37.7 %collective-permute-start.16 = (bf16[128,2048]{1,0:T(8,128)(2,1)S(1)}, bf16[128,2048]{1,0:T(8,128)(2,1)S(1)}, u32[]{:S(2)}, u32[]{:S(2)}) collective-permute-start(bf16[128,2048]{1,0:T(8,128)(2,1)S(1)} %slice.338), channel_id=1, source_target_pairs={{0,2},{1,3},{2,0},{3,1},{4,6},{5,7},{6,4},{7,5},{8,10},{9,11},{10,... | collective-permute-start | bytes 1572872 | tf_op jit(solution)/shard_map/ppermute | solution.py:99
  192.0 34.5 %collective-permute-start.17 = (bf16[128,2048]{1,0:T(8,128)(2,1)S(1)}, bf16[128,2048]{1,0:T(8,128)(2,1)}, u32[]{:S(2)}, u32[]{:S(2)}) collective-permute-start(bf16[128,2048]{1,0:T(8,128)(2,1)S(1)} %slice.339), channel_id=1, source_target_pairs={{0,1},{1,0},{2,3},{3,2},{4,5},{5,4},{6,7},{7,6},{8,9},{9,8},{10,11... | collective-permute-start | bytes 1572872 | tf_op jit(solution)/shard_map/ppermute | solution.py:99
  211.2 24.6 %collective-permute-start.12 = (bf16[128,2048]{1,0:T(8,128)(2,1)}, bf16[128,2048]{1,0:T(8,128)(2,1)}, u32[]{:S(2)}, u32[]{:S(2)}) collective-permute-start(bf16[128,2048]{1,0:T(8,128)(2,1)} %slice.336), channel_id=1, source_target_pairs={{0,2},{1,3},{2,0},{3,1},{4,6},{5,7},{6,4},{7,5},{8,10},{9,11},{10,... | collective-permute-start | bytes 1572872 | tf_op jit(solution)/shard_map/ppermute | solution.py:99
  293.4 263.8 %reduce-scatter.6.cloned.1.call-start = ((), (), s32[]{:S(2)}) async-start(), calls=%async_computation.7 | async-start | bytes 7864320 | tf_op jit(solution)/shard_map/reduce_scatter | solution.py:92
  372.9 27.1 %collective-permute-start.25 = (bf16[128,2048]{1,0:T(8,128)(2,1)}, bf16[128,2048]{1,0:T(8,128)(2,1)S(1)}, u32[]{:S(2)}, u32[]{:S(2)}) collective-permute-start(bf16[128,2048]{1,0:T(8,128)(2,1)} %slice.346), channel_id=1, source_target_pairs={{0,2},{1,3},{2,0},{3,1},{4,6},{5,7},{6,4},{7,5},{8,10},{9,11},{10,... | collective-permute-start | bytes 1572872 | tf_op jit(solution)/shard_map/ppermute | solution.py:99
  377.4 24.2 %collective-permute-start.20 = (bf16[128,2048]{1,0:T(8,128)(2,1)}, bf16[128,2048]{1,0:T(8,128)(2,1)S(1)}, u32[]{:S(2)}, u32[]{:S(2)}) collective-permute-start(bf16[128,2048]{1,0:T(8,128)(2,1)} %slice.341), channel_id=1, source_target_pairs={{0,1},{1,0},{2,3},{3,2},{4,5},{5,4},{6,7},{7,6},{8,9},{9,8},{10,11... | collective-permute-start | bytes 1572872 | tf_op jit(solution)/shard_map/ppermute | solution.py:99
  389.3 32.1 %collective-permute-start.44 = (bf16[1024,2048]{1,0:T(8,128)(2,1)S(1)}, bf16[1024,2048]{1,0:T(8,128)(2,1)S(1)}, u32[]{:S(2)}, u32[]{:S(2)}) collective-permute-start(bf16[1024,2048]{1,0:T(8,128)(2,1)S(1)} %convolution_convert_fusion.1), channel_id=1, source_target_pairs={{0,4},{4,0},{8,12},{12,8},{16,20},{20,16},{24,28},{28,24},{1,5},{5... | collective-permute-start | bytes 12582920 | tf_op jit(solution)/shard_map/ppermute | solution.py:77
  391.8 27.1 %collective-permute-start.45 = (bf16[1024,1024]{1,0:T(8,128)(2,1)S(1)}, bf16[1024,1024]{1,0:T(8,128)(2,1)S(1)}, u32[]{:S(2)}, u32[]{:S(2)}) collective-permute-start(bf16[1024,1024]{1,0:T(8,128)(2,1)S(1)} %convolution_convert_fusion.6), channel_id=1, source_target_pairs={{0,4},{4,0},{8,12},{12,8},{16,20},{20,16},{24,28},{28,24},{1,5},{5... | collective-permute-start | bytes 6291464 | tf_op jit(solution)/shard_map/ppermute | solution.py:77
  416.9 28.9 %collective-permute-start.26 = (bf16[256,2048]{1,0:T(8,128)(2,1)S(1)}, bf16[256,2048]{1,0:T(8,128)(2,1)}, u32[]{:S(2)}, u32[]{:S(2)}) collective-permute-start(bf16[256,2048]{1,0:T(8,128)(2,1)S(1)} %get-tuple-element.118.refs_0_), channel_id=1, source_target_pairs={{0,1},{1,0},{2,3},{3,2},{4,5},{5,4},{6,7},{7,6},{8,9},{9,8},{10,11... | collective-permute-start | bytes 3145736 | tf_op jit(solution)/shard_map/ppermute | solution.py:99
  418.4 27.4 %collective-permute-start.27 = (bf16[256,2048]{1,0:T(8,128)(2,1)S(1)}, bf16[256,2048]{1,0:T(8,128)(2,1)}, u32[]{:S(2)}, u32[]{:S(2)}) collective-permute-start(bf16[256,2048]{1,0:T(8,128)(2,1)S(1)} %get-tuple-element.118.refs_0_), channel_id=1, source_target_pairs={{0,2},{1,3},{2,0},{3,1},{4,6},{5,7},{6,4},{7,5},{8,10},{9,11},{10,... | collective-permute-start | bytes 3145736 | tf_op jit(solution)/shard_map/ppermute | solution.py:99
  445.8 192.4 %reduce-scatter.8.cloned.1.call-start = ((), (), s32[]{:S(2)}) async-start(), calls=%async_computation.8 | async-start | bytes 5242880 | tf_op jit(solution)/shard_map/reduce_scatter | solution.py:92
  529.4 33.5 %collective-permute-start.30 = (bf16[128,2048]{1,0:T(8,128)(2,1)}, bf16[128,2048]{1,0:T(8,128)(2,1)}, u32[]{:S(2)}, u32[]{:S(2)}) collective-permute-start(bf16[128,2048]{1,0:T(8,128)(2,1)} %slice.350), channel_id=1, source_target_pairs={{0,1},{1,0},{2,3},{3,2},{4,5},{5,4},{6,7},{7,6},{8,9},{9,8},{10,11... | collective-permute-start | bytes 1572872 | tf_op jit(solution)/shard_map/ppermute | solution.py:99
  531.8 31.1 %collective-permute-start.35 = (bf16[128,2048]{1,0:T(8,128)(2,1)}, bf16[128,2048]{1,0:T(8,128)(2,1)}, u32[]{:S(2)}, u32[]{:S(2)}) collective-permute-start(bf16[128,2048]{1,0:T(8,128)(2,1)} %slice.355), channel_id=1, source_target_pairs={{0,2},{1,3},{2,0},{3,1},{4,6},{5,7},{6,4},{7,5},{8,10},{9,11},{10,... | collective-permute-start | bytes 1572872 | tf_op jit(solution)/shard_map/ppermute | solution.py:99
  532.4 30.6 %collective-permute-start.32 = (bf16[128,2048]{1,0:T(8,128)(2,1)S(1)}, bf16[128,2048]{1,0:T(8,128)(2,1)}, u32[]{:S(2)}, u32[]{:S(2)}) collective-permute-start(bf16[128,2048]{1,0:T(8,128)(2,1)S(1)} %add_convert_fusion.9), channel_id=1, source_target_pairs={{0,1},{1,0},{2,3},{3,2},{4,5},{5,4},{6,7},{7,6},{8,9},{9,8},{10,11... | collective-permute-start | bytes 1572872 | tf_op jit(solution)/shard_map/ppermute | solution.py:99
  534.0 28.9 %collective-permute-start.34 = (bf16[128,2048]{1,0:T(8,128)(2,1)S(1)}, bf16[128,2048]{1,0:T(8,128)(2,1)}, u32[]{:S(2)}, u32[]{:S(2)}) collective-permute-start(bf16[128,2048]{1,0:T(8,128)(2,1)S(1)} %add_convert_fusion.8), channel_id=1, source_target_pairs={{0,2},{1,3},{2,0},{3,1},{4,6},{5,7},{6,4},{7,5},{8,10},{9,11},{10,... | collective-permute-start | bytes 1572872 | tf_op jit(solution)/shard_map/ppermute | solution.py:99
  579.1 22.6 %collective-permute-start.43 = (bf16[128,2048]{1,0:T(8,128)(2,1)S(1)}, bf16[128,2048]{1,0:T(8,128)(2,1)S(1)}, u32[]{:S(2)}, u32[]{:S(2)}) collective-permute-start(bf16[128,2048]{1,0:T(8,128)(2,1)S(1)} %slice.365), channel_id=1, source_target_pairs={{0,2},{1,3},{2,0},{3,1},{4,6},{5,7},{6,4},{7,5},{8,10},{9,11},{10,... | collective-permute-start | bytes 1572872 | tf_op jit(solution)/shard_map/ppermute | solution.py:99
  579.7 21.9 %collective-permute-start.38 = (bf16[128,2048]{1,0:T(8,128)(2,1)S(1)}, bf16[128,2048]{1,0:T(8,128)(2,1)S(1)}, u32[]{:S(2)}, u32[]{:S(2)}) collective-permute-start(bf16[128,2048]{1,0:T(8,128)(2,1)S(1)} %slice.360), channel_id=1, source_target_pairs={{0,1},{1,0},{2,3},{3,2},{4,5},{5,4},{6,7},{7,6},{8,9},{9,8},{10,11... | collective-permute-start | bytes 1572872 | tf_op jit(solution)/shard_map/ppermute | solution.py:99
  588.9 22.5 %collective-permute-start.42 = (bf16[128,2048]{1,0:T(8,128)(2,1)S(1)}, bf16[128,2048]{1,0:T(8,128)(2,1)S(1)}, u32[]{:S(2)}, u32[]{:S(2)}) collective-permute-start(bf16[128,2048]{1,0:T(8,128)(2,1)S(1)} %add_convert_fusion.6), channel_id=1, source_target_pairs={{0,2},{1,3},{2,0},{3,1},{4,6},{5,7},{6,4},{7,5},{8,10},{9,11},{10,... | collective-permute-start | bytes 1572872 | tf_op jit(solution)/shard_map/ppermute | solution.py:99
  (77 other events, 817.8 us)
Sparse Core Ops, SparseCore 0:
  12.7 85.1 all-gather.3
  99.6 114.9 all-gather.5
  216.2 114.8 all-gather.7
  333.3 108.9 reduce-scatter.3
  445.9 111.2 reduce-scatter.5
  560.8 77.2 reduce-scatter.7

commit v5 on v4

--- a/solution.py
+++ b/solution.py
@@ -89,10 +89,52 @@
 def scatter_dp(pairs):
     count = lax.axis_size("dp")
     groups = [list(range(core, count, 2)) for core in range(2)]
-    total = lax.psum_scatter(
+    return lax.psum_scatter(
         pairs, "dp", scatter_dimension=0, tiled=True, axis_index_groups=groups
     )
-    return total.astype(F32)
+
+
+def pack_kernel(q_ref, k_ref, v_ref, o_ref, out_ref):
+    width = q_ref.shape[1]
+    for n, ref in enumerate((q_ref, k_ref, v_ref)):
+        out_ref[:, n * width : (n + 1) * width] = ref[...]
+    out_ref[:, 3 * width :] = o_ref[...].astype(F32).T.astype(BF16)
+
+
+def pack_mixed(query, key, value, output):
+    rows, width = query.shape
+    tile = min(rows, 128)
+    plain = pl.BlockSpec((tile, width), lambda n: (n, 0))
+    return pl.pallas_call(
+        pack_kernel,
+        out_shape=jax.ShapeDtypeStruct((rows, 4 * width), BF16),
+        grid=(rows // tile,),
+        in_specs=[plain, plain, plain, pl.BlockSpec((width, tile), lambda n: (0, n))],
+        out_specs=pl.BlockSpec((tile, 4 * width), lambda n: (n, 0)),
+        cost_estimate=pl.CostEstimate(flops=0, bytes_accessed=16 * rows * width, transcendentals=0),
+    )(query, key, value, output)
+
+
+def split_kernel(in_ref, q_ref, k_ref, v_ref, o_ref):
+    width = q_ref.shape[1]
+    for n, ref in enumerate((q_ref, k_ref, v_ref)):
+        ref[...] = in_ref[:, n * width : (n + 1) * width].astype(F32)
+    o_ref[...] = in_ref[:, 3 * width :].astype(F32).T
+
+
+def split_mixed(total):
+    rows, width = total.shape[0], total.shape[1] // 4
+    tile = min(rows, 128)
+    plain = pl.BlockSpec((tile, width), lambda n: (n, 0))
+    return pl.pallas_call(
+        split_kernel,
+        out_shape=[jax.ShapeDtypeStruct((rows, width), F32)] * 3
+        + [jax.ShapeDtypeStruct((width, rows), F32)],
+        grid=(rows // tile,),
+        in_specs=[pl.BlockSpec((tile, 4 * width), lambda n: (n, 0))],
+        out_specs=[plain, plain, plain, pl.BlockSpec((width, tile), lambda n: (0, n))],
+        cost_estimate=pl.CostEstimate(flops=0, bytes_accessed=6 * total.size, transcendentals=0),
+    )(total)
 
 
 def flip(value, bits):
@@ -426,9 +468,11 @@
 
     half = hidden_width // 2
 
-    mixed = gather_dp(
-        jnp.concatenate([query_weight, key_weight, value_weight, output_weight.T], axis=1), 0
+    mixed_own = pack_mixed(query_weight, key_weight, value_weight, output_weight)
+    mixed_own, gate_weight, up_weight, down_weight = lax.optimization_barrier(
+        (mixed_own, gate_weight, up_weight, down_weight)
     )
+    mixed = gather_dp(mixed_own, 0)
     heads_full, out_full = mixed[:, : 3 * heads_width], mixed[:, 3 * heads_width :]
     wide = [
         gather_dp(
@@ -508,15 +552,12 @@
 
     d_normed_one = scatter_rows(heads_back_piece)
     input_grad = (d_middle + norm_backward(normed_one, inverse_one, d_normed_one)).astype(BF16)
-    wide_sum = [first_sum, second_sum]
+    wide_sum = [first_sum.astype(F32), second_sum.astype(F32)]
 
     return (
         output,
         input_grad,
-        mixed_sum[:, :heads_width],
-        mixed_sum[:, heads_width : 2 * heads_width],
-        mixed_sum[:, 2 * heads_width : 3 * heads_width],
-        mixed_sum[:, 3 * heads_width :].T,
+        *split_mixed(mixed_sum),
         jnp.concatenate([part[:, :half] for part in wide_sum], axis=1),
         jnp.concatenate([part[:, half : 2 * half] for part in wide_sum], axis=1),
         jnp.concatenate([part[:, 2 * half :].T for part in wide_sum], axis=0),

time: 655 us -> 648 us (0.989)
  other arithmetic: 44.1 us -> 34.3 us
  local copies, waits for them, and re-layouts: 45.3 us -> 37.4 us
    ppermute x40, waiting for transfers between devices: 158 us -> 168 us  [flip(): lax.ppermute(value, 'tensor', [(k, k ^ bits) for k in range(lax.axis_size...]
    convert_element_type x3 -> x2, other arithmetic: 8.45 us -> 0.7 us  [per_device(): wide_sum = [first_sum.astype(F32), second_sum.astype(F32)]]
    unnamed x121 -> x113, local copies, waits for them, and re-layouts: 15.2 us -> 10.5 us
  transfers between devices with their start and end apart: 52 -> 52, of which waited for: 28 -> 30; matrix products, arithmetic and copies ran while one was open for 32% -> 32% of each run, Pallas kernels for 15% -> 16%
where the time goes in v5:
time: 648 us; the launch traced here: 642 us
  waiting for transfers between devices  259 us (40%)
  matrix products  140 us (22%)
  Pallas kernels  105 us (16%)
  starting transfers between devices  51.3 us (8%)
  local copies, waits for them, and re-layouts  37.4 us (6%)
  other arithmetic  34.3 us (5%)
  between operations  15.7 us (2%)
    ppermute x40, waiting for transfers between devices, flip(): lax.ppermute(value, 'tensor', [(k, k ^ bits) for k in range(lax.axis_size...  168 us
    dot_general x21, matrix products, dot_last(): lax.dot_general(left, right, (((1,), (1,)), ((), ())), preferred_element_...  73.6 us
    all_gather x3, waiting for transfers between devices, gather_dp(): return lax.all_gather(own, 'dp', axis=axis, tiled=True)  51.7 us
    ppermute x40, starting transfers between devices, flip(): lax.ppermute(value, 'tensor', [(k, k ^ bits) for k in range(lax.axis_size...  49.8 us
    dot_general x12, matrix products, dot_first(): lax.dot_general(left, right, (((0,), (0,)), ((), ())), preferred_element_...  48.1 us
    pallas_call x2, Pallas kernels, feed(): pl.pallas_call(feed_kernel, out_shape=[jax.ShapeDtypeStruct((rows, width)...  42.8 us
    reduce_scatter x3, waiting for transfers between devices, scatter_dp(): lax.psum_scatter(pairs, 'dp', scatter_dimension=0, tiled=True, axis_index...  31.3 us
    pallas_call x4, Pallas kernels, join(): pl.pallas_call(join_kernel, out_shape=[jax.ShapeDtypeStruct((rows, width)...  24.1 us
  transfers between devices with their start and end apart: 52, of which 30 were waited for; matrix products, arithmetic and copies ran while one was open for 32% of the time, Pallas kernels for 16%

profile of v5, /device:TPU:0, one launch (start us, length us, event | category | flops | bytes accessed | tf_op | source)
XLA Modules:
  0.0 642.2 jit_solution(18260266918601729083)
XLA Ops:
  23.0 19.9 %collective-permute-done.refs_1_ = bf16[256,2048]{1,0:T(8,128)(2,1)S(1)} collective-permute-done((bf16[256,2048]{1,0:T(8,128)(2,1)S(1)}, bf16[256,2048]{1,0:T(8,128)(2,1)S(1)}, u32[]{:S(2)}, u32[]{:S(2)}) %collective-permute-start) | collective-permute-done | bytes 1048608 | tf_op jit(solution)/shard_map/ppermute | solution.py:141
  60.5 6.1 shard_map.169
  66.6 28.4 %all-gather.4.cloned.1.call-done = bf16[2048,2048]{1,0:T(8,128)(2,1)} async-done(((bf16[256,2048]{1,0:T(8,128)(2,1)}), bf16[2048,2048]{1,0:T(8,128)(2,1)}) %all-gather.4.cloned.1.call-update) | async-done | bytes 8388624 | tf_op jit(solution)/shard_map/all_gather | solution.py:72
  95.0 11.7 %fusion.18.refs_1_.refs_2_.refs_3_ = f32[1024,1536]{1,0:T(8,128)} fusion(bf16[1024,2048]{1,0:T(8,128)(2,1)} %get-tuple-element.56, bf16[2048,2048]{1,0:T(8,128)(2,1)} %all-gather.4.cloned.1.call-done), kind=kOutput, calls=%fused_computation.29 | convolution fusion | flops 6442450944 | bytes 16777216 | tf_op jit(solution)/shard_map/dot_general | solution.py:56
  106.7 14.6 %shard_map.171 = (bf16[1024,512]{1,0:T(8,128)(2,1)}, bf16[1024,1536]{1,0:T(8,128)(2,1)}) custom-call(s32[1]{0:T(128)} %bitcast.2.refs_0_, f32[1024,1536]{1,0:T(8,128)} %fusion.18.refs_1_.refs_2_.refs_3_, f32[1024,1536]{1,0:T(8,128)} %fusion.18.refs_1_.refs_2_.refs_3_, f32[1024,1536]{1,0:T(8,128)} %fusion.18.refs_1_.refs_2_.refs_3_, ...), custom_call_target="tpu_custom_call" | custom-call | flops 2147483648 | bytes 10485760 | tf_op jit(solution)/shard_map/pallas_call | solution.py:331
  132.7 7.3 %collective-permute-done.7 = bf16[128,2048]{1,0:T(8,128)(2,1)S(1)} collective-permute-done((bf16[128,2048]{1,0:T(8,128)(2,1)S(1)}, bf16[128,2048]{1,0:T(8,128)(2,1)S(1)}, u32[]{:S(2)}, u32[]{:S(2)}) %collective-permute-start.7) | collective-permute-done | bytes 524320 | tf_op jit(solution)/shard_map/ppermute | solution.py:141
  147.4 7.9 %collective-permute-done.9 = bf16[128,2048]{1,0:T(8,128)(2,1)S(1)} collective-permute-done((bf16[128,2048]{1,0:T(8,128)(2,1)S(1)}, bf16[128,2048]{1,0:T(8,128)(2,1)S(1)}, u32[]{:S(2)}, u32[]{:S(2)}) %collective-permute-start.9) | collective-permute-done | bytes 524320 | tf_op jit(solution)/shard_map/ppermute | solution.py:141
  156.8 9.7 %collective-permute-done.8 = bf16[128,2048]{1,0:T(8,128)(2,1)S(1)} collective-permute-done((bf16[128,2048]{1,0:T(8,128)(2,1)S(1)}, bf16[128,2048]{1,0:T(8,128)(2,1)S(1)}, u32[]{:S(2)}, u32[]{:S(2)}) %collective-permute-start.8) | collective-permute-done | bytes 524320 | tf_op jit(solution)/shard_map/ppermute | solution.py:141
  170.1 14.8 %collective-permute-done.14.refs_1_ = bf16[256,2048]{1,0:T(8,128)(2,1)S(1)} collective-permute-done((bf16[256,2048]{1,0:T(8,128)(2,1)S(1)}, bf16[256,2048]{1,0:T(8,128)(2,1)S(1)}, u32[]{:S(2)}, u32[]{:S(2)}) %collective-permute-start.14) | collective-permute-done | bytes 1048608 | tf_op jit(solution)/shard_map/ppermute | solution.py:141
  189.6 17.8 %collective-permute-done.10.refs_1_ = bf16[256,2048]{1,0:T(8,128)(2,1)S(1)} collective-permute-done((bf16[256,2048]{1,0:T(8,128)(2,1)S(1)}, bf16[256,2048]{1,0:T(8,128)(2,1)S(1)}, u32[]{:S(2)}, u32[]{:S(2)}) %collective-permute-start.10) | collective-permute-done | bytes 1048608 | tf_op jit(solution)/shard_map/ppermute | solution.py:141
  212.9 9.9 %collective-permute-done.16.refs_3_ = bf16[128,2048]{1,0:T(8,128)(2,1)S(1)} collective-permute-done((bf16[128,2048]{1,0:T(8,128)(2,1)S(1)}, bf16[128,2048]{1,0:T(8,128)(2,1)S(1)}, u32[]{:S(2)}, u32[]{:S(2)}) %collective-permute-start.16) | collective-permute-done | bytes 524320 | tf_op jit(solution)/shard_map/ppermute | solution.py:141
  223.6 5.9 shard_map.173
  233.1 6.0 shard_map.172
  239.0 21.6 %shard_map.174 = (bf16[1024,1024]{1,0:T(8,128)(2,1)}, bf16[1024,2048]{1,0:T(8,128)(2,1)}) custom-call(bf16[1024,2048]{1,0:T(8,128)(2,1)} %get-tuple-element.62.h_ref, bf16[1024,2048]{1,0:T(8,128)(2,1)} %get-tuple-element.64.g_ref, bf16[2048,3072]{1,0:T(8,128)(2,1)} %all-gather.6.cloned.1.call-done.gate_ref.up_ref.down_ref, ...), custom_call_target="tpu_custom_call" | custom-call | flops 12884901888 | bytes 27262976 | tf_op jit(solution)/shard_map/pallas_call | solution.py:248
  260.6 7.7 %convolution_convert_fusion.2 = bf16[1024,2048]{1,0:T(8,128)(2,1)S(1)} fusion(bf16[1024,1024]{1,0:T(8,128)(2,1)} %get-tuple-element.72, bf16[1024,2048]{1,0:T(8,128)(2,1)} %get-tuple-element.71), kind=kOutput, calls=%fused_computation.20 | convolution fusion | flops 4297064448 | bytes 10485760 | tf_op jit(solution)/shard_map/dot_general | solution.py:60
  271.4 8.0 %collective-permute-done.19 = bf16[1024,1024]{1,0:T(8,128)(2,1)S(1)} collective-permute-done((bf16[1024,1024]{1,0:T(8,128)(2,1)S(1)}, bf16[1024,1024]{1,0:T(8,128)(2,1)S(1)}, u32[]{:S(2)}, u32[]{:S(2)}) %collective-permute-start.19) | collective-permute-done | bytes 2097184 | tf_op jit(solution)/shard_map/ppermute | solution.py:77
  290.6 14.5 %fusion = f32[1024,2048]{1,0:T(8,128)} fusion(bf16[1024,2048]{1,0:T(8,128)(2,1)} %get-tuple-element.71, bf16[2048,3072]{1,0:T(8,128)(2,1)} %all-gather.6.cloned.1.call-done.gate_ref.up_ref.down_ref), kind=kOutput, calls=%fused_computation | convolution fusion | flops 8589934592 | bytes 20971520 | tf_op jit(solution)/shard_map/dot_general | solution.py:64
  305.1 23.3 %all-gather.8.cloned.1.call-done.gate_ref.up_ref.down_ref = bf16[2048,3072]{1,0:T(8,128)(2,1)} async-done(((bf16[256,3072]{1,0:T(8,128)(2,1)}), bf16[2048,3072]{1,0:T(8,128)(2,1)}) %all-gather.8.cloned.1.call-update) | async-done | bytes 12582928 | tf_op jit(solution)/shard_map/all_gather | solution.py:72
  328.4 21.2 %shard_map.175 = (bf16[1024,1024]{1,0:T(8,128)(2,1)}, bf16[1024,2048]{1,0:T(8,128)(2,1)}) custom-call(bf16[1024,2048]{1,0:T(8,128)(2,1)} %get-tuple-element.62.h_ref, bf16[1024,2048]{1,0:T(8,128)(2,1)} %get-tuple-element.64.g_ref, bf16[2048,3072]{1,0:T(8,128)(2,1)} %all-gather.8.cloned.1.call-done.gate_ref.up_ref.down_ref, ...), custom_call_target="tpu_custom_call" | custom-call | flops 12884901888 | bytes 27262976 | tf_op jit(solution)/shard_map/pallas_call | solution.py:248
  352.9 6.6 %fusion.66 = bf16[256,2048]{1,0:T(8,128)(2,1)S(1)} fusion(bf16[2048,3072]{1,0:T(8,128)(2,1)} %all-gather.8.cloned.1.call-done.gate_ref.up_ref.down_ref, f32[1024,2048]{1,0:T(8,128)} %fusion, bf16[1024,2048]{1,0:T(8,128)(2,1)S(1)} %copy-done.19), kind=kOutput, calls=%fused_computation.60 | convolution fusion | flops 2148532224 | bytes 12582912 | tf_op jit(solution)/shard_map/dot_general | solution.py:64
  380.0 7.1 %convolution_convert_fusion.1 = bf16[1024,2048]{1,0:T(8,128)(2,1)S(1)} fusion(bf16[1024,1024]{1,0:T(8,128)(2,1)} %get-tuple-element.72, bf16[1024,2048]{1,0:T(8,128)(2,1)S(1)} %copy-done.19), kind=kOutput, calls=%fused_computation.19 | convolution fusion | flops 4297064448 | bytes 10485760 | tf_op jit(solution)/shard_map/dot_general | solution.py:60
  399.1 10.2 %collective-permute-done.24 = bf16[128,2048]{1,0:T(8,128)(2,1)S(1)} collective-permute-done((bf16[128,2048]{1,0:T(8,128)(2,1)S(1)}, bf16[128,2048]{1,0:T(8,128)(2,1)S(1)}, u32[]{:S(2)}, u32[]{:S(2)}) %collective-permute-start.24) | collective-permute-done | bytes 524320 | tf_op jit(solution)/shard_map/ppermute | solution.py:141
  428.7 9.4 %collective-permute-done.26.refs_1_ = bf16[256,2048]{1,0:T(8,128)(2,1)} collective-permute-done((bf16[256,2048]{1,0:T(8,128)(2,1)S(1)}, bf16[256,2048]{1,0:T(8,128)(2,1)}, u32[]{:S(2)}, u32[]{:S(2)}) %collective-permute-start.26) | collective-permute-done | bytes 1048608 | tf_op jit(solution)/shard_map/ppermute | solution.py:141
  447.8 6.6 %collective-permute-done.28.refs_3_ = bf16[128,2048]{1,0:T(8,128)(2,1)S(1)} collective-permute-done((bf16[128,2048]{1,0:T(8,128)(2,1)S(1)}, bf16[128,2048]{1,0:T(8,128)(2,1)S(1)}, u32[]{:S(2)}, u32[]{:S(2)}) %collective-permute-start.28) | collective-permute-done | bytes 524320 | tf_op jit(solution)/shard_map/ppermute | solution.py:141
  457.5 6.1 shard_map.176
  463.6 6.2 convolution_convert_fusion.9.refs_4_
  469.8 18.4 %shard_map.177 = bf16[1024,1536]{1,0:T(8,128)(2,1)} custom-call(s32[1]{0:T(128)} %bitcast.2.refs_0_, bf16[1024,1536]{1,0:T(8,128)(2,1)} %get-tuple-element.69.refs_1_.refs_2_.refs_3_, bf16[1024,1536]{1,0:T(8,128)(2,1)} %get-tuple-element.69.refs_1_.refs_2_.refs_3_, bf16[1024,1536]{1,0:T(8,128)(2,1)} %get-tuple-element.69.refs_1_.refs_2_.refs_3_, ...), custom_call_target="tpu_custom_call" | custom-call | flops 5368709120 | bytes 7340032 | tf_op jit(solution)/shard_map/pallas_call | solution.py:422
  537.5 15.5 %reduce-scatter.6.cloned.1.call-done = bf16[256,3072]{1,0:T(8,128)(2,1)} async-done(((bf16[1024,3072]{1,0:T(8,128)(2,1)}), bf16[256,3072]{1,0:T(8,128)(2,1)}) %reduce-scatter.6.cloned.1.call-update) | async-done | bytes 1572880 | tf_op jit(solution)/shard_map/reduce_scatter | solution.py:92
  572.0 8.7 %collective-permute-done.41 = bf16[128,2048]{1,0:T(8,128)(2,1)S(1)} collective-permute-done((bf16[128,2048]{1,0:T(8,128)(2,1)S(1)}, bf16[128,2048]{1,0:T(8,128)(2,1)S(1)}, u32[]{:S(2)}, u32[]{:S(2)}) %collective-permute-start.41) | collective-permute-done | bytes 524320 | tf_op jit(solution)/shard_map/ppermute | solution.py:141
  585.7 7.5 %collective-permute-done.43 = bf16[128,2048]{1,0:T(8,128)(2,1)S(1)} collective-permute-done((bf16[128,2048]{1,0:T(8,128)(2,1)S(1)}, bf16[128,2048]{1,0:T(8,128)(2,1)S(1)}, u32[]{:S(2)}, u32[]{:S(2)}) %collective-permute-start.43) | collective-permute-done | bytes 524320 | tf_op jit(solution)/shard_map/ppermute | solution.py:141
  593.2 9.8 %collective-permute-done.42 = bf16[128,2048]{1,0:T(8,128)(2,1)S(1)} collective-permute-done((bf16[128,2048]{1,0:T(8,128)(2,1)S(1)}, bf16[128,2048]{1,0:T(8,128)(2,1)S(1)}, u32[]{:S(2)}, u32[]{:S(2)}) %collective-permute-start.42) | collective-permute-done | bytes 524320 | tf_op jit(solution)/shard_map/ppermute | solution.py:141
  617.0 15.5 %reduce-scatter.8.cloned.1.call-done.in_ref = bf16[256,2048]{1,0:T(8,128)(2,1)} async-done(((bf16[1024,2048]{1,0:T(8,128)(2,1)}), bf16[256,2048]{1,0:T(8,128)(2,1)}) %reduce-scatter.8.cloned.1.call-update) | async-done | bytes 1048592 | tf_op jit(solution)/shard_map/reduce_scatter | solution.py:92
  (319 shorter events, 242.7 us)
Async XLA Ops:
  7.2 87.8 %all-gather.4.cloned.1.call-start = ((), (), s32[]{:S(2)}) async-start(), calls=%async_computation.3 | async-start | bytes 9437184 | tf_op jit(solution)/shard_map/all_gather | solution.py:72
  9.5 229.5 %all-gather.6.cloned.1.call-start = ((), (), s32[]{:S(2)}) async-start(), calls=%async_computation.4 | async-start | bytes 14155776 | tf_op jit(solution)/shard_map/all_gather | solution.py:72
  13.3 315.1 %all-gather.8.cloned.1.call-start = ((), (), s32[]{:S(2)}) async-start(), calls=%async_computation.5 | async-start | bytes 14155776 | tf_op jit(solution)/shard_map/all_gather | solution.py:72
  14.7 424.9 %reduce-scatter.4.cloned.1.call-start = ((), (), s32[]{:S(2)}) async-start(), calls=%async_computation.6 | async-start | bytes 7864320 | tf_op jit(solution)/shard_map/reduce_scatter | solution.py:92
  16.8 26.2 %collective-permute-start = (bf16[256,2048]{1,0:T(8,128)(2,1)S(1)}, bf16[256,2048]{1,0:T(8,128)(2,1)S(1)}, u32[]{:S(2)}, u32[]{:S(2)}) collective-permute-start(bf16[256,2048]{1,0:T(8,128)(2,1)S(1)} %fusion.91.refs_0_), channel_id=1, source_target_pairs={{0,1},{1,0},{2,3},{3,2},{4,5},{5,4},{6,7},{7,6},{8,9},{9,8},{10,11... | collective-permute-start | bytes 3145736 | tf_op jit(solution)/shard_map/ppermute | solution.py:141
  19.8 25.8 %collective-permute-start.1 = (bf16[256,2048]{1,0:T(8,128)(2,1)S(1)}, bf16[256,2048]{1,0:T(8,128)(2,1)}, u32[]{:S(2)}, u32[]{:S(2)}) collective-permute-start(bf16[256,2048]{1,0:T(8,128)(2,1)S(1)} %fusion.91.refs_0_), channel_id=1, source_target_pairs={{0,2},{1,3},{2,0},{3,1},{4,6},{5,7},{6,4},{7,5},{8,10},{9,11},{10,... | collective-permute-start | bytes 3145736 | tf_op jit(solution)/shard_map/ppermute | solution.py:141
  131.6 23.7 %collective-permute-start.9 = (bf16[128,2048]{1,0:T(8,128)(2,1)S(1)}, bf16[128,2048]{1,0:T(8,128)(2,1)S(1)}, u32[]{:S(2)}, u32[]{:S(2)}) collective-permute-start(bf16[128,2048]{1,0:T(8,128)(2,1)S(1)} %slice.319), channel_id=1, source_target_pairs={{0,2},{1,3},{2,0},{3,1},{4,6},{5,7},{6,4},{7,5},{8,10},{9,11},{10,... | collective-permute-start | bytes 1572872 | tf_op jit(solution)/shard_map/ppermute | solution.py:141
  132.3 24.6 %collective-permute-start.4 = (bf16[128,2048]{1,0:T(8,128)(2,1)S(1)}, bf16[128,2048]{1,0:T(8,128)(2,1)S(1)}, u32[]{:S(2)}, u32[]{:S(2)}) collective-permute-start(bf16[128,2048]{1,0:T(8,128)(2,1)S(1)} %slice.314), channel_id=1, source_target_pairs={{0,1},{1,0},{2,3},{3,2},{4,5},{5,4},{6,7},{7,6},{8,9},{9,8},{10,11... | collective-permute-start | bytes 1572872 | tf_op jit(solution)/shard_map/ppermute | solution.py:141
  140.1 26.5 %collective-permute-start.8 = (bf16[128,2048]{1,0:T(8,128)(2,1)S(1)}, bf16[128,2048]{1,0:T(8,128)(2,1)S(1)}, u32[]{:S(2)}, u32[]{:S(2)}) collective-permute-start(bf16[128,2048]{1,0:T(8,128)(2,1)S(1)} %add_convert_fusion.12), channel_id=1, source_target_pairs={{0,2},{1,3},{2,0},{3,1},{4,6},{5,7},{6,4},{7,5},{8,10},{9,11},{10,... | collective-permute-start | bytes 1572872 | tf_op jit(solution)/shard_map/ppermute | solution.py:141
  144.2 22.3 %collective-permute-start.6 = (bf16[128,2048]{1,0:T(8,128)(2,1)S(1)}, bf16[128,2048]{1,0:T(8,128)(2,1)S(1)}, u32[]{:S(2)}, u32[]{:S(2)}) collective-permute-start(bf16[128,2048]{1,0:T(8,128)(2,1)S(1)} %add_convert_fusion.13), channel_id=1, source_target_pairs={{0,1},{1,0},{2,3},{3,2},{4,5},{5,4},{6,7},{7,6},{8,9},{9,8},{10,11... | collective-permute-start | bytes 1572872 | tf_op jit(solution)/shard_map/ppermute | solution.py:141
  145.0 39.9 %collective-permute-start.14 = (bf16[256,2048]{1,0:T(8,128)(2,1)S(1)}, bf16[256,2048]{1,0:T(8,128)(2,1)S(1)}, u32[]{:S(2)}, u32[]{:S(2)}) collective-permute-start(bf16[256,2048]{1,0:T(8,128)(2,1)S(1)} %fusion.98.refs_0_), channel_id=1, source_target_pairs={{0,1},{1,0},{2,3},{3,2},{4,5},{5,4},{6,7},{7,6},{8,9},{9,8},{10,11... | collective-permute-start | bytes 3145736 | tf_op jit(solution)/shard_map/ppermute | solution.py:141
  155.3 33.7 %collective-permute-start.15 = (bf16[256,2048]{1,0:T(8,128)(2,1)S(1)}, bf16[256,2048]{1,0:T(8,128)(2,1)S(1)}, u32[]{:S(2)}, u32[]{:S(2)}) collective-permute-start(bf16[256,2048]{1,0:T(8,128)(2,1)S(1)} %fusion.98.refs_0_), channel_id=1, source_target_pairs={{0,2},{1,3},{2,0},{3,1},{4,6},{5,7},{6,4},{7,5},{8,10},{9,11},{10,... | collective-permute-start | bytes 3145736 | tf_op jit(solution)/shard_map/ppermute | solution.py:141
  167.9 39.5 %collective-permute-start.10 = (bf16[256,2048]{1,0:T(8,128)(2,1)S(1)}, bf16[256,2048]{1,0:T(8,128)(2,1)S(1)}, u32[]{:S(2)}, u32[]{:S(2)}) collective-permute-start(bf16[256,2048]{1,0:T(8,128)(2,1)S(1)} %fusion.99.refs_0_), channel_id=1, source_target_pairs={{0,1},{1,0},{2,3},{3,2},{4,5},{5,4},{6,7},{7,6},{8,9},{9,8},{10,11... | collective-permute-start | bytes 3145736 | tf_op jit(solution)/shard_map/ppermute | solution.py:141
  168.4 43.1 %collective-permute-start.11 = (bf16[256,2048]{1,0:T(8,128)(2,1)S(1)}, bf16[256,2048]{1,0:T(8,128)(2,1)S(1)}, u32[]{:S(2)}, u32[]{:S(2)}) collective-permute-start(bf16[256,2048]{1,0:T(8,128)(2,1)S(1)} %fusion.99.refs_0_), channel_id=1, source_target_pairs={{0,2},{1,3},{2,0},{3,1},{4,6},{5,7},{6,4},{7,5},{8,10},{9,11},{10,... | collective-permute-start | bytes 3145736 | tf_op jit(solution)/shard_map/ppermute | solution.py:141
  185.0 37.8 %collective-permute-start.16 = (bf16[128,2048]{1,0:T(8,128)(2,1)S(1)}, bf16[128,2048]{1,0:T(8,128)(2,1)S(1)}, u32[]{:S(2)}, u32[]{:S(2)}) collective-permute-start(bf16[128,2048]{1,0:T(8,128)(2,1)S(1)} %slice.322), channel_id=1, source_target_pairs={{0,2},{1,3},{2,0},{3,1},{4,6},{5,7},{6,4},{7,5},{8,10},{9,11},{10,... | collective-permute-start | bytes 1572872 | tf_op jit(solution)/shard_map/ppermute | solution.py:141
  189.1 34.5 %collective-permute-start.17 = (bf16[128,2048]{1,0:T(8,128)(2,1)S(1)}, bf16[128,2048]{1,0:T(8,128)(2,1)}, u32[]{:S(2)}, u32[]{:S(2)}) collective-permute-start(bf16[128,2048]{1,0:T(8,128)(2,1)S(1)} %slice.323), channel_id=1, source_target_pairs={{0,1},{1,0},{2,3},{3,2},{4,5},{5,4},{6,7},{7,6},{8,9},{9,8},{10,11... | collective-permute-start | bytes 1572872 | tf_op jit(solution)/shard_map/ppermute | solution.py:141
  208.3 24.8 %collective-permute-start.12 = (bf16[128,2048]{1,0:T(8,128)(2,1)}, bf16[128,2048]{1,0:T(8,128)(2,1)}, u32[]{:S(2)}, u32[]{:S(2)}) collective-permute-start(bf16[128,2048]{1,0:T(8,128)(2,1)} %slice.320), channel_id=1, source_target_pairs={{0,2},{1,3},{2,0},{3,1},{4,6},{5,7},{6,4},{7,5},{8,10},{9,11},{10,... | collective-permute-start | bytes 1572872 | tf_op jit(solution)/shard_map/ppermute | solution.py:141
  290.6 262.4 %reduce-scatter.6.cloned.1.call-start = ((), (), s32[]{:S(2)}) async-start(), calls=%async_computation.7 | async-start | bytes 7864320 | tf_op jit(solution)/shard_map/reduce_scatter | solution.py:92
  370.4 27.1 %collective-permute-start.25 = (bf16[128,2048]{1,0:T(8,128)(2,1)}, bf16[128,2048]{1,0:T(8,128)(2,1)S(1)}, u32[]{:S(2)}, u32[]{:S(2)}) collective-permute-start(bf16[128,2048]{1,0:T(8,128)(2,1)} %slice.332), channel_id=1, source_target_pairs={{0,2},{1,3},{2,0},{3,1},{4,6},{5,7},{6,4},{7,5},{8,10},{9,11},{10,... | collective-permute-start | bytes 1572872 | tf_op jit(solution)/shard_map/ppermute | solution.py:141
  375.0 24.1 %collective-permute-start.20 = (bf16[128,2048]{1,0:T(8,128)(2,1)}, bf16[128,2048]{1,0:T(8,128)(2,1)S(1)}, u32[]{:S(2)}, u32[]{:S(2)}) collective-permute-start(bf16[128,2048]{1,0:T(8,128)(2,1)} %slice.327), channel_id=1, source_target_pairs={{0,1},{1,0},{2,3},{3,2},{4,5},{5,4},{6,7},{7,6},{8,9},{9,8},{10,11... | collective-permute-start | bytes 1572872 | tf_op jit(solution)/shard_map/ppermute | solution.py:141
  387.1 33.5 %collective-permute-start.44 = (bf16[1024,2048]{1,0:T(8,128)(2,1)S(1)}, bf16[1024,2048]{1,0:T(8,128)(2,1)S(1)}, u32[]{:S(2)}, u32[]{:S(2)}) collective-permute-start(bf16[1024,2048]{1,0:T(8,128)(2,1)S(1)} %convolution_convert_fusion.1), channel_id=1, source_target_pairs={{0,4},{4,0},{8,12},{12,8},{16,20},{20,16},{24,28},{28,24},{1,5},{5... | collective-permute-start | bytes 12582920 | tf_op jit(solution)/shard_map/ppermute | solution.py:77
  389.6 26.9 %collective-permute-start.45 = (bf16[1024,1024]{1,0:T(8,128)(2,1)S(1)}, bf16[1024,1024]{1,0:T(8,128)(2,1)}, u32[]{:S(2)}, u32[]{:S(2)}) collective-permute-start(bf16[1024,1024]{1,0:T(8,128)(2,1)S(1)} %convolution_convert_fusion.6), channel_id=1, source_target_pairs={{0,4},{4,0},{8,12},{12,8},{16,20},{20,16},{24,28},{28,24},{1,5},{5... | collective-permute-start | bytes 6291464 | tf_op jit(solution)/shard_map/ppermute | solution.py:77
  414.5 23.6 %collective-permute-start.26 = (bf16[256,2048]{1,0:T(8,128)(2,1)S(1)}, bf16[256,2048]{1,0:T(8,128)(2,1)}, u32[]{:S(2)}, u32[]{:S(2)}) collective-permute-start(bf16[256,2048]{1,0:T(8,128)(2,1)S(1)} %get-tuple-element.134.refs_0_), channel_id=1, source_target_pairs={{0,1},{1,0},{2,3},{3,2},{4,5},{5,4},{6,7},{7,6},{8,9},{9,8},{10,11... | collective-permute-start | bytes 3145736 | tf_op jit(solution)/shard_map/ppermute | solution.py:141
  416.0 23.4 %collective-permute-start.27 = (bf16[256,2048]{1,0:T(8,128)(2,1)S(1)}, bf16[256,2048]{1,0:T(8,128)(2,1)}, u32[]{:S(2)}, u32[]{:S(2)}) collective-permute-start(bf16[256,2048]{1,0:T(8,128)(2,1)S(1)} %get-tuple-element.134.refs_0_), channel_id=1, source_target_pairs={{0,2},{1,3},{2,0},{3,1},{4,6},{5,7},{6,4},{7,5},{8,10},{9,11},{10,... | collective-permute-start | bytes 3145736 | tf_op jit(solution)/shard_map/ppermute | solution.py:141
  439.6 192.9 %reduce-scatter.8.cloned.1.call-start = ((), (), s32[]{:S(2)}) async-start(), calls=%async_computation.8 | async-start | bytes 5242880 | tf_op jit(solution)/shard_map/reduce_scatter | solution.py:92
  523.2 32.0 %collective-permute-start.30 = (bf16[128,2048]{1,0:T(8,128)(2,1)}, bf16[128,2048]{1,0:T(8,128)(2,1)}, u32[]{:S(2)}, u32[]{:S(2)}) collective-permute-start(bf16[128,2048]{1,0:T(8,128)(2,1)} %slice.336), channel_id=1, source_target_pairs={{0,1},{1,0},{2,3},{3,2},{4,5},{5,4},{6,7},{7,6},{8,9},{9,8},{10,11... | collective-permute-start | bytes 1572872 | tf_op jit(solution)/shard_map/ppermute | solution.py:141
  525.1 30.1 %collective-permute-start.35 = (bf16[128,2048]{1,0:T(8,128)(2,1)}, bf16[128,2048]{1,0:T(8,128)(2,1)}, u32[]{:S(2)}, u32[]{:S(2)}) collective-permute-start(bf16[128,2048]{1,0:T(8,128)(2,1)} %slice.341), channel_id=1, source_target_pairs={{0,2},{1,3},{2,0},{3,1},{4,6},{5,7},{6,4},{7,5},{8,10},{9,11},{10,... | collective-permute-start | bytes 1572872 | tf_op jit(solution)/shard_map/ppermute | solution.py:141
  526.0 29.2 %collective-permute-start.32 = (bf16[128,2048]{1,0:T(8,128)(2,1)S(1)}, bf16[128,2048]{1,0:T(8,128)(2,1)}, u32[]{:S(2)}, u32[]{:S(2)}) collective-permute-start(bf16[128,2048]{1,0:T(8,128)(2,1)S(1)} %add_convert_fusion.9), channel_id=1, source_target_pairs={{0,1},{1,0},{2,3},{3,2},{4,5},{5,4},{6,7},{7,6},{8,9},{9,8},{10,11... | collective-permute-start | bytes 1572872 | tf_op jit(solution)/shard_map/ppermute | solution.py:141
  527.7 27.6 %collective-permute-start.34 = (bf16[128,2048]{1,0:T(8,128)(2,1)S(1)}, bf16[128,2048]{1,0:T(8,128)(2,1)}, u32[]{:S(2)}, u32[]{:S(2)}) collective-permute-start(bf16[128,2048]{1,0:T(8,128)(2,1)S(1)} %add_convert_fusion.8), channel_id=1, source_target_pairs={{0,2},{1,3},{2,0},{3,1},{4,6},{5,7},{6,4},{7,5},{8,10},{9,11},{10,... | collective-permute-start | bytes 1572872 | tf_op jit(solution)/shard_map/ppermute | solution.py:141
  570.6 22.6 %collective-permute-start.43 = (bf16[128,2048]{1,0:T(8,128)(2,1)S(1)}, bf16[128,2048]{1,0:T(8,128)(2,1)S(1)}, u32[]{:S(2)}, u32[]{:S(2)}) collective-permute-start(bf16[128,2048]{1,0:T(8,128)(2,1)S(1)} %slice.351), channel_id=1, source_target_pairs={{0,2},{1,3},{2,0},{3,1},{4,6},{5,7},{6,4},{7,5},{8,10},{9,11},{10,... | collective-permute-start | bytes 1572872 | tf_op jit(solution)/shard_map/ppermute | solution.py:141
  571.2 21.9 %collective-permute-start.38 = (bf16[128,2048]{1,0:T(8,128)(2,1)S(1)}, bf16[128,2048]{1,0:T(8,128)(2,1)S(1)}, u32[]{:S(2)}, u32[]{:S(2)}) collective-permute-start(bf16[128,2048]{1,0:T(8,128)(2,1)S(1)} %slice.346), channel_id=1, source_target_pairs={{0,1},{1,0},{2,3},{3,2},{4,5},{5,4},{6,7},{7,6},{8,9},{9,8},{10,11... | collective-permute-start | bytes 1572872 | tf_op jit(solution)/shard_map/ppermute | solution.py:141
  580.8 22.1 %collective-permute-start.42 = (bf16[128,2048]{1,0:T(8,128)(2,1)S(1)}, bf16[128,2048]{1,0:T(8,128)(2,1)S(1)}, u32[]{:S(2)}, u32[]{:S(2)}) collective-permute-start(bf16[128,2048]{1,0:T(8,128)(2,1)S(1)} %add_convert_fusion.6), channel_id=1, source_target_pairs={{0,2},{1,3},{2,0},{3,1},{4,6},{5,7},{6,4},{7,5},{8,10},{9,11},{10,... | collective-permute-start | bytes 1572872 | tf_op jit(solution)/shard_map/ppermute | solution.py:141
  (76 other events, 821.7 us)
Sparse Core Ops, SparseCore 0:
  10.2 84.7 all-gather.3
  96.6 115.1 all-gather.5
  213.5 114.8 all-gather.7
  330.6 108.9 reduce-scatter.3
  441.7 111.2 reduce-scatter.5
  555.2 77.2 reduce-scatter.7

commit v6 on v5

--- a/solution.py
+++ b/solution.py
@@ -552,7 +552,7 @@
 
     d_normed_one = scatter_rows(heads_back_piece)
     input_grad = (d_middle + norm_backward(normed_one, inverse_one, d_normed_one)).astype(BF16)
-    wide_sum = [first_sum.astype(F32), second_sum.astype(F32)]
+    wide_sum = [after(first_sum, d_pre).astype(F32), after(second_sum, feed_out).astype(F32)]
 
     return (
         output,

time: 648 us -> 648 us (level)
  waiting for transfers between devices: 259 us -> 267 us
  local copies, waits for them, and re-layouts: 37.4 us -> 30.2 us
    ppermute x40, waiting for transfers between devices: 168 us -> 178 us  [flip(): lax.ppermute(value, 'tensor', [(k, k ^ bits) for k in range(lax.axis_size...]
  transfers between devices with their start and end apart: 52 -> 52, of which waited for: 30 -> 30; matrix products, arithmetic and copies ran while one was open for 32% -> 31% of each run, Pallas kernels for 16% -> 16%
where the time goes in v6:
time: 648 us; the launch traced here: 642 us
  waiting for transfers between devices  267 us (41%)
  matrix products  139 us (21%)
  Pallas kernels  105 us (16%)
  starting transfers between devices  49.1 us (8%)
  other arithmetic  36.1 us (6%)
  local copies, waits for them, and re-layouts  30.2 us (5%)
  between operations  15.8 us (2%)
    ppermute x40, waiting for transfers between devices, flip(): lax.ppermute(value, 'tensor', [(k, k ^ bits) for k in range(lax.axis_size...  178 us
    dot_general x21, matrix products, dot_last(): lax.dot_general(left, right, (((1,), (1,)), ((), ())), preferred_element_...  73.7 us
    all_gather x3, waiting for transfers between devices, gather_dp(): return lax.all_gather(own, 'dp', axis=axis, tiled=True)  49.9 us
    ppermute x40, starting transfers between devices, flip(): lax.ppermute(value, 'tensor', [(k, k ^ bits) for k in range(lax.axis_size...  48.1 us
    dot_general x12, matrix products, dot_first(): lax.dot_general(left, right, (((0,), (0,)), ((), ())), preferred_element_...  47.1 us
    pallas_call x2, Pallas kernels, feed(): pl.pallas_call(feed_kernel, out_shape=[jax.ShapeDtypeStruct((rows, width)...  43 us
    reduce_scatter x3, waiting for transfers between devices, scatter_dp(): lax.psum_scatter(pairs, 'dp', scatter_dimension=0, tiled=True, axis_index...  32 us
    pallas_call x4, Pallas kernels, join(): pl.pallas_call(join_kernel, out_shape=[jax.ShapeDtypeStruct((rows, width)...  24.2 us
  transfers between devices with their start and end apart: 52, of which 30 were waited for; matrix products, arithmetic and copies ran while one was open for 31% of the time, Pallas kernels for 16%

profile of v6, /device:TPU:0, one launch (start us, length us, event | category | flops | bytes accessed | tf_op | source)
XLA Modules:
  0.0 642.2 jit_solution(10386411985373103077)
XLA Ops:
  22.8 20.0 %collective-permute-done.1.refs_2_ = bf16[256,2048]{1,0:T(8,128)(2,1)S(1)} collective-permute-done((bf16[256,2048]{1,0:T(8,128)(2,1)S(1)}, bf16[256,2048]{1,0:T(8,128)(2,1)S(1)}, u32[]{:S(2)}, u32[]{:S(2)}) %collective-permute-start.1) | collective-permute-done | bytes 1048608 | tf_op jit(solution)/shard_map/ppermute | solution.py:141
  60.2 6.2 shard_map.169
  66.4 28.6 %all-gather.4.cloned.1.call-done = bf16[2048,2048]{1,0:T(8,128)(2,1)} async-done(((bf16[256,2048]{1,0:T(8,128)(2,1)}), bf16[2048,2048]{1,0:T(8,128)(2,1)}) %all-gather.4.cloned.1.call-update) | async-done | bytes 8388624 | tf_op jit(solution)/shard_map/all_gather | solution.py:72
  95.0 11.7 %fusion.18.refs_1_.refs_2_.refs_3_ = f32[1024,1536]{1,0:T(8,128)} fusion(bf16[1024,2048]{1,0:T(8,128)(2,1)} %get-tuple-element.58, bf16[2048,2048]{1,0:T(8,128)(2,1)} %all-gather.4.cloned.1.call-done), kind=kOutput, calls=%fused_computation.29 | convolution fusion | flops 6442450944 | bytes 16777216 | tf_op jit(solution)/shard_map/dot_general | solution.py:56
  106.7 14.6 %shard_map.171 = (bf16[1024,512]{1,0:T(8,128)(2,1)}, bf16[1024,1536]{1,0:T(8,128)(2,1)}) custom-call(s32[1]{0:T(128)} %bitcast.2.refs_0_, f32[1024,1536]{1,0:T(8,128)} %fusion.18.refs_1_.refs_2_.refs_3_, f32[1024,1536]{1,0:T(8,128)} %fusion.18.refs_1_.refs_2_.refs_3_, f32[1024,1536]{1,0:T(8,128)} %fusion.18.refs_1_.refs_2_.refs_3_, ...), custom_call_target="tpu_custom_call" | custom-call | flops 2147483648 | bytes 10485760 | tf_op jit(solution)/shard_map/pallas_call | solution.py:331
  132.7 7.3 %collective-permute-done.5 = bf16[128,2048]{1,0:T(8,128)(2,1)S(1)} collective-permute-done((bf16[128,2048]{1,0:T(8,128)(2,1)S(1)}, bf16[128,2048]{1,0:T(8,128)(2,1)S(1)}, u32[]{:S(2)}, u32[]{:S(2)}) %collective-permute-start.5) | collective-permute-done | bytes 524320 | tf_op jit(solution)/shard_map/ppermute | solution.py:141
  141.9 13.5 %collective-permute-done.7 = bf16[128,2048]{1,0:T(8,128)(2,1)S(1)} collective-permute-done((bf16[128,2048]{1,0:T(8,128)(2,1)S(1)}, bf16[128,2048]{1,0:T(8,128)(2,1)S(1)}, u32[]{:S(2)}, u32[]{:S(2)}) %collective-permute-start.7) | collective-permute-done | bytes 524320 | tf_op jit(solution)/shard_map/ppermute | solution.py:141
  160.2 6.4 collective-permute-done.6
  173.9 19.0 %collective-permute-done.15.refs_2_ = bf16[256,2048]{1,0:T(8,128)(2,1)S(1)} collective-permute-done((bf16[256,2048]{1,0:T(8,128)(2,1)S(1)}, bf16[256,2048]{1,0:T(8,128)(2,1)S(1)}, u32[]{:S(2)}, u32[]{:S(2)}) %collective-permute-start.15) | collective-permute-done | bytes 1048608 | tf_op jit(solution)/shard_map/ppermute | solution.py:141
  195.2 20.1 %collective-permute-done.11.refs_2_ = bf16[256,2048]{1,0:T(8,128)(2,1)S(1)} collective-permute-done((bf16[256,2048]{1,0:T(8,128)(2,1)S(1)}, bf16[256,2048]{1,0:T(8,128)(2,1)S(1)}, u32[]{:S(2)}, u32[]{:S(2)}) %collective-permute-start.11) | collective-permute-done | bytes 1048608 | tf_op jit(solution)/shard_map/ppermute | solution.py:141
  226.6 6.0 shard_map.173
  235.1 6.0 shard_map.172
  241.0 21.8 %shard_map.174 = (bf16[1024,1024]{1,0:T(8,128)(2,1)}, bf16[1024,2048]{1,0:T(8,128)(2,1)}) custom-call(bf16[1024,2048]{1,0:T(8,128)(2,1)} %get-tuple-element.64.h_ref, bf16[1024,2048]{1,0:T(8,128)(2,1)} %get-tuple-element.66.g_ref, bf16[2048,3072]{1,0:T(8,128)(2,1)} %all-gather.6.cloned.1.call-done.gate_ref.up_ref.down_ref, ...), custom_call_target="tpu_custom_call" | custom-call | flops 12884901888 | bytes 27262976 | tf_op jit(solution)/shard_map/pallas_call | solution.py:248
  262.8 7.6 %convolution_convert_fusion.2 = bf16[1024,2048]{1,0:T(8,128)(2,1)S(1)} fusion(bf16[1024,1024]{1,0:T(8,128)(2,1)} %get-tuple-element.74, bf16[1024,2048]{1,0:T(8,128)(2,1)} %get-tuple-element.73), kind=kOutput, calls=%fused_computation.20 | convolution fusion | flops 4297064448 | bytes 10485760 | tf_op jit(solution)/shard_map/dot_general | solution.py:60
  273.5 7.7 %collective-permute-done.19 = bf16[1024,1024]{1,0:T(8,128)(2,1)S(1)} collective-permute-done((bf16[1024,1024]{1,0:T(8,128)(2,1)S(1)}, bf16[1024,1024]{1,0:T(8,128)(2,1)S(1)}, u32[]{:S(2)}, u32[]{:S(2)}) %collective-permute-start.19) | collective-permute-done | bytes 2097184 | tf_op jit(solution)/shard_map/ppermute | solution.py:77
  292.4 14.7 %fusion = f32[1024,2048]{1,0:T(8,128)} fusion(bf16[1024,2048]{1,0:T(8,128)(2,1)} %get-tuple-element.73, bf16[2048,3072]{1,0:T(8,128)(2,1)} %all-gather.6.cloned.1.call-done.gate_ref.up_ref.down_ref), kind=kOutput, calls=%fused_computation | convolution fusion | flops 8589934592 | bytes 20971520 | tf_op jit(solution)/shard_map/dot_general | solution.py:64
  307.1 21.3 %all-gather.8.cloned.1.call-done.gate_ref.up_ref.down_ref = bf16[2048,3072]{1,0:T(8,128)(2,1)} async-done(((bf16[256,3072]{1,0:T(8,128)(2,1)}), bf16[2048,3072]{1,0:T(8,128)(2,1)}) %all-gather.8.cloned.1.call-update) | async-done | bytes 12582928 | tf_op jit(solution)/shard_map/all_gather | solution.py:72
  328.4 21.2 %shard_map.175 = (bf16[1024,1024]{1,0:T(8,128)(2,1)}, bf16[1024,2048]{1,0:T(8,128)(2,1)}) custom-call(bf16[1024,2048]{1,0:T(8,128)(2,1)} %get-tuple-element.64.h_ref, bf16[1024,2048]{1,0:T(8,128)(2,1)} %get-tuple-element.66.g_ref, bf16[2048,3072]{1,0:T(8,128)(2,1)} %all-gather.8.cloned.1.call-done.gate_ref.up_ref.down_ref, ...), custom_call_target="tpu_custom_call" | custom-call | flops 12884901888 | bytes 27262976 | tf_op jit(solution)/shard_map/pallas_call | solution.py:248
  349.6 6.8 %fusion.66 = bf16[256,2048]{1,0:T(8,128)(2,1)S(1)} fusion(bf16[2048,3072]{1,0:T(8,128)(2,1)} %all-gather.8.cloned.1.call-done.gate_ref.up_ref.down_ref, f32[1024,2048]{1,0:T(8,128)} %fusion, bf16[1024,2048]{1,0:T(8,128)(2,1)} %get-tuple-element.98), kind=kOutput, calls=%fused_computation.60 | convolution fusion | flops 2148532224 | bytes 12582912 | tf_op jit(solution)/shard_map/dot_general | solution.py:64
  373.0 7.1 %convolution_convert_fusion.1 = bf16[1024,2048]{1,0:T(8,128)(2,1)S(1)} fusion(bf16[1024,1024]{1,0:T(8,128)(2,1)} %get-tuple-element.74, bf16[1024,2048]{1,0:T(8,128)(2,1)S(1)} %copy-done.19), kind=kOutput, calls=%fused_computation.19 | convolution fusion | flops 4297064448 | bytes 10485760 | tf_op jit(solution)/shard_map/dot_general | solution.py:60
  385.8 11.3 %collective-permute-done.20 = bf16[128,2048]{1,0:T(8,128)(2,1)S(1)} collective-permute-done((bf16[128,2048]{1,0:T(8,128)(2,1)S(1)}, bf16[128,2048]{1,0:T(8,128)(2,1)S(1)}, u32[]{:S(2)}, u32[]{:S(2)}) %collective-permute-start.20) | collective-permute-done | bytes 524320 | tf_op jit(solution)/shard_map/ppermute | solution.py:141
  398.2 10.5 %collective-permute-done.24 = bf16[128,2048]{1,0:T(8,128)(2,1)S(1)} collective-permute-done((bf16[128,2048]{1,0:T(8,128)(2,1)S(1)}, bf16[128,2048]{1,0:T(8,128)(2,1)S(1)}, u32[]{:S(2)}, u32[]{:S(2)}) %collective-permute-start.24) | collective-permute-done | bytes 524320 | tf_op jit(solution)/shard_map/ppermute | solution.py:141
  426.6 12.1 %collective-permute-done.27.refs_2_ = bf16[256,2048]{1,0:T(8,128)(2,1)} collective-permute-done((bf16[256,2048]{1,0:T(8,128)(2,1)S(1)}, bf16[256,2048]{1,0:T(8,128)(2,1)}, u32[]{:S(2)}, u32[]{:S(2)}) %collective-permute-start.27) | collective-permute-done | bytes 1048608 | tf_op jit(solution)/shard_map/ppermute | solution.py:141
  447.8 6.6 %collective-permute-done.29.refs_4_ = bf16[128,2048]{1,0:T(8,128)(2,1)S(1)} collective-permute-done((bf16[128,2048]{1,0:T(8,128)(2,1)S(1)}, bf16[128,2048]{1,0:T(8,128)(2,1)S(1)}, u32[]{:S(2)}, u32[]{:S(2)}) %collective-permute-start.29) | collective-permute-done | bytes 524320 | tf_op jit(solution)/shard_map/ppermute | solution.py:141
  457.6 6.1 shard_map.176
  463.7 6.2 convolution_convert_fusion.9.refs_4_
  469.8 18.5 %shard_map.177 = bf16[1024,1536]{1,0:T(8,128)(2,1)} custom-call(s32[1]{0:T(128)} %bitcast.2.refs_0_, bf16[1024,1536]{1,0:T(8,128)(2,1)} %get-tuple-element.71.refs_1_.refs_2_.refs_3_, bf16[1024,1536]{1,0:T(8,128)(2,1)} %get-tuple-element.71.refs_1_.refs_2_.refs_3_, bf16[1024,1536]{1,0:T(8,128)(2,1)} %get-tuple-element.71.refs_1_.refs_2_.refs_3_, ...), custom_call_target="tpu_custom_call" | custom-call | flops 5368709120 | bytes 7340032 | tf_op jit(solution)/shard_map/pallas_call | solution.py:422
  537.0 16.0 %reduce-scatter.6.cloned.1.call-done = bf16[256,3072]{1,0:T(8,128)(2,1)} async-done(((bf16[1024,3072]{1,0:T(8,128)(2,1)}), bf16[256,3072]{1,0:T(8,128)(2,1)}) %reduce-scatter.6.cloned.1.call-update) | async-done | bytes 1572880 | tf_op jit(solution)/shard_map/reduce_scatter | solution.py:92
  572.2 8.7 %collective-permute-done.39 = bf16[128,2048]{1,0:T(8,128)(2,1)S(1)} collective-permute-done((bf16[128,2048]{1,0:T(8,128)(2,1)S(1)}, bf16[128,2048]{1,0:T(8,128)(2,1)S(1)}, u32[]{:S(2)}, u32[]{:S(2)}) %collective-permute-start.39) | collective-permute-done | bytes 524320 | tf_op jit(solution)/shard_map/ppermute | solution.py:141
  585.9 7.4 %collective-permute-done.38 = bf16[128,2048]{1,0:T(8,128)(2,1)S(1)} collective-permute-done((bf16[128,2048]{1,0:T(8,128)(2,1)S(1)}, bf16[128,2048]{1,0:T(8,128)(2,1)S(1)}, u32[]{:S(2)}, u32[]{:S(2)}) %collective-permute-start.38) | collective-permute-done | bytes 524320 | tf_op jit(solution)/shard_map/ppermute | solution.py:141
  593.3 9.8 %collective-permute-done.40 = bf16[128,2048]{1,0:T(8,128)(2,1)S(1)} collective-permute-done((bf16[128,2048]{1,0:T(8,128)(2,1)S(1)}, bf16[128,2048]{1,0:T(8,128)(2,1)S(1)}, u32[]{:S(2)}, u32[]{:S(2)}) %collective-permute-start.40) | collective-permute-done | bytes 524320 | tf_op jit(solution)/shard_map/ppermute | solution.py:141
  617.2 15.3 %reduce-scatter.8.cloned.1.call-done.in_ref = bf16[256,2048]{1,0:T(8,128)(2,1)} async-done(((bf16[1024,2048]{1,0:T(8,128)(2,1)}), bf16[256,2048]{1,0:T(8,128)(2,1)}) %reduce-scatter.8.cloned.1.call-update) | async-done | bytes 1048592 | tf_op jit(solution)/shard_map/reduce_scatter | solution.py:92
  (321 shorter events, 230.6 us)
Async XLA Ops:
  7.2 87.8 %all-gather.4.cloned.1.call-start = ((), (), s32[]{:S(2)}) async-start(), calls=%async_computation.3 | async-start | bytes 9437184 | tf_op jit(solution)/shard_map/all_gather | solution.py:72
  9.5 231.5 %all-gather.6.cloned.1.call-start = ((), (), s32[]{:S(2)}) async-start(), calls=%async_computation.4 | async-start | bytes 14155776 | tf_op jit(solution)/shard_map/all_gather | solution.py:72
  13.1 315.3 %all-gather.8.cloned.1.call-start = ((), (), s32[]{:S(2)}) async-start(), calls=%async_computation.5 | async-start | bytes 14155776 | tf_op jit(solution)/shard_map/all_gather | solution.py:72
  14.4 425.1 %reduce-scatter.4.cloned.1.call-start = ((), (), s32[]{:S(2)}) async-start(), calls=%async_computation.6 | async-start | bytes 7864320 | tf_op jit(solution)/shard_map/reduce_scatter | solution.py:92
  16.6 26.2 %collective-permute-start.1 = (bf16[256,2048]{1,0:T(8,128)(2,1)S(1)}, bf16[256,2048]{1,0:T(8,128)(2,1)S(1)}, u32[]{:S(2)}, u32[]{:S(2)}) collective-permute-start(bf16[256,2048]{1,0:T(8,128)(2,1)S(1)} %fusion.91.refs_0_), channel_id=1, source_target_pairs={{0,2},{1,3},{2,0},{3,1},{4,6},{5,7},{6,4},{7,5},{8,10},{9,11},{10,... | collective-permute-start | bytes 3145736 | tf_op jit(solution)/shard_map/ppermute | solution.py:141
  19.6 25.8 %collective-permute-start = (bf16[256,2048]{1,0:T(8,128)(2,1)S(1)}, bf16[256,2048]{1,0:T(8,128)(2,1)}, u32[]{:S(2)}, u32[]{:S(2)}) collective-permute-start(bf16[256,2048]{1,0:T(8,128)(2,1)S(1)} %fusion.91.refs_0_), channel_id=1, source_target_pairs={{0,1},{1,0},{2,3},{3,2},{4,5},{5,4},{6,7},{7,6},{8,9},{9,8},{10,11... | collective-permute-start | bytes 3145736 | tf_op jit(solution)/shard_map/ppermute | solution.py:141
  129.3 29.4 %collective-permute-start.4 = (bf16[128,2048]{1,0:T(8,128)(2,1)S(1)}, bf16[128,2048]{1,0:T(8,128)(2,1)S(1)}, u32[]{:S(2)}, u32[]{:S(2)}) collective-permute-start(bf16[128,2048]{1,0:T(8,128)(2,1)S(1)} %slice.314), channel_id=1, source_target_pairs={{0,1},{1,0},{2,3},{3,2},{4,5},{5,4},{6,7},{7,6},{8,9},{9,8},{10,11... | collective-permute-start | bytes 1572872 | tf_op jit(solution)/shard_map/ppermute | solution.py:141
  130.8 24.6 %collective-permute-start.7 = (bf16[128,2048]{1,0:T(8,128)(2,1)S(1)}, bf16[128,2048]{1,0:T(8,128)(2,1)S(1)}, u32[]{:S(2)}, u32[]{:S(2)}) collective-permute-start(bf16[128,2048]{1,0:T(8,128)(2,1)S(1)} %get-tuple-element.172), channel_id=1, source_target_pairs={{0,1},{1,0},{2,3},{3,2},{4,5},{5,4},{6,7},{7,6},{8,9},{9,8},{10,11... | collective-permute-start | bytes 1572872 | tf_op jit(solution)/shard_map/ppermute | solution.py:141
  132.2 28.0 %collective-permute-start.9 = (bf16[128,2048]{1,0:T(8,128)(2,1)S(1)}, bf16[128,2048]{1,0:T(8,128)(2,1)S(1)}, u32[]{:S(2)}, u32[]{:S(2)}) collective-permute-start(bf16[128,2048]{1,0:T(8,128)(2,1)S(1)} %slice.319), channel_id=1, source_target_pairs={{0,2},{1,3},{2,0},{3,1},{4,6},{5,7},{6,4},{7,5},{8,10},{9,11},{10,... | collective-permute-start | bytes 1572872 | tf_op jit(solution)/shard_map/ppermute | solution.py:141
  140.1 26.5 %collective-permute-start.6 = (bf16[128,2048]{1,0:T(8,128)(2,1)S(1)}, bf16[128,2048]{1,0:T(8,128)(2,1)S(1)}, u32[]{:S(2)}, u32[]{:S(2)}) collective-permute-start(bf16[128,2048]{1,0:T(8,128)(2,1)S(1)} %add_convert_fusion.13), channel_id=1, source_target_pairs={{0,1},{1,0},{2,3},{3,2},{4,5},{5,4},{6,7},{7,6},{8,9},{9,8},{10,11... | collective-permute-start | bytes 1572872 | tf_op jit(solution)/shard_map/ppermute | solution.py:141
  156.3 36.6 %collective-permute-start.15 = (bf16[256,2048]{1,0:T(8,128)(2,1)S(1)}, bf16[256,2048]{1,0:T(8,128)(2,1)S(1)}, u32[]{:S(2)}, u32[]{:S(2)}) collective-permute-start(bf16[256,2048]{1,0:T(8,128)(2,1)S(1)} %fusion.98.refs_0_), channel_id=1, source_target_pairs={{0,2},{1,3},{2,0},{3,1},{4,6},{5,7},{6,4},{7,5},{8,10},{9,11},{10,... | collective-permute-start | bytes 3145736 | tf_op jit(solution)/shard_map/ppermute | solution.py:141
  158.7 35.7 %collective-permute-start.14 = (bf16[256,2048]{1,0:T(8,128)(2,1)S(1)}, bf16[256,2048]{1,0:T(8,128)(2,1)S(1)}, u32[]{:S(2)}, u32[]{:S(2)}) collective-permute-start(bf16[256,2048]{1,0:T(8,128)(2,1)S(1)} %fusion.98.refs_0_), channel_id=1, source_target_pairs={{0,1},{1,0},{2,3},{3,2},{4,5},{5,4},{6,7},{7,6},{8,9},{9,8},{10,11... | collective-permute-start | bytes 3145736 | tf_op jit(solution)/shard_map/ppermute | solution.py:141
  171.7 43.6 %collective-permute-start.11 = (bf16[256,2048]{1,0:T(8,128)(2,1)S(1)}, bf16[256,2048]{1,0:T(8,128)(2,1)S(1)}, u32[]{:S(2)}, u32[]{:S(2)}) collective-permute-start(bf16[256,2048]{1,0:T(8,128)(2,1)S(1)} %fusion.99.refs_0_), channel_id=1, source_target_pairs={{0,2},{1,3},{2,0},{3,1},{4,6},{5,7},{6,4},{7,5},{8,10},{9,11},{10,... | collective-permute-start | bytes 3145736 | tf_op jit(solution)/shard_map/ppermute | solution.py:141
  172.2 45.4 %collective-permute-start.10 = (bf16[256,2048]{1,0:T(8,128)(2,1)S(1)}, bf16[256,2048]{1,0:T(8,128)(2,1)S(1)}, u32[]{:S(2)}, u32[]{:S(2)}) collective-permute-start(bf16[256,2048]{1,0:T(8,128)(2,1)S(1)} %fusion.99.refs_0_), channel_id=1, source_target_pairs={{0,1},{1,0},{2,3},{3,2},{4,5},{5,4},{6,7},{7,6},{8,9},{9,8},{10,11... | collective-permute-start | bytes 3145736 | tf_op jit(solution)/shard_map/ppermute | solution.py:141
  192.9 29.9 %collective-permute-start.17 = (bf16[128,2048]{1,0:T(8,128)(2,1)S(1)}, bf16[128,2048]{1,0:T(8,128)(2,1)S(1)}, u32[]{:S(2)}, u32[]{:S(2)}) collective-permute-start(bf16[128,2048]{1,0:T(8,128)(2,1)S(1)} %slice.323), channel_id=1, source_target_pairs={{0,1},{1,0},{2,3},{3,2},{4,5},{5,4},{6,7},{7,6},{8,9},{9,8},{10,11... | collective-permute-start | bytes 1572872 | tf_op jit(solution)/shard_map/ppermute | solution.py:141
  194.5 32.2 %collective-permute-start.16 = (bf16[128,2048]{1,0:T(8,128)(2,1)S(1)}, bf16[128,2048]{1,0:T(8,128)(2,1)}, u32[]{:S(2)}, u32[]{:S(2)}) collective-permute-start(bf16[128,2048]{1,0:T(8,128)(2,1)S(1)} %slice.322), channel_id=1, source_target_pairs={{0,2},{1,3},{2,0},{3,1},{4,6},{5,7},{6,4},{7,5},{8,10},{9,11},{10,... | collective-permute-start | bytes 1572872 | tf_op jit(solution)/shard_map/ppermute | solution.py:141
  292.4 260.7 %reduce-scatter.6.cloned.1.call-start = ((), (), s32[]{:S(2)}) async-start(), calls=%async_computation.7 | async-start | bytes 7864320 | tf_op jit(solution)/shard_map/reduce_scatter | solution.py:92
  357.5 27.0 %collective-permute-start.21 = (bf16[128,2048]{1,0:T(8,128)(2,1)}, bf16[128,2048]{1,0:T(8,128)(2,1)S(1)}, u32[]{:S(2)}, u32[]{:S(2)}) collective-permute-start(bf16[128,2048]{1,0:T(8,128)(2,1)} %get-tuple-element.163), channel_id=1, source_target_pairs={{0,2},{1,3},{2,0},{3,1},{4,6},{5,7},{6,4},{7,5},{8,10},{9,11},{10,... | collective-permute-start | bytes 1572872 | tf_op jit(solution)/shard_map/ppermute | solution.py:141
  359.0 25.4 %collective-permute-start.23 = (bf16[128,2048]{1,0:T(8,128)(2,1)}, bf16[128,2048]{1,0:T(8,128)(2,1)S(1)}, u32[]{:S(2)}, u32[]{:S(2)}) collective-permute-start(bf16[128,2048]{1,0:T(8,128)(2,1)} %get-tuple-element.164), channel_id=1, source_target_pairs={{0,1},{1,0},{2,3},{3,2},{4,5},{5,4},{6,7},{7,6},{8,9},{9,8},{10,11... | collective-permute-start | bytes 1572872 | tf_op jit(solution)/shard_map/ppermute | solution.py:141
  380.1 38.3 %collective-permute-start.44 = (bf16[1024,2048]{1,0:T(8,128)(2,1)S(1)}, bf16[1024,2048]{1,0:T(8,128)(2,1)S(1)}, u32[]{:S(2)}, u32[]{:S(2)}) collective-permute-start(bf16[1024,2048]{1,0:T(8,128)(2,1)S(1)} %convolution_convert_fusion.1), channel_id=1, source_target_pairs={{0,4},{4,0},{8,12},{12,8},{16,20},{20,16},{24,28},{28,24},{1,5},{5... | collective-permute-start | bytes 12582920 | tf_op jit(solution)/shard_map/ppermute | solution.py:77
  384.4 31.5 %collective-permute-start.45 = (bf16[1024,1024]{1,0:T(8,128)(2,1)S(1)}, bf16[1024,1024]{1,0:T(8,128)(2,1)S(1)}, u32[]{:S(2)}, u32[]{:S(2)}) collective-permute-start(bf16[1024,1024]{1,0:T(8,128)(2,1)S(1)} %convolution_convert_fusion.6), channel_id=1, source_target_pairs={{0,4},{4,0},{8,12},{12,8},{16,20},{20,16},{24,28},{28,24},{1,5},{5... | collective-permute-start | bytes 6291464 | tf_op jit(solution)/shard_map/ppermute | solution.py:77
  384.6 24.1 %collective-permute-start.24 = (bf16[128,2048]{1,0:T(8,128)(2,1)S(1)}, bf16[128,2048]{1,0:T(8,128)(2,1)S(1)}, u32[]{:S(2)}, u32[]{:S(2)}) collective-permute-start(bf16[128,2048]{1,0:T(8,128)(2,1)S(1)} %add_convert_fusion.10), channel_id=1, source_target_pairs={{0,2},{1,3},{2,0},{3,1},{4,6},{5,7},{6,4},{7,5},{8,10},{9,11},{10,... | collective-permute-start | bytes 1572872 | tf_op jit(solution)/shard_map/ppermute | solution.py:141
  414.5 24.1 %collective-permute-start.27 = (bf16[256,2048]{1,0:T(8,128)(2,1)S(1)}, bf16[256,2048]{1,0:T(8,128)(2,1)}, u32[]{:S(2)}, u32[]{:S(2)}) collective-permute-start(bf16[256,2048]{1,0:T(8,128)(2,1)S(1)} %get-tuple-element.140.refs_0_), channel_id=1, source_target_pairs={{0,2},{1,3},{2,0},{3,1},{4,6},{5,7},{6,4},{7,5},{8,10},{9,11},{10,... | collective-permute-start | bytes 3145736 | tf_op jit(solution)/shard_map/ppermute | solution.py:141
  415.1 23.9 %collective-permute-start.26 = (bf16[256,2048]{1,0:T(8,128)(2,1)S(1)}, bf16[256,2048]{1,0:T(8,128)(2,1)}, u32[]{:S(2)}, u32[]{:S(2)}) collective-permute-start(bf16[256,2048]{1,0:T(8,128)(2,1)S(1)} %get-tuple-element.140.refs_0_), channel_id=1, source_target_pairs={{0,1},{1,0},{2,3},{3,2},{4,5},{5,4},{6,7},{7,6},{8,9},{9,8},{10,11... | collective-permute-start | bytes 3145736 | tf_op jit(solution)/shard_map/ppermute | solution.py:141
  439.6 192.9 %reduce-scatter.8.cloned.1.call-start = ((), (), s32[]{:S(2)}) async-start(), calls=%async_computation.8 | async-start | bytes 5242880 | tf_op jit(solution)/shard_map/reduce_scatter | solution.py:92
  491.3 36.2 %collective-permute-start.37 = (bf16[1024,512]{1,0:T(8,128)(2,1)S(1)}, bf16[1024,512]{1,0:T(8,128)(2,1)S(1)}, u32[]{:S(2)}, u32[]{:S(2)}) collective-permute-start(bf16[1024,512]{1,0:T(8,128)(2,1)S(1)} %convolution_convert_fusion.8), channel_id=1, source_target_pairs={{0,4},{4,0},{8,12},{12,8},{16,20},{20,16},{24,28},{28,24},{1,5},{5... | collective-permute-start | bytes 3145736 | tf_op jit(solution)/shard_map/ppermute | solution.py:77
  498.8 25.2 %collective-permute-start.31 = (bf16[128,2048]{1,0:T(8,128)(2,1)S(1)}, bf16[128,2048]{1,0:T(8,128)(2,1)S(1)}, u32[]{:S(2)}, u32[]{:S(2)}) collective-permute-start(bf16[128,2048]{1,0:T(8,128)(2,1)S(1)} %get-tuple-element.161), channel_id=1, source_target_pairs={{0,2},{1,3},{2,0},{3,1},{4,6},{5,7},{6,4},{7,5},{8,10},{9,11},{10,... | collective-permute-start | bytes 1572872 | tf_op jit(solution)/shard_map/ppermute | solution.py:141
  500.4 25.1 %collective-permute-start.33 = (bf16[128,2048]{1,0:T(8,128)(2,1)S(1)}, bf16[128,2048]{1,0:T(8,128)(2,1)S(1)}, u32[]{:S(2)}, u32[]{:S(2)}) collective-permute-start(bf16[128,2048]{1,0:T(8,128)(2,1)S(1)} %get-tuple-element.162), channel_id=1, source_target_pairs={{0,1},{1,0},{2,3},{3,2},{4,5},{5,4},{6,7},{7,6},{8,9},{9,8},{10,11... | collective-permute-start | bytes 1572872 | tf_op jit(solution)/shard_map/ppermute | solution.py:141
  506.7 48.5 %collective-permute-start.30 = (bf16[128,2048]{1,0:T(8,128)(2,1)}, bf16[128,2048]{1,0:T(8,128)(2,1)}, u32[]{:S(2)}, u32[]{:S(2)}) collective-permute-start(bf16[128,2048]{1,0:T(8,128)(2,1)} %slice.336), channel_id=1, source_target_pairs={{0,1},{1,0},{2,3},{3,2},{4,5},{5,4},{6,7},{7,6},{8,9},{9,8},{10,11... | collective-permute-start | bytes 1572872 | tf_op jit(solution)/shard_map/ppermute | solution.py:141
  524.0 31.3 %collective-permute-start.35 = (bf16[128,2048]{1,0:T(8,128)(2,1)}, bf16[128,2048]{1,0:T(8,128)(2,1)}, u32[]{:S(2)}, u32[]{:S(2)}) collective-permute-start(bf16[128,2048]{1,0:T(8,128)(2,1)} %slice.341), channel_id=1, source_target_pairs={{0,2},{1,3},{2,0},{3,1},{4,6},{5,7},{6,4},{7,5},{8,10},{9,11},{10,... | collective-permute-start | bytes 1572872 | tf_op jit(solution)/shard_map/ppermute | solution.py:141
  525.5 29.8 %collective-permute-start.32 = (bf16[128,2048]{1,0:T(8,128)(2,1)}, bf16[128,2048]{1,0:T(8,128)(2,1)}, u32[]{:S(2)}, u32[]{:S(2)}) collective-permute-start(bf16[128,2048]{1,0:T(8,128)(2,1)} %add_convert_fusion.9), channel_id=1, source_target_pairs={{0,1},{1,0},{2,3},{3,2},{4,5},{5,4},{6,7},{7,6},{8,9},{9,8},{10,11... | collective-permute-start | bytes 1572872 | tf_op jit(solution)/shard_map/ppermute | solution.py:141
  527.4 27.9 %collective-permute-start.34 = (bf16[128,2048]{1,0:T(8,128)(2,1)}, bf16[128,2048]{1,0:T(8,128)(2,1)}, u32[]{:S(2)}, u32[]{:S(2)}) collective-permute-start(bf16[128,2048]{1,0:T(8,128)(2,1)} %add_convert_fusion.8), channel_id=1, source_target_pairs={{0,2},{1,3},{2,0},{3,1},{4,6},{5,7},{6,4},{7,5},{8,10},{9,11},{10,... | collective-permute-start | bytes 1572872 | tf_op jit(solution)/shard_map/ppermute | solution.py:141
  (77 other events, 844.7 us)
Sparse Core Ops, SparseCore 0:
  10.2 84.7 all-gather.3
  96.6 115.1 all-gather.5
  213.5 114.8 all-gather.7
  330.6 108.9 reduce-scatter.3
  441.7 111.2 reduce-scatter.5
  555.2 77.2 reduce-scatter.7

commit v7 on v5

--- a/solution.py
+++ b/solution.py
@@ -220,7 +220,7 @@
     two_low = flip(two[half:], 2)
     one_low = flip((one[half:].astype(F32) + low.astype(F32)).astype(BF16), 1)
     two_top = flip((two[:half].astype(F32) + top.astype(F32)).astype(BF16), 2)
-    own = lax.optimization_barrier(piece(0, two))
+    own = lax.optimization_barrier(piece(0, two)).astype(F32)
     ones = jnp.concatenate([one_top, one_low], axis=0).astype(F32)
     twos = jnp.concatenate([two_top, two_low], axis=0).astype(F32)
     return own + ones + twos
@@ -502,11 +502,10 @@
 
     context, saved = attend_forward(t_arg, dot_plain(h1, heads_full), segc, segr, cos, sin)
 
-    def attention_piece(j, earlier):
-        rows = rows_of(context, j)
-        return dot_last(rows if earlier is None else after(rows, earlier), out_full)
-
-    middle = residual + scatter_rows(attention_piece)
+    def whole(value):
+        return lambda j, earlier: rows_of(value, j)
+
+    middle = residual + scatter_rows(whole(dot_last(context, out_full).astype(BF16)))
     normed_two, inverse_two = norm_forward(middle)
     h2, h2_own, h2_peer = gather_rows(normed_two.astype(BF16))
 
@@ -537,20 +536,14 @@
     mixed_grad = pair_sum([(h1_own, h1_peer, d_pre), (d_attention_own, d_attention_peer, context)])
     mixed_sum = scatter_dp(after(mixed_grad, second_sum))
 
-    def feed_piece(j, earlier):
-        rows = after(rows_of(hidden_0, j), d_pre if earlier is None else earlier)
-        return dot_last(rows, wide[0][:, 2 * half :]) + dot_last(
-            rows_of(hidden_1, j), wide_1[:, 2 * half :]
-        )
-
-    feed_out = scatter_rows(feed_piece)
+    fed = dot_last(after(hidden_0, d_pre), wide[0][:, 2 * half :]) + dot_last(
+        hidden_1, wide_1[:, 2 * half :]
+    )
+    feed_out = scatter_rows(whole(fed.astype(BF16)))
     output = (valid * (middle + feed_out)).astype(BF16)
 
-    def heads_back_piece(j, earlier):
-        rows = after(rows_of(d_pre, j), mixed_grad if earlier is None else earlier)
-        return dot_last(rows, heads_full)
-
-    d_normed_one = scatter_rows(heads_back_piece)
+    headed = dot_last(after(d_pre, mixed_grad), heads_full).astype(BF16)
+    d_normed_one = scatter_rows(whole(headed))
     input_grad = (d_middle + norm_backward(normed_one, inverse_one, d_normed_one)).astype(BF16)
     wide_sum = [first_sum.astype(F32), second_sum.astype(F32)]
 

time: 648 us -> 670 us (1.034)
  waiting for transfers between devices: 259 us -> 297 us
  local copies, waits for them, and re-layouts: 37.4 us -> 27.3 us
    ppermute x40, waiting for transfers between devices: 168 us -> 203 us  [flip(): lax.ppermute(value, 'tensor', [(k, k ^ bits) for k in range(lax.axis_size...]
    slice x4 -> x6, local copies, waits for them, and re-layouts: 9.58 us -> 2.31 us  [rows_of(): return value[j * local:(j + 1) * local]]
    dot_general x21 -> x9, matrix products: 73.6 us -> 71.2 us  [dot_last(): lax.dot_general(left, right, (((1,), (1,)), ((), ())), preferred_element_...]
  transfers between devices with their start and end apart: 52 -> 52, of which waited for: 30 -> 30; matrix products, arithmetic and copies ran while one was open for 32% -> 28% of each run, Pallas kernels for 16% -> 15%
where the time goes in v7:
time: 670 us; the launch traced here: 664 us
  waiting for transfers between devices  297 us (44%)
  matrix products  136 us (20%)
  Pallas kernels  105 us (16%)
  starting transfers between devices  49.3 us (7%)
  other arithmetic  34.6 us (5%)
  local copies, waits for them, and re-layouts  27.3 us (4%)
  between operations  15.2 us (2%)
    ppermute x40, waiting for transfers between devices, flip(): lax.ppermute(value, 'tensor', [(k, k ^ bits) for k in range(lax.axis_size...  203 us
    dot_general x9, matrix products, dot_last(): lax.dot_general(left, right, (((1,), (1,)), ((), ())), preferred_element_...  71.2 us
    all_gather x3, waiting for transfers between devices, gather_dp(): return lax.all_gather(own, 'dp', axis=axis, tiled=True)  51.3 us
    ppermute x40, starting transfers between devices, flip(): lax.ppermute(value, 'tensor', [(k, k ^ bits) for k in range(lax.axis_size...  47.4 us
    dot_general x12, matrix products, dot_first(): lax.dot_general(left, right, (((0,), (0,)), ((), ())), preferred_element_...  46.7 us
    pallas_call x2, Pallas kernels, feed(): pl.pallas_call(feed_kernel, out_shape=[jax.ShapeDtypeStruct((rows, width)...  43 us
    reduce_scatter x3, waiting for transfers between devices, scatter_dp(): lax.psum_scatter(pairs, 'dp', scatter_dimension=0, tiled=True, axis_index...  35 us
    pallas_call x4, Pallas kernels, join(): pl.pallas_call(join_kernel, out_shape=[jax.ShapeDtypeStruct((rows, width)...  24.5 us
  transfers between devices with their start and end apart: 52, of which 30 were waited for; matrix products, arithmetic and copies ran while one was open for 28% of the time, Pallas kernels for 15%

profile of v7, /device:TPU:0, one launch (start us, length us, event | category | flops | bytes accessed | tf_op | source)
XLA Modules:
  0.0 664.4 jit_solution(598765833729819169)
XLA Ops:
  21.4 21.2 %collective-permute-done.refs_1_ = bf16[256,2048]{1,0:T(8,128)(2,1)S(1)} collective-permute-done((bf16[256,2048]{1,0:T(8,128)(2,1)S(1)}, bf16[256,2048]{1,0:T(8,128)(2,1)S(1)}, u32[]{:S(2)}, u32[]{:S(2)}) %collective-permute-start) | collective-permute-done | bytes 1048608 | tf_op jit(solution)/shard_map/ppermute | solution.py:141
  60.2 6.4 shard_map.169
  66.6 28.4 %all-gather.4.cloned.1.call-done = bf16[2048,2048]{1,0:T(8,128)(2,1)} async-done(((bf16[256,2048]{1,0:T(8,128)(2,1)}), bf16[2048,2048]{1,0:T(8,128)(2,1)}) %all-gather.4.cloned.1.call-update) | async-done | bytes 8388624 | tf_op jit(solution)/shard_map/all_gather | solution.py:72
  95.0 11.8 %fusion.4.refs_1_.refs_2_.refs_3_ = f32[1024,1536]{1,0:T(8,128)} fusion(bf16[1024,2048]{1,0:T(8,128)(2,1)} %get-tuple-element.47, bf16[2048,2048]{1,0:T(8,128)(2,1)} %all-gather.4.cloned.1.call-done), kind=kOutput, calls=%fused_computation.10 | convolution fusion | flops 6442450944 | bytes 16777216 | tf_op jit(solution)/shard_map/dot_general | solution.py:56
  106.7 14.6 %shard_map.171 = (bf16[1024,512]{1,0:T(8,128)(2,1)}, bf16[1024,1536]{1,0:T(8,128)(2,1)}) custom-call(s32[1]{0:T(128)} %bitcast.2.refs_0_, f32[1024,1536]{1,0:T(8,128)} %fusion.4.refs_1_.refs_2_.refs_3_, f32[1024,1536]{1,0:T(8,128)} %fusion.4.refs_1_.refs_2_.refs_3_, f32[1024,1536]{1,0:T(8,128)} %fusion.4.refs_1_.refs_2_.refs_3_, ...), custom_call_target="tpu_custom_call" | custom-call | flops 2147483648 | bytes 10485760 | tf_op jit(solution)/shard_map/pallas_call | solution.py:331
  133.4 9.7 %collective-permute-done.5 = bf16[128,2048]{1,0:T(8,128)(2,1)S(1)} collective-permute-done((bf16[128,2048]{1,0:T(8,128)(2,1)}, bf16[128,2048]{1,0:T(8,128)(2,1)S(1)}, u32[]{:S(2)}, u32[]{:S(2)}) %collective-permute-start.5) | collective-permute-done | bytes 524320 | tf_op jit(solution)/shard_map/ppermute | solution.py:141
  149.2 6.6 collective-permute-done.4
  156.1 10.9 %collective-permute-done.6 = bf16[128,2048]{1,0:T(8,128)(2,1)S(1)} collective-permute-done((bf16[128,2048]{1,0:T(8,128)(2,1)S(1)}, bf16[128,2048]{1,0:T(8,128)(2,1)S(1)}, u32[]{:S(2)}, u32[]{:S(2)}) %collective-permute-start.6) | collective-permute-done | bytes 524320 | tf_op jit(solution)/shard_map/ppermute | solution.py:141
  170.5 19.0 %collective-permute-done.14.refs_1_ = bf16[256,2048]{1,0:T(8,128)(2,1)S(1)} collective-permute-done((bf16[256,2048]{1,0:T(8,128)(2,1)S(1)}, bf16[256,2048]{1,0:T(8,128)(2,1)S(1)}, u32[]{:S(2)}, u32[]{:S(2)}) %collective-permute-start.14) | collective-permute-done | bytes 1048608 | tf_op jit(solution)/shard_map/ppermute | solution.py:141
  191.7 20.2 %collective-permute-done.10.refs_1_ = bf16[256,2048]{1,0:T(8,128)(2,1)S(1)} collective-permute-done((bf16[256,2048]{1,0:T(8,128)(2,1)S(1)}, bf16[256,2048]{1,0:T(8,128)(2,1)S(1)}, u32[]{:S(2)}, u32[]{:S(2)}) %collective-permute-start.10) | collective-permute-done | bytes 1048608 | tf_op jit(solution)/shard_map/ppermute | solution.py:141
  239.5 21.4 %shard_map.174 = (bf16[1024,1024]{1,0:T(8,128)(2,1)}, bf16[1024,2048]{1,0:T(8,128)(2,1)}) custom-call(bf16[1024,2048]{1,0:T(8,128)(2,1)} %get-tuple-element.50.h_ref, bf16[1024,2048]{1,0:T(8,128)(2,1)} %get-tuple-element.52.g_ref, bf16[2048,3072]{1,0:T(8,128)(2,1)} %all-gather.6.cloned.1.call-done.gate_ref.up_ref.down_ref, ...), custom_call_target="tpu_custom_call" | custom-call | flops 12884901888 | bytes 27262976 | tf_op jit(solution)/shard_map/pallas_call | solution.py:248
  260.9 7.7 %convolution_convert_fusion.3 = bf16[1024,2048]{1,0:T(8,128)(2,1)S(1)} fusion(bf16[1024,1024]{1,0:T(8,128)(2,1)} %get-tuple-element.60, bf16[1024,2048]{1,0:T(8,128)(2,1)} %get-tuple-element.59), kind=kOutput, calls=%fused_computation.31 | convolution fusion | flops 4297064448 | bytes 10485760 | tf_op jit(solution)/shard_map/dot_general | solution.py:60
  271.7 8.0 %collective-permute-done.19 = bf16[1024,1024]{1,0:T(8,128)(2,1)S(1)} collective-permute-done((bf16[1024,1024]{1,0:T(8,128)(2,1)S(1)}, bf16[1024,1024]{1,0:T(8,128)(2,1)S(1)}, u32[]{:S(2)}, u32[]{:S(2)}) %collective-permute-start.19) | collective-permute-done | bytes 2097184 | tf_op jit(solution)/shard_map/ppermute | solution.py:77
  291.0 14.5 %fusion = f32[1024,2048]{1,0:T(8,128)} fusion(bf16[1024,2048]{1,0:T(8,128)(2,1)} %get-tuple-element.59, bf16[2048,3072]{1,0:T(8,128)(2,1)} %all-gather.6.cloned.1.call-done.gate_ref.up_ref.down_ref), kind=kOutput, calls=%fused_computation | convolution fusion | flops 8589934592 | bytes 20971520 | tf_op jit(solution)/shard_map/dot_general | solution.py:64
  305.5 22.9 %all-gather.8.cloned.1.call-done.gate_ref.up_ref.down_ref = bf16[2048,3072]{1,0:T(8,128)(2,1)} async-done(((bf16[256,3072]{1,0:T(8,128)(2,1)}), bf16[2048,3072]{1,0:T(8,128)(2,1)}) %all-gather.8.cloned.1.call-update) | async-done | bytes 12582928 | tf_op jit(solution)/shard_map/all_gather | solution.py:72
  328.4 21.5 %shard_map.175 = (bf16[1024,1024]{1,0:T(8,128)(2,1)}, bf16[1024,2048]{1,0:T(8,128)(2,1)}) custom-call(bf16[1024,2048]{1,0:T(8,128)(2,1)} %get-tuple-element.50.h_ref, bf16[1024,2048]{1,0:T(8,128)(2,1)} %get-tuple-element.52.g_ref, bf16[2048,3072]{1,0:T(8,128)(2,1)} %all-gather.8.cloned.1.call-done.gate_ref.up_ref.down_ref, ...), custom_call_target="tpu_custom_call" | custom-call | flops 12884901888 | bytes 27262976 | tf_op jit(solution)/shard_map/pallas_call | solution.py:248
  353.1 6.7 %fusion.41 = bf16[256,2048]{1,0:T(8,128)(2,1)S(1)} fusion(bf16[2048,3072]{1,0:T(8,128)(2,1)} %all-gather.8.cloned.1.call-done.gate_ref.up_ref.down_ref, f32[1024,2048]{1,0:T(8,128)} %fusion, bf16[1024,2048]{1,0:T(8,128)(2,1)S(1)} %copy-done.19), kind=kOutput, calls=%fused_computation.41 | convolution fusion | flops 2148532224 | bytes 12582912 | tf_op jit(solution)/shard_map/dot_general | solution.py:64
  388.9 8.6 %collective-permute-done.21 = bf16[128,2048]{1,0:T(8,128)(2,1)S(1)} collective-permute-done((bf16[128,2048]{1,0:T(8,128)(2,1)S(1)}, bf16[128,2048]{1,0:T(8,128)(2,1)S(1)}, u32[]{:S(2)}, u32[]{:S(2)}) %collective-permute-start.21) | collective-permute-done | bytes 524320 | tf_op jit(solution)/shard_map/ppermute | solution.py:141
  399.9 8.1 %collective-permute-done.25 = bf16[128,2048]{1,0:T(8,128)(2,1)S(1)} collective-permute-done((bf16[128,2048]{1,0:T(8,128)(2,1)S(1)}, bf16[128,2048]{1,0:T(8,128)(2,1)S(1)}, u32[]{:S(2)}, u32[]{:S(2)}) %collective-permute-start.25) | collective-permute-done | bytes 524320 | tf_op jit(solution)/shard_map/ppermute | solution.py:141
  412.3 9.1 %collective-permute-done.22 = bf16[128,2048]{1,0:T(8,128)(2,1)S(1)} collective-permute-done((bf16[128,2048]{1,0:T(8,128)(2,1)S(1)}, bf16[128,2048]{1,0:T(8,128)(2,1)S(1)}, u32[]{:S(2)}, u32[]{:S(2)}) %collective-permute-start.22) | collective-permute-done | bytes 524320 | tf_op jit(solution)/shard_map/ppermute | solution.py:141
  440.2 8.9 %collective-permute-done.26.refs_1_ = bf16[256,2048]{1,0:T(8,128)(2,1)} collective-permute-done((bf16[256,2048]{1,0:T(8,128)(2,1)S(1)}, bf16[256,2048]{1,0:T(8,128)(2,1)}, u32[]{:S(2)}, u32[]{:S(2)}) %collective-permute-start.26) | collective-permute-done | bytes 1048608 | tf_op jit(solution)/shard_map/ppermute | solution.py:141
  454.7 8.3 %collective-permute-done.28.refs_3_ = bf16[128,2048]{1,0:T(8,128)(2,1)S(1)} collective-permute-done((bf16[128,2048]{1,0:T(8,128)(2,1)S(1)}, bf16[128,2048]{1,0:T(8,128)(2,1)S(1)}, u32[]{:S(2)}, u32[]{:S(2)}) %collective-permute-start.28) | collective-permute-done | bytes 524320 | tf_op jit(solution)/shard_map/ppermute | solution.py:141
  478.4 18.3 %shard_map.177 = bf16[1024,1536]{1,0:T(8,128)(2,1)} custom-call(s32[1]{0:T(128)} %bitcast.2.refs_0_, bf16[1024,1536]{1,0:T(8,128)(2,1)} %get-tuple-element.57.refs_1_.refs_2_.refs_3_, bf16[1024,1536]{1,0:T(8,128)(2,1)} %get-tuple-element.57.refs_1_.refs_2_.refs_3_, bf16[1024,1536]{1,0:T(8,128)(2,1)} %get-tuple-element.57.refs_1_.refs_2_.refs_3_, ...), custom_call_target="tpu_custom_call" | custom-call | flops 5368709120 | bytes 7340032 | tf_op jit(solution)/shard_map/pallas_call | solution.py:422
  504.9 9.5 %fusion.14 = f32[1024,2048]{1,0:T(8,128)} fusion(bf16[1024,1024]{1,0:T(8,128)(2,1)S(1)} %copy-done.45, bf16[2048,3072]{1,0:T(8,128)(2,1)} %all-gather.6.cloned.1.call-done.gate_ref.up_ref.down_ref), kind=kOutput, calls=%fused_computation.20 | convolution fusion | flops 4294967296 | bytes 14680064 | tf_op jit(solution)/shard_map/dot_general | solution.py:64
  523.4 35.0 %reduce-scatter.6.cloned.1.call-done = bf16[256,3072]{1,0:T(8,128)(2,1)} async-done(((bf16[1024,3072]{1,0:T(8,128)(2,1)}), bf16[256,3072]{1,0:T(8,128)(2,1)}) %reduce-scatter.6.cloned.1.call-update) | async-done | bytes 1572880 | tf_op jit(solution)/shard_map/reduce_scatter | solution.py:92
  558.5 9.8 %add_convert_fusion.1 = bf16[1024,2048]{1,0:T(8,128)(2,1)S(1)} fusion(f32[1024,2048]{1,0:T(8,128)} %fusion.14, bf16[1024,1024]{1,0:T(8,128)(2,1)} %get-tuple-element.72, bf16[2048,3072]{1,0:T(8,128)(2,1)} %all-gather.8.cloned.1.call-done.gate_ref.up_ref.down_ref), kind=kOutput, calls=%fused_computation.3 | convolution fusion | flops 4299161600 | bytes 18874368 | tf_op jit(solution)/shard_map/dot_general | solution.py:64
  571.7 9.0 %fusion.18 = bf16[1024,2048]{1,0:T(8,128)(2,1)S(1)} fusion(bf16[1024,1536]{1,0:T(8,128)(2,1)S(1)} %copy-done.48, bf16[2048,2048]{1,0:T(8,128)(2,1)} %all-gather.4.cloned.1.call-done), kind=kOutput, calls=%fused_computation.27 | convolution fusion | flops 6444548096 | bytes 13631488 | tf_op jit(solution)/shard_map/dot_general | solution.py:64
  587.0 8.8 %collective-permute-done.39 = bf16[128,2048]{1,0:T(8,128)(2,1)S(1)} collective-permute-done((bf16[128,2048]{1,0:T(8,128)(2,1)S(1)}, bf16[128,2048]{1,0:T(8,128)(2,1)S(1)}, u32[]{:S(2)}, u32[]{:S(2)}) %collective-permute-start.39) | collective-permute-done | bytes 524320 | tf_op jit(solution)/shard_map/ppermute | solution.py:141
  599.2 9.3 %collective-permute-done.30 = bf16[128,2048]{1,0:T(8,128)(2,1)S(1)} collective-permute-done((bf16[128,2048]{1,0:T(8,128)(2,1)S(1)}, bf16[128,2048]{1,0:T(8,128)(2,1)S(1)}, u32[]{:S(2)}, u32[]{:S(2)}) %collective-permute-start.30) | collective-permute-done | bytes 524320 | tf_op jit(solution)/shard_map/ppermute | solution.py:141
  610.5 9.2 %collective-permute-done.32 = bf16[128,2048]{1,0:T(8,128)(2,1)S(1)} collective-permute-done((bf16[128,2048]{1,0:T(8,128)(2,1)S(1)}, bf16[128,2048]{1,0:T(8,128)(2,1)S(1)}, u32[]{:S(2)}, u32[]{:S(2)}) %collective-permute-start.32) | collective-permute-done | bytes 524320 | tf_op jit(solution)/shard_map/ppermute | solution.py:141
  622.0 8.9 %collective-permute-done.38 = bf16[128,2048]{1,0:T(8,128)(2,1)S(1)} collective-permute-done((bf16[128,2048]{1,0:T(8,128)(2,1)S(1)}, bf16[128,2048]{1,0:T(8,128)(2,1)S(1)}, u32[]{:S(2)}, u32[]{:S(2)}) %collective-permute-start.38) | collective-permute-done | bytes 524320 | tf_op jit(solution)/shard_map/ppermute | solution.py:141
  630.9 9.8 %collective-permute-done.40 = bf16[128,2048]{1,0:T(8,128)(2,1)S(1)} collective-permute-done((bf16[128,2048]{1,0:T(8,128)(2,1)S(1)}, bf16[128,2048]{1,0:T(8,128)(2,1)S(1)}, u32[]{:S(2)}, u32[]{:S(2)}) %collective-permute-start.40) | collective-permute-done | bytes 524320 | tf_op jit(solution)/shard_map/ppermute | solution.py:141
  (289 shorter events, 227.0 us)
Async XLA Ops:
  7.2 87.8 %all-gather.4.cloned.1.call-start = ((), (), s32[]{:S(2)}) async-start(), calls=%async_computation.3 | async-start | bytes 9437184 | tf_op jit(solution)/shard_map/all_gather | solution.py:72
  9.5 229.9 %all-gather.6.cloned.1.call-start = ((), (), s32[]{:S(2)}) async-start(), calls=%async_computation.4 | async-start | bytes 14155776 | tf_op jit(solution)/shard_map/all_gather | solution.py:72
  13.0 315.4 %all-gather.8.cloned.1.call-start = ((), (), s32[]{:S(2)}) async-start(), calls=%async_computation.5 | async-start | bytes 14155776 | tf_op jit(solution)/shard_map/all_gather | solution.py:72
  14.4 435.9 %reduce-scatter.4.cloned.1.call-start = ((), (), s32[]{:S(2)}) async-start(), calls=%async_computation.6 | async-start | bytes 7864320 | tf_op jit(solution)/shard_map/reduce_scatter | solution.py:92
  16.4 26.2 %collective-permute-start = (bf16[256,2048]{1,0:T(8,128)(2,1)S(1)}, bf16[256,2048]{1,0:T(8,128)(2,1)S(1)}, u32[]{:S(2)}, u32[]{:S(2)}) collective-permute-start(bf16[256,2048]{1,0:T(8,128)(2,1)S(1)} %fusion.48.refs_0_), channel_id=1, source_target_pairs={{0,1},{1,0},{2,3},{3,2},{4,5},{5,4},{6,7},{7,6},{8,9},{9,8},{10,11... | collective-permute-start | bytes 3145736 | tf_op jit(solution)/shard_map/ppermute | solution.py:141
  19.5 25.8 %collective-permute-start.1 = (bf16[256,2048]{1,0:T(8,128)(2,1)S(1)}, bf16[256,2048]{1,0:T(8,128)(2,1)}, u32[]{:S(2)}, u32[]{:S(2)}) collective-permute-start(bf16[256,2048]{1,0:T(8,128)(2,1)S(1)} %fusion.48.refs_0_), channel_id=1, source_target_pairs={{0,2},{1,3},{2,0},{3,1},{4,6},{5,7},{6,4},{7,5},{8,10},{9,11},{10,... | collective-permute-start | bytes 3145736 | tf_op jit(solution)/shard_map/ppermute | solution.py:141
  132.4 23.3 %collective-permute-start.4 = (bf16[128,2048]{1,0:T(8,128)(2,1)}, bf16[128,2048]{1,0:T(8,128)(2,1)S(1)}, u32[]{:S(2)}, u32[]{:S(2)}) collective-permute-start(bf16[128,2048]{1,0:T(8,128)(2,1)} %get-tuple-element.135), channel_id=1, source_target_pairs={{0,1},{1,0},{2,3},{3,2},{4,5},{5,4},{6,7},{7,6},{8,9},{9,8},{10,11... | collective-permute-start | bytes 1572872 | tf_op jit(solution)/shard_map/ppermute | solution.py:141
  133.1 23.1 %collective-permute-start.9 = (bf16[128,2048]{1,0:T(8,128)(2,1)}, bf16[128,2048]{1,0:T(8,128)(2,1)S(1)}, u32[]{:S(2)}, u32[]{:S(2)}) collective-permute-start(bf16[128,2048]{1,0:T(8,128)(2,1)} %get-tuple-element.136), channel_id=1, source_target_pairs={{0,2},{1,3},{2,0},{3,1},{4,6},{5,7},{6,4},{7,5},{8,10},{9,11},{10,... | collective-permute-start | bytes 1572872 | tf_op jit(solution)/shard_map/ppermute | solution.py:141
  146.4 20.6 %collective-permute-start.6 = (bf16[128,2048]{1,0:T(8,128)(2,1)S(1)}, bf16[128,2048]{1,0:T(8,128)(2,1)S(1)}, u32[]{:S(2)}, u32[]{:S(2)}) collective-permute-start(bf16[128,2048]{1,0:T(8,128)(2,1)S(1)} %get-tuple-element.139), channel_id=1, source_target_pairs={{0,1},{1,0},{2,3},{3,2},{4,5},{5,4},{6,7},{7,6},{8,9},{9,8},{10,11... | collective-permute-start | bytes 1572872 | tf_op jit(solution)/shard_map/ppermute | solution.py:141
  148.8 40.7 %collective-permute-start.14 = (bf16[256,2048]{1,0:T(8,128)(2,1)S(1)}, bf16[256,2048]{1,0:T(8,128)(2,1)S(1)}, u32[]{:S(2)}, u32[]{:S(2)}) collective-permute-start(bf16[256,2048]{1,0:T(8,128)(2,1)S(1)} %fusion.55.refs_0_), channel_id=1, source_target_pairs={{0,1},{1,0},{2,3},{3,2},{4,5},{5,4},{6,7},{7,6},{8,9},{9,8},{10,11... | collective-permute-start | bytes 3145736 | tf_op jit(solution)/shard_map/ppermute | solution.py:141
  155.8 34.2 %collective-permute-start.15 = (bf16[256,2048]{1,0:T(8,128)(2,1)S(1)}, bf16[256,2048]{1,0:T(8,128)(2,1)S(1)}, u32[]{:S(2)}, u32[]{:S(2)}) collective-permute-start(bf16[256,2048]{1,0:T(8,128)(2,1)S(1)} %fusion.55.refs_0_), channel_id=1, source_target_pairs={{0,2},{1,3},{2,0},{3,1},{4,6},{5,7},{6,4},{7,5},{8,10},{9,11},{10,... | collective-permute-start | bytes 3145736 | tf_op jit(solution)/shard_map/ppermute | solution.py:141
  168.4 43.5 %collective-permute-start.10 = (bf16[256,2048]{1,0:T(8,128)(2,1)S(1)}, bf16[256,2048]{1,0:T(8,128)(2,1)S(1)}, u32[]{:S(2)}, u32[]{:S(2)}) collective-permute-start(bf16[256,2048]{1,0:T(8,128)(2,1)S(1)} %fusion.59.refs_0_), channel_id=1, source_target_pairs={{0,1},{1,0},{2,3},{3,2},{4,5},{5,4},{6,7},{7,6},{8,9},{9,8},{10,11... | collective-permute-start | bytes 3145736 | tf_op jit(solution)/shard_map/ppermute | solution.py:141
  170.0 43.2 %collective-permute-start.11 = (bf16[256,2048]{1,0:T(8,128)(2,1)S(1)}, bf16[256,2048]{1,0:T(8,128)(2,1)S(1)}, u32[]{:S(2)}, u32[]{:S(2)}) collective-permute-start(bf16[256,2048]{1,0:T(8,128)(2,1)S(1)} %fusion.59.refs_0_), channel_id=1, source_target_pairs={{0,2},{1,3},{2,0},{3,1},{4,6},{5,7},{6,4},{7,5},{8,10},{9,11},{10,... | collective-permute-start | bytes 3145736 | tf_op jit(solution)/shard_map/ppermute | solution.py:141
  189.5 32.2 %collective-permute-start.16 = (bf16[128,2048]{1,0:T(8,128)(2,1)S(1)}, bf16[128,2048]{1,0:T(8,128)(2,1)S(1)}, u32[]{:S(2)}, u32[]{:S(2)}) collective-permute-start(bf16[128,2048]{1,0:T(8,128)(2,1)S(1)} %slice.292), channel_id=1, source_target_pairs={{0,2},{1,3},{2,0},{3,1},{4,6},{5,7},{6,4},{7,5},{8,10},{9,11},{10,... | collective-permute-start | bytes 1572872 | tf_op jit(solution)/shard_map/ppermute | solution.py:141
  190.0 33.3 %collective-permute-start.17 = (bf16[128,2048]{1,0:T(8,128)(2,1)S(1)}, bf16[128,2048]{1,0:T(8,128)(2,1)}, u32[]{:S(2)}, u32[]{:S(2)}) collective-permute-start(bf16[128,2048]{1,0:T(8,128)(2,1)S(1)} %slice.293), channel_id=1, source_target_pairs={{0,1},{1,0},{2,3},{3,2},{4,5},{5,4},{6,7},{7,6},{8,9},{9,8},{10,11... | collective-permute-start | bytes 1572872 | tf_op jit(solution)/shard_map/ppermute | solution.py:141
  212.8 19.5 %collective-permute-start.12 = (bf16[128,2048]{1,0:T(8,128)(2,1)}, bf16[128,2048]{1,0:T(8,128)(2,1)}, u32[]{:S(2)}, u32[]{:S(2)}) collective-permute-start(bf16[128,2048]{1,0:T(8,128)(2,1)} %slice.290), channel_id=1, source_target_pairs={{0,2},{1,3},{2,0},{3,1},{4,6},{5,7},{6,4},{7,5},{8,10},{9,11},{10,... | collective-permute-start | bytes 1572872 | tf_op jit(solution)/shard_map/ppermute | solution.py:141
  290.9 267.5 %reduce-scatter.6.cloned.1.call-start = ((), (), s32[]{:S(2)}) async-start(), calls=%async_computation.7 | async-start | bytes 7864320 | tf_op jit(solution)/shard_map/reduce_scatter | solution.py:92
  382.3 49.9 %collective-permute-start.44 = (bf16[1024,2048]{1,0:T(8,128)(2,1)S(1)}, bf16[1024,2048]{1,0:T(8,128)(2,1)S(1)}, u32[]{:S(2)}, u32[]{:S(2)}) collective-permute-start(bf16[1024,2048]{1,0:T(8,128)(2,1)S(1)} %convolution_convert_fusion.2), channel_id=1, source_target_pairs={{0,4},{4,0},{8,12},{12,8},{16,20},{20,16},{24,28},{28,24},{1,5},{5... | collective-permute-start | bytes 12582920 | tf_op jit(solution)/shard_map/ppermute | solution.py:77
  388.2 39.9 %collective-permute-start.45 = (bf16[1024,1024]{1,0:T(8,128)(2,1)S(1)}, bf16[1024,1024]{1,0:T(8,128)(2,1)S(1)}, u32[]{:S(2)}, u32[]{:S(2)}) collective-permute-start(bf16[1024,1024]{1,0:T(8,128)(2,1)S(1)} %convolution_convert_fusion.4), channel_id=1, source_target_pairs={{0,4},{4,0},{8,12},{12,8},{16,20},{20,16},{24,28},{28,24},{1,5},{5... | collective-permute-start | bytes 6291464 | tf_op jit(solution)/shard_map/ppermute | solution.py:77
  388.3 19.8 %collective-permute-start.25 = (bf16[128,2048]{1,0:T(8,128)(2,1)S(1)}, bf16[128,2048]{1,0:T(8,128)(2,1)S(1)}, u32[]{:S(2)}, u32[]{:S(2)}) collective-permute-start(bf16[128,2048]{1,0:T(8,128)(2,1)S(1)} %slice.302), channel_id=1, source_target_pairs={{0,2},{1,3},{2,0},{3,1},{4,6},{5,7},{6,4},{7,5},{8,10},{9,11},{10,... | collective-permute-start | bytes 1572872 | tf_op jit(solution)/shard_map/ppermute | solution.py:141
  399.1 22.2 %collective-permute-start.22 = (bf16[128,2048]{1,0:T(8,128)(2,1)S(1)}, bf16[128,2048]{1,0:T(8,128)(2,1)S(1)}, u32[]{:S(2)}, u32[]{:S(2)}) collective-permute-start(bf16[128,2048]{1,0:T(8,128)(2,1)S(1)} %add_convert_fusion.12), channel_id=1, source_target_pairs={{0,1},{1,0},{2,3},{3,2},{4,5},{5,4},{6,7},{7,6},{8,9},{9,8},{10,11... | collective-permute-start | bytes 1572872 | tf_op jit(solution)/shard_map/ppermute | solution.py:141
  425.2 23.9 %collective-permute-start.26 = (bf16[256,2048]{1,0:T(8,128)(2,1)S(1)}, bf16[256,2048]{1,0:T(8,128)(2,1)}, u32[]{:S(2)}, u32[]{:S(2)}) collective-permute-start(bf16[256,2048]{1,0:T(8,128)(2,1)S(1)} %get-tuple-element.116.refs_0_), channel_id=1, source_target_pairs={{0,1},{1,0},{2,3},{3,2},{4,5},{5,4},{6,7},{7,6},{8,9},{9,8},{10,11... | collective-permute-start | bytes 3145736 | tf_op jit(solution)/shard_map/ppermute | solution.py:141
  426.6 23.6 %collective-permute-start.27 = (bf16[256,2048]{1,0:T(8,128)(2,1)S(1)}, bf16[256,2048]{1,0:T(8,128)(2,1)}, u32[]{:S(2)}, u32[]{:S(2)}) collective-permute-start(bf16[256,2048]{1,0:T(8,128)(2,1)S(1)} %get-tuple-element.116.refs_0_), channel_id=1, source_target_pairs={{0,2},{1,3},{2,0},{3,1},{4,6},{5,7},{6,4},{7,5},{8,10},{9,11},{10,... | collective-permute-start | bytes 3145736 | tf_op jit(solution)/shard_map/ppermute | solution.py:141
  450.3 204.6 %reduce-scatter.8.cloned.1.call-start = ((), (), s32[]{:S(2)}) async-start(), calls=%async_computation.8 | async-start | bytes 5242880 | tf_op jit(solution)/shard_map/reduce_scatter | solution.py:92
  583.9 24.6 %collective-permute-start.30 = (bf16[128,2048]{1,0:T(8,128)(2,1)S(1)}, bf16[128,2048]{1,0:T(8,128)(2,1)S(1)}, u32[]{:S(2)}, u32[]{:S(2)}) collective-permute-start(bf16[128,2048]{1,0:T(8,128)(2,1)S(1)} %get-tuple-element.131), channel_id=1, source_target_pairs={{0,1},{1,0},{2,3},{3,2},{4,5},{5,4},{6,7},{7,6},{8,9},{9,8},{10,11... | collective-permute-start | bytes 1572872 | tf_op jit(solution)/shard_map/ppermute | solution.py:141
  584.5 24.5 %collective-permute-start.35 = (bf16[128,2048]{1,0:T(8,128)(2,1)S(1)}, bf16[128,2048]{1,0:T(8,128)(2,1)S(1)}, u32[]{:S(2)}, u32[]{:S(2)}) collective-permute-start(bf16[128,2048]{1,0:T(8,128)(2,1)S(1)} %get-tuple-element.129), channel_id=1, source_target_pairs={{0,2},{1,3},{2,0},{3,1},{4,6},{5,7},{6,4},{7,5},{8,10},{9,11},{10,... | collective-permute-start | bytes 1572872 | tf_op jit(solution)/shard_map/ppermute | solution.py:141
  585.4 34.3 %collective-permute-start.32 = (bf16[128,2048]{1,0:T(8,128)(2,1)S(1)}, bf16[128,2048]{1,0:T(8,128)(2,1)S(1)}, u32[]{:S(2)}, u32[]{:S(2)}) collective-permute-start(bf16[128,2048]{1,0:T(8,128)(2,1)S(1)} %get-tuple-element.127), channel_id=1, source_target_pairs={{0,1},{1,0},{2,3},{3,2},{4,5},{5,4},{6,7},{7,6},{8,9},{9,8},{10,11... | collective-permute-start | bytes 1572872 | tf_op jit(solution)/shard_map/ppermute | solution.py:141
  595.7 24.5 %collective-permute-start.34 = (bf16[128,2048]{1,0:T(8,128)(2,1)S(1)}, bf16[128,2048]{1,0:T(8,128)(2,1)S(1)}, u32[]{:S(2)}, u32[]{:S(2)}) collective-permute-start(bf16[128,2048]{1,0:T(8,128)(2,1)S(1)} %get-tuple-element.126), channel_id=1, source_target_pairs={{0,2},{1,3},{2,0},{3,1},{4,6},{5,7},{6,4},{7,5},{8,10},{9,11},{10,... | collective-permute-start | bytes 1572872 | tf_op jit(solution)/shard_map/ppermute | solution.py:141
  597.2 33.7 %collective-permute-start.38 = (bf16[128,2048]{1,0:T(8,128)(2,1)S(1)}, bf16[128,2048]{1,0:T(8,128)(2,1)S(1)}, u32[]{:S(2)}, u32[]{:S(2)}) collective-permute-start(bf16[128,2048]{1,0:T(8,128)(2,1)S(1)} %get-tuple-element.120), channel_id=1, source_target_pairs={{0,1},{1,0},{2,3},{3,2},{4,5},{5,4},{6,7},{7,6},{8,9},{9,8},{10,11... | collective-permute-start | bytes 1572872 | tf_op jit(solution)/shard_map/ppermute | solution.py:141
  608.5 22.5 %collective-permute-start.43 = (bf16[128,2048]{1,0:T(8,128)(2,1)S(1)}, bf16[128,2048]{1,0:T(8,128)(2,1)S(1)}, u32[]{:S(2)}, u32[]{:S(2)}) collective-permute-start(bf16[128,2048]{1,0:T(8,128)(2,1)S(1)} %get-tuple-element.121), channel_id=1, source_target_pairs={{0,2},{1,3},{2,0},{3,1},{4,6},{5,7},{6,4},{7,5},{8,10},{9,11},{10,... | collective-permute-start | bytes 1572872 | tf_op jit(solution)/shard_map/ppermute | solution.py:141
  609.0 31.7 %collective-permute-start.40 = (bf16[128,2048]{1,0:T(8,128)(2,1)S(1)}, bf16[128,2048]{1,0:T(8,128)(2,1)S(1)}, u32[]{:S(2)}, u32[]{:S(2)}) collective-permute-start(bf16[128,2048]{1,0:T(8,128)(2,1)S(1)} %get-tuple-element.124), channel_id=1, source_target_pairs={{0,1},{1,0},{2,3},{3,2},{4,5},{5,4},{6,7},{7,6},{8,9},{9,8},{10,11... | collective-permute-start | bytes 1572872 | tf_op jit(solution)/shard_map/ppermute | solution.py:141
  619.7 21.0 %collective-permute-start.42 = (bf16[128,2048]{1,0:T(8,128)(2,1)S(1)}, bf16[128,2048]{1,0:T(8,128)(2,1)S(1)}, u32[]{:S(2)}, u32[]{:S(2)}) collective-permute-start(bf16[128,2048]{1,0:T(8,128)(2,1)S(1)} %get-tuple-element.125), channel_id=1, source_target_pairs={{0,2},{1,3},{2,0},{3,1},{4,6},{5,7},{6,4},{7,5},{8,10},{9,11},{10,... | collective-permute-start | bytes 1572872 | tf_op jit(solution)/shard_map/ppermute | solution.py:141
  (73 other events, 824.8 us)
Sparse Core Ops, SparseCore 0:
  10.2 84.7 all-gather.3
  96.6 115.1 all-gather.5
  213.5 114.8 all-gather.7
  330.6 108.9 reduce-scatter.3
  450.4 107.9 reduce-scatter.5
  560.6 77.2 reduce-scatter.7
